TPU v7x, 128 devices: a whole 4x4x4 slice. The times are simulated.
128 devices in a mesh: section: 2 (over y_hi), row: 8 (over z, core), tp: 8 (over x, y_lo).
Axes of the slice: x: 4, y: 4 (y_hi: 2, y_lo: 2; y = y_hi * 2 + y_lo), z: 4, core: 2. Of those that a mesh axis runs over, the one named last changes fastest.
Arguments:
- section_feeds: bfloat16 [2, 2, 128, 8192], P('section', None, None, 'row'), may hold values from -6 to 6
- norm_gain: float32 [2, 8192], P('section', 'row'), may hold values from 0.1 to 1.9
- up_weight: bfloat16 [2, 8192, 32768], P('section', 'row', 'tp'), may hold values from -0.0625 to 0.0625
- down_weight: bfloat16 [2, 32768, 8192], P('section', 'tp', 'row'), may hold values from -0.03125 to 0.03125
Outputs:
- section_ends: bfloat16 [2, 2, 128, 8192], P('section', None, None, 'row')
All inputs are finite; a program needn't handle non-finite values.
Results may differ from a plain program's by a relative error of at most 0.011.
Values may be sent and summed in bfloat16 or wider, within the bound.
No kernel may reach another device: no remote copies, remote signals or barrier semaphores. Data moves between devices by JAX's collectives and lax.ppermute only.
A program may use at most 128 MiB of HBM per device.

v0:
```python
import functools

import jax
import jax.numpy as jnp
from jax import lax
from jax.experimental import pallas as pl
from jax.experimental.pallas import tpu as pltpu
from jax.sharding import PartitionSpec as P

epsilon = 1e-05
gelu_coeff = 0.7978845608028654
LANES = 128
EXTRA = 32
f32 = jnp.float32
bf16 = jnp.bfloat16
NN = (((1,), (0,)), ((), ()))
NT = (((1,), (1,)), ((), ()))
HBM = pl.BlockSpec(memory_space=pltpu.HBM)
VMEM = pl.BlockSpec(memory_space=pltpu.VMEM)
SMEM = pl.BlockSpec(memory_space=pltpu.SMEM)


def gelu_tangent(inputs):
    return jnp.tanh(gelu_coeff * (inputs + 0.044715 * inputs * inputs * inputs))


def gelu_value(inputs):
    return 0.5 * inputs * (1.0 + gelu_tangent(inputs))


def pieces(value):
    high = value.astype(bf16)
    rest = value - high.astype(f32)
    middle = rest.astype(bf16)
    low = (rest - middle.astype(f32)).astype(bf16)
    return high, middle, low


def pieces32(value):
    return tuple(part.astype(f32) for part in pieces(value))


def mul(a, b, dims):
    return lax.dot_general(a, b, dims, preferred_element_type=f32)


def norm_stats(raw, gain_row):
    values = raw.astype(f32)
    mean = jnp.sum(values, axis=1, keepdims=True) / values.shape[1]
    centred = values - mean
    squares = jnp.sum(centred * centred, axis=1, keepdims=True)
    return (centred * gain_row).astype(bf16), pieces32(mean) + pieces32(squares)


def put_stats(to, start, lanes, stats, row_at):
    lane = lax.broadcasted_iota(jnp.int32, (1, LANES), 1)
    ext = jnp.zeros((stats[0].shape[0], LANES), f32)
    for i, part in enumerate(stats):
        ext = ext + jnp.where(lane == i * 8 + row_at, part, 0.0)
    to[pl.ds(start, ext.shape[0]), pl.ds(lanes, LANES)] = ext.astype(to.dtype)


def placed(parts, row_at):
    spot = lax.broadcasted_iota(jnp.int32, (EXTRA, 1), 0)
    return sum(jnp.where(spot == 3 * row_at + j, part, 0.0) for j, part in enumerate(parts))


def store_halves(own, other, columns, result):
    half = result.shape[0] // 2
    own[pl.ds(0, half), columns] = result[:half]
    other[pl.ds(0, half), columns] = result[half:].astype(bf16)


def start_kernel(part, at, x, gain, up, down, *refs):
    outs, (xs_out, x_here, up_tiles, down_tiles, sems) = refs[:2], refs[2:]
    own, other = outs
    first = at[0] == 1
    core, row_at = at[1], at[2]
    count, _, wide = up_tiles.shape
    half = outs[0].shape[0] - EXTRA

    def tile(n):
        return pl.ds((part * count + n) * wide, wide)

    def up_copy(n):
        return pltpu.make_async_copy(up.at[:, tile(n)], up_tiles.at[n], sems.at[0, n])

    def down_copy(n):
        return pltpu.make_async_copy(down.at[tile(n)], down_tiles.at[n], sems.at[1, n])

    if part == 0:
        x_copy = pltpu.make_async_copy(x, x_here, sems.at[2, 0])
        x_copy.start()
    for n in range(count):
        up_copy(n).start()

    @pl.when(jnp.logical_not(first))
    def _():
        for n in range(count):
            down_copy(n).start()

    if part == 0:
        x_copy.wait()
        gain_row = gain[...]
        for kk in range(2):

            def prepare(p, carry):
                raw = x_here[(core + kk) % 2, p]
                scaled, stats = norm_stats(raw, gain_row)
                rows = pl.ds(pl.multiple_of((kk * 4 + p) * 32, 32), 32)
                xs_out[rows, :] = jnp.where(first, scaled, raw)
                put_stats(outs[kk], pl.multiple_of(p * 32, 32), count * wide, stats, row_at)
                return carry

            lax.fori_loop(0, 4, prepare, 0)
        xs_out[pl.ds(2 * half, EXTRA), :] = placed(pieces32(gain_row), row_at).astype(bf16)
        for to in outs[:2]:
            to[pl.ds(half, EXTRA), pl.ds(count * wide, LANES)] = jnp.zeros((EXTRA, LANES), to.dtype)
        xs = xs_out
    else:
        xs = x

    for n in range(count):

        def store(columns, result, extra):
            store_halves(own, other, columns, result)
            rows = placed(pieces32(jnp.sum(extra, axis=0, keepdims=True)), row_at)
            own[pl.ds(half, EXTRA), columns] = rows
            other[pl.ds(half, EXTRA), columns] = rows.astype(bf16)

        up_copy(n).wait()

        @pl.when(first)
        def _():
            result = mul(xs[...], up_tiles[n], NN)
            store(pl.ds(n * wide, wide), result[: 2 * half], result[2 * half :])

        @pl.when(jnp.logical_not(first))
        def _():
            down_copy(n).wait()

            def piece(i, carry):
                columns = pl.ds(pl.multiple_of(i * 256, 256), 256)
                store(
                    pl.ds(pl.multiple_of(n * wide + i * 256, 256), 256),
                    mul(xs[pl.ds(0, 2 * half), :], down_tiles[n, columns], NT),
                    mul(xs[pl.ds(2 * half, EXTRA), :], up_tiles[n, :, columns], NN),
                )
                return carry

            lax.fori_loop(0, wide // 256, piece, 0)


def start_in(at, x, gain, up, down):
    width, hidden = up.shape
    wide, count = hidden // 4, 2
    rows = 128 + EXTRA
    halves = []
    for part in range(2):
        outs = pl.pallas_call(
            functools.partial(start_kernel, part),
            out_shape=half_shapes(rows, count * wide + (0 if part else LANES))
            + [jax.ShapeDtypeStruct((256 + EXTRA if part == 0 else 16, width), bf16)],
            in_specs=[SMEM, VMEM if part else HBM, VMEM, HBM, HBM],
            out_specs=[VMEM] * 3,
            scratch_shapes=[
                pltpu.VMEM(x.shape if part == 0 else (16, 128), bf16),
                pltpu.VMEM((count, width, wide), bf16),
                pltpu.VMEM((count, wide, width), bf16),
                pltpu.SemaphoreType.DMA((3, count)),
            ],
            compiler_params=pltpu.CompilerParams(vmem_limit_bytes=16 * 1024 * 1024),
            cost_estimate=pl.CostEstimate(
                flops=256 * width * hidden, bytes_accessed=width * hidden, transcendentals=0
            ),
            name=f"start_in_{part}",
        )(
            at,
            x if part else pltpu.with_memory_space_constraint(x, pltpu.HBM),
            gain,
            pltpu.with_memory_space_constraint(up, pltpu.HBM),
            pltpu.with_memory_space_constraint(down, pltpu.HBM),
        )
        x = outs[2]
        halves.append(outs[:2])
    return halves


def up_kernel(part, at, x, gain, up, *refs):
    outs, (xs_out, up_tiles, sems) = refs[:2], refs[2:]
    count, _, wide = up_tiles.shape

    def up_copy(n):
        tile = pl.ds((part * count + n) * wide, wide)
        return pltpu.make_async_copy(up.at[:, tile], up_tiles.at[n], sems.at[n])

    for n in range(count):
        up_copy(n).start()
    if part == 0:
        gain_row = gain[...]
        for kk in range(2):

            def prepare(p, carry):
                scaled, stats = norm_stats(x[kk * 4 + p], gain_row)
                xs_out[pl.ds(pl.multiple_of((kk * 4 + p) * 32, 32), 32), :] = scaled
                put_stats(outs[kk], pl.multiple_of(p * 32, 32), count * wide, stats, at[2])
                return carry

            lax.fori_loop(0, 4, prepare, 0)
    xs = x if part else xs_out
    for n in range(count):
        up_copy(n).wait()
        store_halves(*outs, pl.ds(n * wide, wide), mul(xs[...], up_tiles[n], NN))


def up_in(at, x, gain, up):
    width, hidden = up.shape
    wide, count = hidden // 4, 2
    halves = []
    for part in range(2):
        outs = pl.pallas_call(
            functools.partial(up_kernel, part),
            out_shape=half_shapes(128, count * wide + (0 if part else LANES))
            + [jax.ShapeDtypeStruct((256 if part == 0 else 16, width), bf16)],
            in_specs=[SMEM, VMEM, VMEM, HBM],
            out_specs=[VMEM] * 3,
            scratch_shapes=[
                pltpu.VMEM((count, width, wide), bf16),
                pltpu.SemaphoreType.DMA((count,)),
            ],
            compiler_params=pltpu.CompilerParams(vmem_limit_bytes=10 * 1024 * 1024),
            cost_estimate=pl.CostEstimate(
                flops=256 * width * hidden, bytes_accessed=width * hidden, transcendentals=0
            ),
            name=f"up_in_{part}",
        )(at, x, gain, pltpu.with_memory_space_constraint(up, pltpu.HBM))
        x = outs[2]
        halves.append(outs[:2])
    return halves


def down_back_kernel(part, x, down, own, other):
    wide = own.shape[1] // 2
    for n in range(2):
        result = mul(x[...], down[pl.ds((2 * part + n) * wide, wide), :], NT)
        store_halves(own, other, pl.ds(n * wide, wide), result)


def local_call(kernel, shapes, operands, name, flops, nbytes, smem=False, scratch=()):
    specs = [SMEM if smem and i == 0 else VMEM for i in range(len(operands))]
    return pl.pallas_call(
        kernel,
        out_shape=shapes,
        in_specs=specs,
        out_specs=[VMEM] * len(shapes),
        scratch_shapes=list(scratch),
        compiler_params=pltpu.CompilerParams(vmem_limit_bytes=6 * 1024 * 1024),
        cost_estimate=pl.CostEstimate(flops=flops, bytes_accessed=nbytes, transcendentals=0),
        name=name,
    )(*operands)


def half_shapes(rows, columns):
    return [
        jax.ShapeDtypeStruct((rows, columns), f32),
        jax.ShapeDtypeStruct((rows, columns), bf16),
    ]


def down_back_in(x, down):
    hidden, width = down.shape
    halves = []
    for part in range(2):
        outs = local_call(
            functools.partial(down_back_kernel, part),
            half_shapes(128, hidden // 2),
            (x.reshape(256, width), down),
            f"down_back_{part}",
            256 * width * hidden,
            width * hidden,
        )
        halves.append(outs)
    return halves


def row_out_kernel(mode, at, *refs):
    inputs, rest, (out, xs) = refs[:4], refs[4:-2], refs[-2:]
    first = at[0] == 1
    half, columns = 128, xs.shape[1] // 2
    width = out.shape[-1]
    slot = 0
    for i in range(2):
        for j in range(2):
            ref = inputs[2 * i + j]
            xs[pl.ds(i * half, half), pl.ds(j * columns, columns)] = ref[:, pl.ds(0, columns)]

    def terms():
        gain, x = rest[:2]
        for i in range(2):
            early, late = (r[:, pl.ds(columns, LANES)].astype(f32) for r in inputs[2 * i : 2 * i + 2])
            ext = early + late
            first0, second0, first1, second1, mean, inv_std = (
                ext[:, 3 * k : 3 * k + 1] + ext[:, 3 * k + 1 : 3 * k + 2] + ext[:, 3 * k + 2 : 3 * k + 3]
                for k in range(6)
            )
            for p in range(4):
                pick = slice(p * 32, p * 32 + 32)
                yield (
                    i * 4 + p,
                    gain,
                    x.at[(at[1] + i) % 2, p] if mode == 2 else x.at[i * 4 + p],
                    (first0 + first1)[pick],
                    (second0 + second1)[pick],
                    mean[pick],
                    inv_std[pick],
                )

    def steps(weight, dims, back):
        saved = list(terms()) if back else []

        def step(n, carry):
            at_n = pl.ds(pl.multiple_of(n * 512, 512), 512)
            tile = weight[:, at_n] if dims is NN else weight[at_n, :]
            result = mul(xs[...], tile, dims)
            if not back:
                for k in range(8):
                    out[slot + k, :, at_n] = result[k * 32 : k * 32 + 32].astype(bf16)
            for k, gain, x, first_sum, second_sum, mean, inv_std in saved:
                grad = result[k * 32 : k * 32 + 32] * gain[:, at_n]
                normed = (x[:, at_n].astype(f32) - mean) * inv_std
                out[slot + k, :, at_n] = (inv_std * (grad - first_sum - normed * second_sum)).astype(bf16)
            return carry

        lax.fori_loop(0, width // 512, step, 0)

    if mode == 0:
        steps(rest[0], NN, False)
    elif mode == 1:
        steps(rest[2], NT, True)
    else:
        pl.when(first)(lambda: steps(rest[2], NT, True))
        pl.when(jnp.logical_not(first))(lambda: steps(rest[3], NN, False))


def row_out(mode, at, mine, others, rest):
    hidden, width = max(rest[-1].shape), min(rest[-1].shape)
    (out,) = local_call(
        functools.partial(row_out_kernel, mode),
        [jax.ShapeDtypeStruct((8, 32, width), bf16)],
        (at, *mine, *others, *rest),
        f"row_out_{mode}",
        2 * 256 * width * hidden,
        2 * width * hidden,
        smem=True,
        scratch=[pltpu.VMEM((256, hidden), bf16)],
    )
    return out


MEAN, INV, SHIFT = 0, 1, 8


def act_kernel(mode, part, at, *refs):
    refs = list(refs)
    first = at[0] == 1
    sums = [(refs.pop(0), refs.pop(0)) for _ in range(2)]
    stats = refs.pop(0) if mode == 2 or part else None
    gains = refs.pop(0) if mode else None
    saved = refs.pop(0) if mode else None
    hidden = refs.pop(0) if mode == 2 else None
    chunk = refs.pop(0)
    saved_out = refs.pop(0) if mode == 0 else None
    hidden_out = refs.pop(0) if mode == 1 else None
    gains_out = refs.pop(0) if mode == 0 else None
    stats_out = refs.pop(0) if mode != 2 and part == 0 else None
    wide = 1024
    total_width = 8192
    lane = lax.broadcasted_iota(jnp.int32, (1, LANES), 1)
    if mode == 0:
        gains = gains_out
        for q, (held, arrived) in enumerate(sums):
            columns = pl.ds(q * wide, wide)
            extra = held[pl.ds(128, EXTRA), pl.ds(0, wide)] + arrived[pl.ds(128, EXTRA), pl.ds(0, wide)].astype(f32)
            for r in range(8):
                gains[pl.ds(r, 1), columns] = jnp.sum(extra[3 * r : 3 * r + 3], axis=0, keepdims=True)
    if stats_out is not None:
        stats = stats_out
        held, arrived = sums[1]
        ext = held[pl.ds(0, 128), pl.ds(wide, LANES)] + arrived[pl.ds(0, 128), pl.ds(wide, LANES)].astype(f32)
        means = [sum(ext[:, 8 * k + r : 8 * k + r + 1] for k in range(3)) for r in range(8)]
        mean = sum(means) / 8
        shifts = [value - mean for value in means]
        squares = jnp.sum(jnp.where((lane >= 24) & (lane < 48), ext, 0.0), axis=1, keepdims=True)
        variance = (squares + wide * sum(value * value for value in shifts)) / total_width
        inv_std = lax.rsqrt(variance + epsilon)
        if mode == 0:
            inv_std = jnp.where(first, inv_std, 1.0)
            shifts = [jnp.where(first, value, 0.0) for value in shifts]
        out = jnp.where(lane == MEAN, mean, 0.0) + jnp.where(lane == INV, inv_std, 0.0)
        for r, value in enumerate(shifts):
            out = out + jnp.where(lane == SHIFT + r, value, 0.0)
        stats[...] = out

    size, span = 16, 512

    def block(i, carry):
        rows = pl.ds(pl.multiple_of(i * size, size), size)
        here = stats[rows, :]
        mean, inv_std = here[:, MEAN : MEAN + 1], here[:, INV : INV + 1]
        shifts = [here[:, SHIFT + r : SHIFT + r + 1] for r in range(8)]
        firsts = jnp.zeros((size, span), f32)
        seconds = jnp.zeros((size, span), f32)
        for n in range(2 * wide // span):
            columns = pl.ds(n * span, span)
            held, arrived = sums[n * span // wide]
            inner = pl.ds(n * span % wide, span)
            value = held[rows, inner] + arrived[rows, inner].astype(f32)
            if mode != 2:
                for r in range(8):
                    value = value + shifts[r] * gains[pl.ds(r, 1), columns]
                value = inv_std * value
            pre = saved[rows, columns] if mode == 2 else value
            if mode == 0:
                saved_out[rows, columns] = pre
                chunk[rows, columns] = gelu_value(pre).astype(bf16)
                continue
            tangent = gelu_tangent(pre)
            slope = 0.5 * (1.0 + tangent) + 0.5 * pre * (1.0 - tangent * tangent) * gelu_coeff * (
                1.0 + 3.0 * 0.044715 * pre * pre
            )
            grad = (value if mode == 2 else saved[rows, columns]) * slope
            grad_sent = grad.astype(bf16)
            if mode == 1:
                hidden_out[rows, columns] = (0.5 * pre * (1.0 + tangent)).astype(bf16)
                chunk[rows, columns] = grad_sent
            else:
                chunk[rows, columns] = jnp.where(first, grad_sent, hidden[rows, columns])
            grad = grad_sent.astype(f32)
            gain_sum = jnp.sum(gains[:, columns], axis=0, keepdims=True)
            firsts = firsts + grad * gain_sum
            seconds = seconds + grad * pre
        if mode:
            values = [
                jnp.sum(v, axis=1, keepdims=True) / total_width for v in (firsts, seconds)
            ] + ([mean, inv_std] if part else [])
            ext = jnp.zeros((size, LANES), f32)
            spot = 6 * part
            for value in values:
                for piece in pieces32(value):
                    ext = ext + jnp.where(lane == spot, piece, 0.0)
                    spot += 1
            chunk[rows, pl.ds(2 * wide, LANES)] = ext.astype(bf16)
        return carry

    lax.fori_loop(0, 128 // size, block, 0)


def act(mode, part, at, sums, stats, gains, saved, hidden):
    wide = 2048
    operands = [at] + [ref for pair in sums for ref in pair]
    if mode == 2 or part:
        operands.append(stats)
    if mode:
        operands += [gains, saved]
    if mode == 2:
        operands.append(hidden)
    shapes = [jax.ShapeDtypeStruct((128, wide + (LANES if mode else 0)), bf16)]
    if mode == 0:
        shapes.append(jax.ShapeDtypeStruct((128, wide), f32))
    if mode == 1:
        shapes.append(jax.ShapeDtypeStruct((128, wide), bf16))
    if mode == 0:
        shapes.append(jax.ShapeDtypeStruct((8, wide), f32))
    if mode != 2 and part == 0:
        shapes.append(jax.ShapeDtypeStruct((128, LANES), f32))
    return local_call(
        functools.partial(act_kernel, mode, part),
        shapes,
        operands,
        f"act_{mode}_{part}",
        40 * 128 * wide,
        16 * 128 * wide,
        smem=True,
    )


def finish_kernel(parts, base, out):
    total = base[...].astype(f32)
    for k in range(8):
        total = total + parts[k].astype(f32)
    total = total.astype(bf16)
    if len(out.shape) == 2:
        out[...] = total
    else:
        for k in range(8):
            out[k] = total


def finish(parts, base, copies):
    block, width = base.shape
    (out,) = local_call(
        finish_kernel,
        [jax.ShapeDtypeStruct((8, block, width) if copies else base.shape, bf16)],
        (parts, base),
        "finish",
        8 * block * width,
        20 * block * width,
    )
    return out


def permuted(array, axis, mapping):
    return lax.ppermute(array, axis, [(i, mapping(i)) for i in range(lax.axis_size(axis))])


def body(section_feeds, norm_gain, up_weight, down_weight):
    up = up_weight[0]
    down = down_weight[0]
    gain = norm_gain
    width, hidden = up.shape
    micro, rows = section_feeds.shape[1], section_feeds.shape[2]
    rsize, tsize = lax.axis_size("row"), lax.axis_size("tp")
    tokens = micro * rows
    block = tokens // tsize
    is_first = lax.axis_index("section") == 0
    row_at = lax.axis_index("row")
    tp_at = lax.axis_index("tp")
    core = row_at % 2
    at = jnp.stack([is_first.astype(jnp.int32), core, row_at])

    def to_global(array):
        blocks = array.reshape(micro, rows, width)
        return jnp.where(core == 0, blocks, blocks[::-1])

    def pair(i):
        return i ^ 1

    def near(i):
        return i ^ 2

    def far(i):
        return i ^ 6

    def row_sum(halves):
        sums = []
        for own, other in halves:
            arrived = permuted(other, "row", pair)
            for columns in (slice(0, hidden // 4), slice(hidden // 4, None)):
                sums.append(own[:, columns] + arrived[:, columns].astype(f32))
        ways = (near, far, near, far)
        arrived = [permuted(h.astype(bf16), "row", way) for h, way in zip(sums, ways)]
        sums = [h + r.astype(f32) for h, r in zip(sums, arrived)]
        ways = (far, near, far, near)
        arrived = [permuted(h.astype(bf16), "row", way) for h, way in zip(sums, ways)]
        quarters = list(zip(sums, arrived))
        return quarters[:2], quarters[2:]

    def swapped(chunks):
        return chunks, [permuted(chunk, "row", pair) for chunk in chunks]

    def along_tp(part):
        return lax.all_to_all(part, "tp", 0, 0)

    blocks = rows // block
    feeds = section_feeds[0].reshape(micro, blocks, block, width)
    own_feed = lax.dynamic_slice(
        feeds, ((core + tp_at // blocks) % 2, tp_at % blocks, 0, 0), (1, 1, block, width)
    )[0, 0]
    early, late = row_sum(start_in(at, feeds, gain, up, down))
    chunk, saved, gains, stats0 = act(0, 0, at, early, None, None, None, None)
    chunks, saved0, gain_rows = [chunk], [saved], [gains]
    chunk, saved, gains = act(0, 1, at, late, stats0, None, None, None)
    chunks, saved0, gain_rows = chunks + [chunk], saved0 + [saved], gain_rows + [gains]
    parts = along_tp(row_out(0, at, *swapped(chunks), (down,)))
    middle = lax.ppermute(finish(parts, own_feed, False), "section", [(0, 1)])
    middles = along_tp(jnp.broadcast_to(middle[None], (tsize,) + middle.shape))

    early, late = row_sum(up_in(at, middles, gain, up))
    chunk0, hidden0, stats1 = act(1, 0, at, early, None, gain_rows[0], saved0[0], None)
    chunk1, hidden1 = act(1, 1, at, late, stats1, gain_rows[1], saved0[1], None)
    chunks = [chunk0, chunk1]
    parts = along_tp(row_out(1, at, *swapped(chunks), (gain, middles, up)))
    back = lax.ppermute(finish(parts, own_feed, False), "section", [(1, 0)])
    backs = along_tp(jnp.broadcast_to(back[None], (tsize,) + back.shape))

    early, late = row_sum(down_back_in(backs, down))
    chunks = []
    for part, sums in enumerate((early, late)):
        kept = (hidden0, hidden1)[part]
        (chunk,) = act(2, part, at, sums, stats0, gain_rows[part], saved0[part], kept)
        chunks.append(chunk)
    parts = along_tp(row_out(2, at, *swapped(chunks), (gain, feeds, up, down)))
    base = jnp.where(is_first, back, middle)
    return to_global(along_tp(finish(parts, base, True)))[None]


def solution(mesh):
    placed = (
        P("section", None, None, "row"),
        P("section", "row"),
        P("section", "row", "tp"),
        P("section", "tp", "row"),
    )
    return jax.shard_map(
        body, mesh=mesh, in_specs=placed, out_specs=P("section", None, None, "row"), check_vma=False
    )
```

profile of v0, /device:TPU:0, one launch (start us, length us, event | category | flops | bytes accessed | tf_op | source)
XLA Modules:
  0.0 237.0 jit_solution(16285306220513199357)
XLA Ops:
  0.8 4.9 %start_in_0.1 = (f32[160,2176]{1,0:T(8,128)S(1)}, bf16[160,2176]{1,0:T(8,128)(2,1)S(1)}, bf16[288,1024]{1,0:T(8,128)(2,1)S(1)}) custom-call(s32[3]{0:T(128)S(1)} %pad_add_fusion.at, bf16[2,4,32,1024]{3,2,1,0:T(8,128)(2,1)} %bitcast.32, f32[1,1024]{1,0:T(1,128)S(1)} %copy-done.1, bf16[1024,4096]{1,0:T(8,128)(2,1)} %bitcast.12, bf16[4096,1024]{1,0:T(8,128)(2,1)} %bitcast.20), custom_call_target="tpu_custom_call" | custom-call | flops 1073741824 | bytes 4194304 | tf_op jit(solution)/shard_map/start_in_0/pallas_call | solution.py:160
  5.8 4.4 %start_in_1.1 = (f32[160,2048]{1,0:T(8,128)S(1)}, bf16[160,2048]{1,0:T(8,128)(2,1)S(1)}, bf16[16,1024]{1,0:T(8,128)(2,1)}) custom-call(s32[3]{0:T(128)S(1)} %pad_add_fusion.at, bf16[288,1024]{1,0:T(8,128)(2,1)S(1)} %get-tuple-element.34.x, f32[1,1024]{1,0:T(1,128)S(1)} %copy-done.1, bf16[1024,4096]{1,0:T(8,128)(2,1)} %bitcast.13, bf16[4096,1024]{1,0:T(8,128)(2,1)} %bitcast.21), custom_call_target="tpu_custom_call" | custom-call | flops 1073741824 | bytes 4194304 | tf_op jit(solution)/shard_map/start_in_1/pallas_call | solution.py:160
  17.0 4.4 %collective-permute-done.1 = bf16[160,1024]{1,0:T(8,128)(2,1)S(1)} collective-permute-done((bf16[160,1024]{1,0:T(8,128)(2,1)S(1)}, bf16[160,1024]{1,0:T(8,128)(2,1)S(1)}, u32[]{:S(2)}, u32[]{:S(2)}) %collective-permute-start.1) | collective-permute-done | bytes 327712 | tf_op jit(solution)/shard_map/ppermute | solution.py:513
  21.6 4.2 %collective-permute-start.2 = (bf16[160,1024]{1,0:T(8,128)(2,1)S(1)}, bf16[160,1024]{1,0:T(8,128)(2,1)S(1)}, u32[]{:S(2)}, u32[]{:S(2)}) collective-permute-start(bf16[160,1024]{1,0:T(8,128)(2,1)S(1)} %get-tuple-element.79), channel_id=1, source_target_pairs={{0,48},{8,56},{16,32},{24,40},{32,16},{40,24},{48,0},{56,8},{1,49}... | collective-permute-start | bytes 983048 | tf_op jit(solution)/shard_map/ppermute | solution.py:513
  26.3 6.5 %collective-permute-done.8 = bf16[160,1024]{1,0:T(8,128)(2,1)S(1)} collective-permute-done((bf16[160,1024]{1,0:T(8,128)(2,1)S(1)}, bf16[160,1024]{1,0:T(8,128)(2,1)S(1)}, u32[]{:S(2)}, u32[]{:S(2)}) %collective-permute-start.8) | collective-permute-done | bytes 327712 | tf_op jit(solution)/shard_map/ppermute | solution.py:513
  35.8 4.0 %collective-permute-done.2.refs_1_ = bf16[160,1024]{1,0:T(8,128)(2,1)S(1)} collective-permute-done((bf16[160,1024]{1,0:T(8,128)(2,1)S(1)}, bf16[160,1024]{1,0:T(8,128)(2,1)S(1)}, u32[]{:S(2)}, u32[]{:S(2)}) %collective-permute-start.2) | collective-permute-done | bytes 327712 | tf_op jit(solution)/shard_map/ppermute | solution.py:513
  39.8 3.1 %act_0_0.1 = (bf16[128,2048]{1,0:T(8,128)(2,1)S(1)}, f32[128,2048]{1,0:T(8,128)S(1)}, f32[8,2048]{1,0:T(8,128)S(1)}, f32[128,128]{1,0:T(8,128)S(1)}) custom-call(s32[3]{0:T(128)S(1)} %pad_add_fusion.at, f32[160,1024]{1,0:T(8,128)S(1)} %get-tuple-element.80.refs_0_, bf16[160,1024]{1,0:T(8,128)(2,1)S(1)} %collective-permute-done.2.refs_1_, ...), custom_call_target="tpu_custom_call" | custom-call | flops 10485760 | bytes 4194304 | tf_op jit(solution)/shard_map/act_0_0/pallas_call | solution.py:251
  49.9 4.0 %row_out_0.1 = bf16[8,32,1024]{2,1,0:T(8,128)(2,1)} custom-call(s32[3]{0:T(128)S(1)} %pad_add_fusion.at, bf16[128,2048]{1,0:T(8,128)(2,1)S(1)} %get-tuple-element.33.refs_0_, bf16[128,2048]{1,0:T(8,128)(2,1)S(1)} %get-tuple-element.38.refs_1_, bf16[128,2048]{1,0:T(8,128)(2,1)S(1)} %collective-permute-done.10.refs_2_, ...), custom_call_target="tpu_custom_call" | custom-call | flops 2147483648 | bytes 8388608 | tf_op jit(solution)/shard_map/row_out_0/pallas_call | solution.py:251
  53.9 5.3 %all-to-all-start = ((bf16[8,32,1024]{2,1,0:T(8,128)(2,1)}), bf16[8,32,1024]{2,1,0:T(8,128)(2,1)S(1)}, u32[]{:S(2)}, u32[]{:S(2)}) async-start(bf16[8,32,1024]{2,1,0:T(8,128)(2,1)} %row_out_0.1), calls=%async_computation | async-start | bytes 1048576 | tf_op jit(solution)/shard_map/all_to_all | solution.py:562
  59.3 9.7 %all-to-all-done.parts = bf16[8,32,1024]{2,1,0:T(8,128)(2,1)S(1)} async-done(((bf16[8,32,1024]{2,1,0:T(8,128)(2,1)}), bf16[8,32,1024]{2,1,0:T(8,128)(2,1)S(1)}, u32[]{:S(2)}, u32[]{:S(2)}) %all-to-all-start) | async-done | bytes 524320 | tf_op jit(solution)/shard_map/all_to_all | solution.py:562
  69.1 9.8 %collective-permute-start.12 = (bf16[32,1024]{1,0:T(8,128)(2,1)S(1)}, bf16[32,1024]{1,0:T(8,128)(2,1)S(1)}, u32[]{:S(2)}, u32[]{:S(2)}) collective-permute-start(bf16[32,1024]{1,0:T(8,128)(2,1)S(1)} %finish.3), channel_id=1, source_target_pairs={{0,64},{1,65},{2,66},{3,67},{4,68},{5,69},{6,70},{7,71},{8,72},{9,... | collective-permute-start | bytes 196616 | tf_op jit(solution)/shard_map/ppermute | solution.py:575
  80.9 11.2 %all_to_all.30.x.refs_5_ = bf16[8,32,1024]{2,1,0:T(8,128)(2,1)S(1)} all-to-all(bf16[8,32,1024]{2,1,0:T(8,128)(2,1)S(1)} %broadcast_in_dim.6), channel_id=1, replica_groups=mesh['section'=2,'row'=8,'tp'=8] {'tp'}, dimensions={0} | all-to-all | bytes 1048576 | tf_op jit(solution)/shard_map/all_to_all | solution.py:562
  92.1 3.6 %up_in_0.1 = (f32[128,2176]{1,0:T(8,128)S(1)}, bf16[128,2176]{1,0:T(8,128)(2,1)S(1)}, bf16[256,1024]{1,0:T(8,128)(2,1)S(1)}) custom-call(s32[3]{0:T(128)S(1)} %pad_add_fusion.at, bf16[8,32,1024]{2,1,0:T(8,128)(2,1)S(1)} %all_to_all.30.x.refs_5_, f32[1,1024]{1,0:T(1,128)S(1)} %copy-done.2, bf16[1024,4096]{1,0:T(8,128)(2,1)} %bitcast.14), custom_call_target="tpu_custom_call" | custom-call | flops 1073741824 | bytes 4194304 | tf_op jit(solution)/shard_map/up_in_0/pallas_call | solution.py:221
  96.0 3.6 %up_in_1.1 = (f32[128,2048]{1,0:T(8,128)S(1)}, bf16[128,2048]{1,0:T(8,128)(2,1)S(1)}, bf16[16,1024]{1,0:T(8,128)(2,1)}) custom-call(s32[3]{0:T(128)S(1)} %pad_add_fusion.at, bf16[256,1024]{1,0:T(8,128)(2,1)S(1)} %get-tuple-element.44.x, f32[1,1024]{1,0:T(1,128)S(1)} %copy-done.2, bf16[1024,4096]{1,0:T(8,128)(2,1)} %bitcast.15), custom_call_target="tpu_custom_call" | custom-call | flops 1073741824 | bytes 4194304 | tf_op jit(solution)/shard_map/up_in_1/pallas_call | solution.py:221
  104.7 4.7 %collective-permute-done.14 = bf16[128,1024]{1,0:T(8,128)(2,1)S(1)} collective-permute-done((bf16[128,1024]{1,0:T(8,128)(2,1)S(1)}, bf16[128,1024]{1,0:T(8,128)(2,1)S(1)}, u32[]{:S(2)}, u32[]{:S(2)}) %collective-permute-start.14) | collective-permute-done | bytes 262176 | tf_op jit(solution)/shard_map/ppermute | solution.py:513
  109.5 2.6 %collective-permute-start.15 = (bf16[128,1024]{1,0:T(8,128)(2,1)S(1)}, bf16[128,1024]{1,0:T(8,128)(2,1)S(1)}, u32[]{:S(2)}, u32[]{:S(2)}) collective-permute-start(bf16[128,1024]{1,0:T(8,128)(2,1)S(1)} %get-tuple-element.71), channel_id=1, source_target_pairs={{0,48},{8,56},{16,32},{24,40},{32,16},{40,24},{48,0},{56,8},{1,49}... | collective-permute-start | bytes 786440 | tf_op jit(solution)/shard_map/ppermute | solution.py:513
  112.5 5.2 %collective-permute-done.21 = bf16[128,1024]{1,0:T(8,128)(2,1)S(1)} collective-permute-done((bf16[128,1024]{1,0:T(8,128)(2,1)S(1)}, bf16[128,1024]{1,0:T(8,128)(2,1)S(1)}, u32[]{:S(2)}, u32[]{:S(2)}) %collective-permute-start.21) | collective-permute-done | bytes 262176 | tf_op jit(solution)/shard_map/ppermute | solution.py:513
  120.4 2.9 %collective-permute-done.15.refs_1_ = bf16[128,1024]{1,0:T(8,128)(2,1)S(1)} collective-permute-done((bf16[128,1024]{1,0:T(8,128)(2,1)S(1)}, bf16[128,1024]{1,0:T(8,128)(2,1)S(1)}, u32[]{:S(2)}, u32[]{:S(2)}) %collective-permute-start.15) | collective-permute-done | bytes 262176 | tf_op jit(solution)/shard_map/ppermute | solution.py:513
  123.3 4.4 %act_1_0.1 = (bf16[128,2176]{1,0:T(8,128)(2,1)S(1)}, bf16[128,2048]{1,0:T(8,128)(2,1)S(1)}, f32[128,128]{1,0:T(8,128)S(1)}) custom-call(s32[3]{0:T(128)S(1)} %pad_add_fusion.at, f32[128,1024]{1,0:T(8,128)S(1)} %get-tuple-element.72.refs_0_, bf16[128,1024]{1,0:T(8,128)(2,1)S(1)} %collective-permute-done.15.refs_1_, ...), custom_call_target="tpu_custom_call" | custom-call | flops 10485760 | bytes 4194304 | tf_op jit(solution)/shard_map/act_1_0/pallas_call | solution.py:251
  127.8 4.0 %act_1_1.1 = (bf16[128,2176]{1,0:T(8,128)(2,1)S(1)}, bf16[128,2048]{1,0:T(8,128)(2,1)S(1)}) custom-call(s32[3]{0:T(128)S(1)} %pad_add_fusion.at, f32[128,1024]{1,0:T(8,128)S(1)} %get-tuple-element.94.refs_0_, bf16[128,1024]{1,0:T(8,128)(2,1)S(1)} %collective-permute-done.20.refs_1_, f32[128,1024]{1,0:T(8,128)S(1)} %get-tuple-element.66.refs_2_, ...), custom_call_target="tpu_custom_call" | custom-call | flops 10485760 | bytes 4194304 | tf_op jit(solution)/shard_map/act_1_1/pallas_call | solution.py:251
  134.0 3.4 %row_out_1.1 = bf16[8,32,1024]{2,1,0:T(8,128)(2,1)S(1)} custom-call(s32[3]{0:T(128)S(1)} %pad_add_fusion.at, bf16[128,2176]{1,0:T(8,128)(2,1)S(1)} %get-tuple-element.43.refs_0_, bf16[128,2176]{1,0:T(8,128)(2,1)S(1)} %get-tuple-element.50.refs_1_, bf16[128,2176]{1,0:T(8,128)(2,1)S(1)} %collective-permute-done.23.refs_2_, ...), custom_call_target="tpu_custom_call" | custom-call | flops 2147483648 | bytes 8388608 | tf_op jit(solution)/shard_map/row_out_1/pallas_call | solution.py:251
  137.4 13.0 %all_to_all.31.parts = bf16[8,32,1024]{2,1,0:T(8,128)(2,1)S(1)} all-to-all(bf16[8,32,1024]{2,1,0:T(8,128)(2,1)S(1)} %row_out_1.1), channel_id=1, replica_groups=mesh['section'=2,'row'=8,'tp'=8] {'tp'}, dimensions={0} | all-to-all | bytes 1048576 | tf_op jit(solution)/shard_map/all_to_all | solution.py:562
  151.8 6.5 %collective-permute-done.25 = bf16[32,1024]{1,0:T(8,128)(2,1)S(1)} collective-permute-done((bf16[32,1024]{1,0:T(8,128)(2,1)S(1)}, bf16[32,1024]{1,0:T(8,128)(2,1)S(1)}, u32[]{:S(2)}, u32[]{:S(2)}) %collective-permute-start.25) | collective-permute-done | bytes 65568 | tf_op jit(solution)/shard_map/ppermute | solution.py:583
  158.3 11.0 %all_to_all.32 = bf16[8,32,1024]{2,1,0:T(8,128)(2,1)S(1)} all-to-all(bf16[8,32,1024]{2,1,0:T(8,128)(2,1)S(1)} %broadcast_in_dim.7), channel_id=1, replica_groups=mesh['section'=2,'row'=8,'tp'=8] {'tp'}, dimensions={0} | all-to-all | bytes 1048576 | tf_op jit(solution)/shard_map/all_to_all | solution.py:562
  177.8 5.5 %collective-permute-done.29 = bf16[128,1024]{1,0:T(8,128)(2,1)S(1)} collective-permute-done((bf16[128,1024]{1,0:T(8,128)(2,1)S(1)}, bf16[128,1024]{1,0:T(8,128)(2,1)S(1)}, u32[]{:S(2)}, u32[]{:S(2)}) %collective-permute-start.29) | collective-permute-done | bytes 262176 | tf_op jit(solution)/shard_map/ppermute | solution.py:513
  186.2 2.7 %collective-permute-done.34 = bf16[128,1024]{1,0:T(8,128)(2,1)S(1)} collective-permute-done((bf16[128,1024]{1,0:T(8,128)(2,1)S(1)}, bf16[128,1024]{1,0:T(8,128)(2,1)S(1)}, u32[]{:S(2)}, u32[]{:S(2)}) %collective-permute-start.34) | collective-permute-done | bytes 262176 | tf_op jit(solution)/shard_map/ppermute | solution.py:513
  191.6 3.6 %collective-permute-done.28.refs_1_ = bf16[128,1024]{1,0:T(8,128)(2,1)S(1)} collective-permute-done((bf16[128,1024]{1,0:T(8,128)(2,1)S(1)}, bf16[128,1024]{1,0:T(8,128)(2,1)S(1)}, u32[]{:S(2)}, u32[]{:S(2)}) %collective-permute-start.28) | collective-permute-done | bytes 262176 | tf_op jit(solution)/shard_map/ppermute | solution.py:513
  204.8 4.3 %row_out_2.1 = bf16[8,32,1024]{2,1,0:T(8,128)(2,1)} custom-call(s32[3]{0:T(128)S(1)} %pad_add_fusion.at, bf16[128,2176]{1,0:T(8,128)(2,1)S(1)} %act_2_0.1.refs_0_, bf16[128,2176]{1,0:T(8,128)(2,1)S(1)} %act_2_1.1.refs_1_, bf16[128,2176]{1,0:T(8,128)(2,1)S(1)} %collective-permute-done.36.refs_2_, bf16[128,2176]{1,0:T(8,128)(2,1)S(1)} %collective-permute-done.37.refs_3_, ...), custom_call_target="tpu_custom_call" | custom-call | flops 2147483648 | bytes 8388608 | tf_op jit(solution)/shard_map/row_out_2/pallas_call | solution.py:251
  209.1 3.5 %all-to-all-start.4 = ((bf16[8,32,1024]{2,1,0:T(8,128)(2,1)}), bf16[8,32,1024]{2,1,0:T(8,128)(2,1)S(1)}, u32[]{:S(2)}, u32[]{:S(2)}) async-start(bf16[8,32,1024]{2,1,0:T(8,128)(2,1)} %row_out_2.1), calls=%async_computation.4 | async-start | bytes 1048576 | tf_op jit(solution)/shard_map/all_to_all | solution.py:562
  212.6 9.9 %all-to-all-done.4.parts = bf16[8,32,1024]{2,1,0:T(8,128)(2,1)S(1)} async-done(((bf16[8,32,1024]{2,1,0:T(8,128)(2,1)}), bf16[8,32,1024]{2,1,0:T(8,128)(2,1)S(1)}, u32[]{:S(2)}, u32[]{:S(2)}) %all-to-all-start.4) | async-done | bytes 524320 | tf_op jit(solution)/shard_map/all_to_all | solution.py:562
  223.4 3.5 %all-to-all-start.5 = ((bf16[8,32,1024]{2,1,0:T(8,128)(2,1)}), bf16[8,32,1024]{2,1,0:T(8,128)(2,1)S(1)}, u32[]{:S(2)}, u32[]{:S(2)}) async-start(bf16[8,32,1024]{2,1,0:T(8,128)(2,1)} %finish.5), calls=%async_computation.5 | async-start | bytes 1048576 | tf_op jit(solution)/shard_map/all_to_all | solution.py:562
  226.9 9.1 %all-to-all-done.5 = bf16[8,32,1024]{2,1,0:T(8,128)(2,1)S(1)} async-done(((bf16[8,32,1024]{2,1,0:T(8,128)(2,1)}), bf16[8,32,1024]{2,1,0:T(8,128)(2,1)S(1)}, u32[]{:S(2)}, u32[]{:S(2)}) %all-to-all-start.5) | async-done | bytes 524320 | tf_op jit(solution)/shard_map/all_to_all | solution.py:562
  (114 shorter events, 57.7 us)
Async XLA Ops:
  5.7 5.1 %collective-permute-start = (bf16[160,2176]{1,0:T(8,128)(2,1)S(1)}, bf16[160,2176]{1,0:T(8,128)(2,1)S(1)}, u32[]{:S(2)}, u32[]{:S(2)}) collective-permute-start(bf16[160,2176]{1,0:T(8,128)(2,1)S(1)} %get-tuple-element.32), channel_id=1, source_target_pairs={{0,8},{8,0},{16,24},{24,16},{32,40},{40,32},{48,56},{56,48},{1,9},... | collective-permute-start | bytes 2088968 | tf_op jit(solution)/shard_map/ppermute | solution.py:513
  10.2 5.4 %collective-permute-start.5 = (bf16[160,2048]{1,0:T(8,128)(2,1)S(1)}, bf16[160,2048]{1,0:T(8,128)(2,1)S(1)}, u32[]{:S(2)}, u32[]{:S(2)}) collective-permute-start(bf16[160,2048]{1,0:T(8,128)(2,1)S(1)} %get-tuple-element.36), channel_id=1, source_target_pairs={{0,8},{8,0},{16,24},{24,16},{32,40},{40,32},{48,56},{56,48},{1,9},... | collective-permute-start | bytes 1966088 | tf_op jit(solution)/shard_map/ppermute | solution.py:513
  10.9 10.6 %collective-permute-start.1 = (bf16[160,1024]{1,0:T(8,128)(2,1)S(1)}, bf16[160,1024]{1,0:T(8,128)(2,1)S(1)}, u32[]{:S(2)}, u32[]{:S(2)}) collective-permute-start(bf16[160,1024]{1,0:T(8,128)(2,1)S(1)} %fusion.2), channel_id=1, source_target_pairs={{0,16},{8,24},{16,0},{24,8},{32,48},{40,56},{48,32},{56,40},{1,17}... | collective-permute-start | bytes 983048 | tf_op jit(solution)/shard_map/ppermute | solution.py:513
  13.0 12.8 %collective-permute-start.3 = (bf16[160,1152]{1,0:T(8,128)(2,1)S(1)}, bf16[160,1152]{1,0:T(8,128)(2,1)S(1)}, u32[]{:S(2)}, u32[]{:S(2)}) collective-permute-start(bf16[160,1152]{1,0:T(8,128)(2,1)S(1)} %fusion.1), channel_id=1, source_target_pairs={{0,48},{8,56},{16,32},{24,40},{32,16},{40,24},{48,0},{56,8},{1,49}... | collective-permute-start | bytes 1105928 | tf_op jit(solution)/shard_map/ppermute | solution.py:513
  15.8 17.0 %collective-permute-start.8 = (bf16[160,1024]{1,0:T(8,128)(2,1)S(1)}, bf16[160,1024]{1,0:T(8,128)(2,1)S(1)}, u32[]{:S(2)}, u32[]{:S(2)}) collective-permute-start(bf16[160,1024]{1,0:T(8,128)(2,1)S(1)} %get-tuple-element.83), channel_id=1, source_target_pairs={{0,48},{8,56},{16,32},{24,40},{32,16},{40,24},{48,0},{56,8},{1,49}... | collective-permute-start | bytes 983048 | tf_op jit(solution)/shard_map/ppermute | solution.py:513
  16.9 15.9 %collective-permute-start.6 = (bf16[160,1024]{1,0:T(8,128)(2,1)S(1)}, bf16[160,1024]{1,0:T(8,128)(2,1)S(1)}, u32[]{:S(2)}, u32[]{:S(2)}) collective-permute-start(bf16[160,1024]{1,0:T(8,128)(2,1)S(1)} %get-tuple-element.84), channel_id=1, source_target_pairs={{0,16},{8,24},{16,0},{24,8},{32,48},{40,56},{48,32},{56,40},{1,17}... | collective-permute-start | bytes 983048 | tf_op jit(solution)/shard_map/ppermute | solution.py:513
  21.6 18.2 %collective-permute-start.2 = (bf16[160,1024]{1,0:T(8,128)(2,1)S(1)}, bf16[160,1024]{1,0:T(8,128)(2,1)S(1)}, u32[]{:S(2)}, u32[]{:S(2)}) collective-permute-start(bf16[160,1024]{1,0:T(8,128)(2,1)S(1)} %get-tuple-element.79), channel_id=1, source_target_pairs={{0,48},{8,56},{16,32},{24,40},{32,16},{40,24},{48,0},{56,8},{1,49}... | collective-permute-start | bytes 983048 | tf_op jit(solution)/shard_map/ppermute | solution.py:513
  26.0 13.8 %collective-permute-start.4 = (bf16[160,1152]{1,0:T(8,128)(2,1)S(1)}, bf16[160,1152]{1,0:T(8,128)(2,1)S(1)}, u32[]{:S(2)}, u32[]{:S(2)}) collective-permute-start(bf16[160,1152]{1,0:T(8,128)(2,1)S(1)} %get-tuple-element.77), channel_id=1, source_target_pairs={{0,16},{8,24},{16,0},{24,8},{32,48},{40,56},{48,32},{56,40},{1,17}... | collective-permute-start | bytes 1105928 | tf_op jit(solution)/shard_map/ppermute | solution.py:513
  33.2 12.4 %collective-permute-start.7 = (bf16[160,1024]{1,0:T(8,128)(2,1)S(1)}, bf16[160,1024]{1,0:T(8,128)(2,1)S(1)}, u32[]{:S(2)}, u32[]{:S(2)}) collective-permute-start(bf16[160,1024]{1,0:T(8,128)(2,1)S(1)} %get-tuple-element.81), channel_id=1, source_target_pairs={{0,48},{8,56},{16,32},{24,40},{32,16},{40,24},{48,0},{56,8},{1,49}... | collective-permute-start | bytes 983048 | tf_op jit(solution)/shard_map/ppermute | solution.py:513
  35.8 9.8 %collective-permute-start.9 = (bf16[160,1024]{1,0:T(8,128)(2,1)S(1)}, bf16[160,1024]{1,0:T(8,128)(2,1)S(1)}, u32[]{:S(2)}, u32[]{:S(2)}) collective-permute-start(bf16[160,1024]{1,0:T(8,128)(2,1)S(1)} %get-tuple-element.73), channel_id=1, source_target_pairs={{0,16},{8,24},{16,0},{24,8},{32,48},{40,56},{48,32},{56,40},{1,17}... | collective-permute-start | bytes 983048 | tf_op jit(solution)/shard_map/ppermute | solution.py:513
  42.9 5.1 %collective-permute-start.10 = (bf16[128,2048]{1,0:T(8,128)(2,1)S(1)}, bf16[128,2048]{1,0:T(8,128)(2,1)S(1)}, u32[]{:S(2)}, u32[]{:S(2)}) collective-permute-start(bf16[128,2048]{1,0:T(8,128)(2,1)S(1)} %get-tuple-element.33.refs_0_), channel_id=1, source_target_pairs={{0,8},{8,0},{16,24},{24,16},{32,40},{40,32},{48,56},{56,48},{1,9},... | collective-permute-start | bytes 1572872 | tf_op jit(solution)/shard_map/ppermute | solution.py:513
  53.9 15.1 %all-to-all-start = ((bf16[8,32,1024]{2,1,0:T(8,128)(2,1)}), bf16[8,32,1024]{2,1,0:T(8,128)(2,1)S(1)}, u32[]{:S(2)}, u32[]{:S(2)}) async-start(bf16[8,32,1024]{2,1,0:T(8,128)(2,1)} %row_out_0.1), calls=%async_computation | async-start | bytes 1048576 | tf_op jit(solution)/shard_map/all_to_all | solution.py:562
  69.1 11.7 %collective-permute-start.12 = (bf16[32,1024]{1,0:T(8,128)(2,1)S(1)}, bf16[32,1024]{1,0:T(8,128)(2,1)S(1)}, u32[]{:S(2)}, u32[]{:S(2)}) collective-permute-start(bf16[32,1024]{1,0:T(8,128)(2,1)S(1)} %finish.3), channel_id=1, source_target_pairs={{0,64},{1,65},{2,66},{3,67},{4,68},{5,69},{6,70},{7,71},{8,72},{9,... | collective-permute-start | bytes 196616 | tf_op jit(solution)/shard_map/ppermute | solution.py:575
  100.2 9.2 %collective-permute-start.14 = (bf16[128,1024]{1,0:T(8,128)(2,1)S(1)}, bf16[128,1024]{1,0:T(8,128)(2,1)S(1)}, u32[]{:S(2)}, u32[]{:S(2)}) collective-permute-start(bf16[128,1024]{1,0:T(8,128)(2,1)S(1)} %fusion.6), channel_id=1, source_target_pairs={{0,16},{8,24},{16,0},{24,8},{32,48},{40,56},{48,32},{56,40},{1,17}... | collective-permute-start | bytes 786440 | tf_op jit(solution)/shard_map/ppermute | solution.py:513
  100.9 11.2 %collective-permute-start.16 = (bf16[128,1152]{1,0:T(8,128)(2,1)S(1)}, bf16[128,1152]{1,0:T(8,128)(2,1)S(1)}, u32[]{:S(2)}, u32[]{:S(2)}) collective-permute-start(bf16[128,1152]{1,0:T(8,128)(2,1)S(1)} %fusion.5), channel_id=1, source_target_pairs={{0,48},{8,56},{16,32},{24,40},{32,16},{40,24},{48,0},{56,8},{1,49}... | collective-permute-start | bytes 884744 | tf_op jit(solution)/shard_map/ppermute | solution.py:513
  103.5 14.2 %collective-permute-start.21 = (bf16[128,1024]{1,0:T(8,128)(2,1)S(1)}, bf16[128,1024]{1,0:T(8,128)(2,1)S(1)}, u32[]{:S(2)}, u32[]{:S(2)}) collective-permute-start(bf16[128,1024]{1,0:T(8,128)(2,1)S(1)} %get-tuple-element.95), channel_id=1, source_target_pairs={{0,48},{8,56},{16,32},{24,40},{32,16},{40,24},{48,0},{56,8},{1,49}... | collective-permute-start | bytes 786440 | tf_op jit(solution)/shard_map/ppermute | solution.py:513
  104.5 13.3 %collective-permute-start.19 = (bf16[128,1024]{1,0:T(8,128)(2,1)S(1)}, bf16[128,1024]{1,0:T(8,128)(2,1)S(1)}, u32[]{:S(2)}, u32[]{:S(2)}) collective-permute-start(bf16[128,1024]{1,0:T(8,128)(2,1)S(1)} %get-tuple-element.96), channel_id=1, source_target_pairs={{0,16},{8,24},{16,0},{24,8},{32,48},{40,56},{48,32},{56,40},{1,17}... | collective-permute-start | bytes 786440 | tf_op jit(solution)/shard_map/ppermute | solution.py:513
  109.5 13.8 %collective-permute-start.15 = (bf16[128,1024]{1,0:T(8,128)(2,1)S(1)}, bf16[128,1024]{1,0:T(8,128)(2,1)S(1)}, u32[]{:S(2)}, u32[]{:S(2)}) collective-permute-start(bf16[128,1024]{1,0:T(8,128)(2,1)S(1)} %get-tuple-element.71), channel_id=1, source_target_pairs={{0,48},{8,56},{16,32},{24,40},{32,16},{40,24},{48,0},{56,8},{1,49}... | collective-permute-start | bytes 786440 | tf_op jit(solution)/shard_map/ppermute | solution.py:513
  112.2 11.1 %collective-permute-start.17 = (bf16[128,1152]{1,0:T(8,128)(2,1)S(1)}, bf16[128,1152]{1,0:T(8,128)(2,1)S(1)}, u32[]{:S(2)}, u32[]{:S(2)}) collective-permute-start(bf16[128,1152]{1,0:T(8,128)(2,1)S(1)} %get-tuple-element.69), channel_id=1, source_target_pairs={{0,16},{8,24},{16,0},{24,8},{32,48},{40,56},{48,32},{56,40},{1,17}... | collective-permute-start | bytes 884744 | tf_op jit(solution)/shard_map/ppermute | solution.py:513
  118.0 9.8 %collective-permute-start.20 = (bf16[128,1024]{1,0:T(8,128)(2,1)S(1)}, bf16[128,1024]{1,0:T(8,128)(2,1)S(1)}, u32[]{:S(2)}, u32[]{:S(2)}) collective-permute-start(bf16[128,1024]{1,0:T(8,128)(2,1)S(1)} %get-tuple-element.93), channel_id=1, source_target_pairs={{0,48},{8,56},{16,32},{24,40},{32,16},{40,24},{48,0},{56,8},{1,49}... | collective-permute-start | bytes 786440 | tf_op jit(solution)/shard_map/ppermute | solution.py:513
  120.4 7.4 %collective-permute-start.22 = (bf16[128,1024]{1,0:T(8,128)(2,1)S(1)}, bf16[128,1024]{1,0:T(8,128)(2,1)S(1)}, u32[]{:S(2)}, u32[]{:S(2)}) collective-permute-start(bf16[128,1024]{1,0:T(8,128)(2,1)S(1)} %get-tuple-element.65), channel_id=1, source_target_pairs={{0,16},{8,24},{16,0},{24,8},{32,48},{40,56},{48,32},{56,40},{1,17}... | collective-permute-start | bytes 786440 | tf_op jit(solution)/shard_map/ppermute | solution.py:513
  150.5 7.8 %collective-permute-start.25 = (bf16[32,1024]{1,0:T(8,128)(2,1)S(1)}, bf16[32,1024]{1,0:T(8,128)(2,1)S(1)}, u32[]{:S(2)}, u32[]{:S(2)}) collective-permute-start(bf16[32,1024]{1,0:T(8,128)(2,1)S(1)} %finish.4), channel_id=1, source_target_pairs={{64,0},{65,1},{66,2},{67,3},{68,4},{69,5},{70,6},{71,7},{72,8},{73... | collective-permute-start | bytes 196616 | tf_op jit(solution)/shard_map/ppermute | solution.py:583
  172.8 10.4 %collective-permute-start.29 = (bf16[128,1024]{1,0:T(8,128)(2,1)S(1)}, bf16[128,1024]{1,0:T(8,128)(2,1)S(1)}, u32[]{:S(2)}, u32[]{:S(2)}) collective-permute-start(bf16[128,1024]{1,0:T(8,128)(2,1)S(1)} %get-tuple-element.91), channel_id=1, source_target_pairs={{0,48},{8,56},{16,32},{24,40},{32,16},{40,24},{48,0},{56,8},{1,49}... | collective-permute-start | bytes 786440 | tf_op jit(solution)/shard_map/ppermute | solution.py:513
  175.3 9.2 %collective-permute-start.27 = (bf16[128,1024]{1,0:T(8,128)(2,1)S(1)}, bf16[128,1024]{1,0:T(8,128)(2,1)S(1)}, u32[]{:S(2)}, u32[]{:S(2)}) collective-permute-start(bf16[128,1024]{1,0:T(8,128)(2,1)S(1)} %get-tuple-element.92), channel_id=1, source_target_pairs={{0,16},{8,24},{16,0},{24,8},{32,48},{40,56},{48,32},{56,40},{1,17}... | collective-permute-start | bytes 786440 | tf_op jit(solution)/shard_map/ppermute | solution.py:513
  175.4 13.5 %collective-permute-start.34 = (bf16[128,1024]{1,0:T(8,128)(2,1)S(1)}, bf16[128,1024]{1,0:T(8,128)(2,1)S(1)}, u32[]{:S(2)}, u32[]{:S(2)}) collective-permute-start(bf16[128,1024]{1,0:T(8,128)(2,1)S(1)} %get-tuple-element.87), channel_id=1, source_target_pairs={{0,48},{8,56},{16,32},{24,40},{32,16},{40,24},{48,0},{56,8},{1,49}... | collective-permute-start | bytes 786440 | tf_op jit(solution)/shard_map/ppermute | solution.py:513
  176.8 13.3 %collective-permute-start.32 = (bf16[128,1024]{1,0:T(8,128)(2,1)S(1)}, bf16[128,1024]{1,0:T(8,128)(2,1)S(1)}, u32[]{:S(2)}, u32[]{:S(2)}) collective-permute-start(bf16[128,1024]{1,0:T(8,128)(2,1)S(1)} %get-tuple-element.88), channel_id=1, source_target_pairs={{0,16},{8,24},{16,0},{24,8},{32,48},{40,56},{48,32},{56,40},{1,17}... | collective-permute-start | bytes 786440 | tf_op jit(solution)/shard_map/ppermute | solution.py:513
  184.7 10.5 %collective-permute-start.28 = (bf16[128,1024]{1,0:T(8,128)(2,1)S(1)}, bf16[128,1024]{1,0:T(8,128)(2,1)S(1)}, u32[]{:S(2)}, u32[]{:S(2)}) collective-permute-start(bf16[128,1024]{1,0:T(8,128)(2,1)S(1)} %get-tuple-element.89), channel_id=1, source_target_pairs={{0,48},{8,56},{16,32},{24,40},{32,16},{40,24},{48,0},{56,8},{1,49}... | collective-permute-start | bytes 786440 | tf_op jit(solution)/shard_map/ppermute | solution.py:513
  186.2 9.5 %collective-permute-start.30 = (bf16[128,1024]{1,0:T(8,128)(2,1)S(1)}, bf16[128,1024]{1,0:T(8,128)(2,1)S(1)}, u32[]{:S(2)}, u32[]{:S(2)}) collective-permute-start(bf16[128,1024]{1,0:T(8,128)(2,1)S(1)} %get-tuple-element.61), channel_id=1, source_target_pairs={{0,16},{8,24},{16,0},{24,8},{32,48},{40,56},{48,32},{56,40},{1,17}... | collective-permute-start | bytes 786440 | tf_op jit(solution)/shard_map/ppermute | solution.py:513
  190.4 9.0 %collective-permute-start.33 = (bf16[128,1024]{1,0:T(8,128)(2,1)S(1)}, bf16[128,1024]{1,0:T(8,128)(2,1)S(1)}, u32[]{:S(2)}, u32[]{:S(2)}) collective-permute-start(bf16[128,1024]{1,0:T(8,128)(2,1)S(1)} %get-tuple-element.85), channel_id=1, source_target_pairs={{0,48},{8,56},{16,32},{24,40},{32,16},{40,24},{48,0},{56,8},{1,49}... | collective-permute-start | bytes 786440 | tf_op jit(solution)/shard_map/ppermute | solution.py:513
  191.6 8.6 %collective-permute-start.35 = (bf16[128,1024]{1,0:T(8,128)(2,1)S(1)}, bf16[128,1024]{1,0:T(8,128)(2,1)S(1)}, u32[]{:S(2)}, u32[]{:S(2)}) collective-permute-start(bf16[128,1024]{1,0:T(8,128)(2,1)S(1)} %get-tuple-element.57), channel_id=1, source_target_pairs={{0,16},{8,24},{16,0},{24,8},{32,48},{40,56},{48,32},{56,40},{1,17}... | collective-permute-start | bytes 786440 | tf_op jit(solution)/shard_map/ppermute | solution.py:513
  209.1 13.5 %all-to-all-start.4 = ((bf16[8,32,1024]{2,1,0:T(8,128)(2,1)}), bf16[8,32,1024]{2,1,0:T(8,128)(2,1)S(1)}, u32[]{:S(2)}, u32[]{:S(2)}) async-start(bf16[8,32,1024]{2,1,0:T(8,128)(2,1)} %row_out_2.1), calls=%async_computation.4 | async-start | bytes 1048576 | tf_op jit(solution)/shard_map/all_to_all | solution.py:562
  223.4 12.6 %all-to-all-start.5 = ((bf16[8,32,1024]{2,1,0:T(8,128)(2,1)}), bf16[8,32,1024]{2,1,0:T(8,128)(2,1)S(1)}, u32[]{:S(2)}, u32[]{:S(2)}) async-start(bf16[8,32,1024]{2,1,0:T(8,128)(2,1)} %finish.5), calls=%async_computation.5 | async-start | bytes 1048576 | tf_op jit(solution)/shard_map/all_to_all | solution.py:562
  (18 other events, 263.7 us)
where the time goes:
time: 237 us
  waiting for transfers between devices  89.6 us (38%)
  starting transfers between devices  56.6 us (24%)
  Pallas kernels  50.6 us (21%)
  blocking collectives  35.2 us (15%)
  other arithmetic  3.56 us (2%)
    ppermute x36, waiting for transfers between devices, permuted(): lax.ppermute(array, axis, [(i, mapping(i)) for i in range(lax.axis_size(a...  52.4 us
    all_to_all x3, blocking collectives, along_tp(): return lax.all_to_all(part, 'tp', 0, 0)  35.2 us
    pallas_call x14, Pallas kernels, local_call(): pl.pallas_call(kernel, out_shape=shapes, in_specs=specs, out_specs=[VMEM]...  34.1 us
    ppermute x36, starting transfers between devices, permuted(): lax.ppermute(array, axis, [(i, mapping(i)) for i in range(lax.axis_size(a...  33.3 us
    all_to_all x3, waiting for transfers between devices, along_tp(): return lax.all_to_all(part, 'tp', 0, 0)  28.8 us
    all_to_all x3, starting transfers between devices, along_tp(): return lax.all_to_all(part, 'tp', 0, 0)  12.3 us
    ppermute x1, starting transfers between devices, body(): middle = lax.ppermute(finish(parts, own_feed, False), 'section', [(0, 1)])  9.8 us
    pallas_call x2, Pallas kernels, start_in(): pl.pallas_call(functools.partial(start_kernel, part), out_shape=half_shap...  9.33 us
  transfers between devices with their start and end apart: 41, of which 23 were waited for; matrix products, arithmetic and copies ran while one was open for 1% of the time, Pallas kernels for 12%

commit v1 on v0

--- a/solution.py
+++ b/solution.py
@@ -71,178 +71,153 @@
     other[pl.ds(0, half), columns] = result[half:].astype(bf16)
 
 
-def start_kernel(part, at, x, gain, up, down, *refs):
-    outs, (xs_out, x_here, up_tiles, down_tiles, sems) = refs[:2], refs[2:]
-    own, other = outs
+def start_kernel(at, x, gain, up, down, *refs):
+    outs, (xs, x_here, gain_here, up_tiles, down_tiles, sems) = refs[:4], refs[4:]
     first = at[0] == 1
     core, row_at = at[1], at[2]
     count, _, wide = up_tiles.shape
     half = outs[0].shape[0] - EXTRA
-
-    def tile(n):
-        return pl.ds((part * count + n) * wide, wide)
+    columns = outs[2].shape[1]
 
     def up_copy(n):
-        return pltpu.make_async_copy(up.at[:, tile(n)], up_tiles.at[n], sems.at[0, n])
+        return pltpu.make_async_copy(up.at[:, pl.ds(n * wide, wide)], up_tiles.at[n], sems.at[0, n])
 
     def down_copy(n):
-        return pltpu.make_async_copy(down.at[tile(n)], down_tiles.at[n], sems.at[1, n])
-
-    if part == 0:
-        x_copy = pltpu.make_async_copy(x, x_here, sems.at[2, 0])
-        x_copy.start()
-    for n in range(count):
-        up_copy(n).start()
+        return pltpu.make_async_copy(down.at[pl.ds(n * wide, wide)], down_tiles.at[n], sems.at[1, n])
+
+    x_copy = pltpu.make_async_copy(x, x_here, sems.at[2, 0])
+    gain_copy = pltpu.make_async_copy(gain, gain_here, sems.at[2, 1])
+    x_copy.start()
+    gain_copy.start()
 
     @pl.when(jnp.logical_not(first))
     def _():
         for n in range(count):
             down_copy(n).start()
 
-    if part == 0:
-        x_copy.wait()
-        gain_row = gain[...]
-        for kk in range(2):
-
-            def prepare(p, carry):
-                raw = x_here[(core + kk) % 2, p]
-                scaled, stats = norm_stats(raw, gain_row)
-                rows = pl.ds(pl.multiple_of((kk * 4 + p) * 32, 32), 32)
-                xs_out[rows, :] = jnp.where(first, scaled, raw)
-                put_stats(outs[kk], pl.multiple_of(p * 32, 32), count * wide, stats, row_at)
-                return carry
-
-            lax.fori_loop(0, 4, prepare, 0)
-        xs_out[pl.ds(2 * half, EXTRA), :] = placed(pieces32(gain_row), row_at).astype(bf16)
-        for to in outs[:2]:
-            to[pl.ds(half, EXTRA), pl.ds(count * wide, LANES)] = jnp.zeros((EXTRA, LANES), to.dtype)
-        xs = xs_out
-    else:
-        xs = x
-
     for n in range(count):
-
-        def store(columns, result, extra):
-            store_halves(own, other, columns, result)
+        up_copy(n).start()
+    x_copy.wait()
+    gain_copy.wait()
+    gain_row = gain_here[...]
+    for kk in range(2):
+
+        def prepare(p, carry):
+            raw = x_here[(core + kk) % 2, p]
+            scaled, stats = norm_stats(raw, gain_row)
+            rows = pl.ds(pl.multiple_of((kk * 4 + p) * 32, 32), 32)
+            xs[rows, :] = jnp.where(first, scaled, raw)
+            put_stats(outs[kk], pl.multiple_of(p * 32, 32), columns, stats, row_at)
+            return carry
+
+        lax.fori_loop(0, 4, prepare, 0)
+    xs[pl.ds(2 * half, EXTRA), :] = placed(pieces32(gain_row), row_at).astype(bf16)
+    for to in outs[:2]:
+        to[pl.ds(half, EXTRA), pl.ds(columns, LANES)] = jnp.zeros((EXTRA, LANES), to.dtype)
+
+    for n in range(count):
+        own, other = outs[n // 2 * 2 : n // 2 * 2 + 2]
+        columns_at = pl.ds(n % 2 * wide, wide)
+
+        def store(result, extra):
+            store_halves(own, other, columns_at, result)
             rows = placed(pieces32(jnp.sum(extra, axis=0, keepdims=True)), row_at)
-            own[pl.ds(half, EXTRA), columns] = rows
-            other[pl.ds(half, EXTRA), columns] = rows.astype(bf16)
-
-        up_copy(n).wait()
+            own[pl.ds(half, EXTRA), columns_at] = rows
+            other[pl.ds(half, EXTRA), columns_at] = rows.astype(bf16)
 
         @pl.when(first)
         def _():
+            up_copy(n).wait()
             result = mul(xs[...], up_tiles[n], NN)
-            store(pl.ds(n * wide, wide), result[: 2 * half], result[2 * half :])
+            store(result[: 2 * half], result[2 * half :])
 
         @pl.when(jnp.logical_not(first))
         def _():
             down_copy(n).wait()
-
-            def piece(i, carry):
-                columns = pl.ds(pl.multiple_of(i * 256, 256), 256)
-                store(
-                    pl.ds(pl.multiple_of(n * wide + i * 256, 256), 256),
-                    mul(xs[pl.ds(0, 2 * half), :], down_tiles[n, columns], NT),
-                    mul(xs[pl.ds(2 * half, EXTRA), :], up_tiles[n, :, columns], NN),
-                )
-                return carry
-
-            lax.fori_loop(0, wide // 256, piece, 0)
+            result = mul(xs[pl.ds(0, 2 * half), :], down_tiles[n], NT)
+            up_copy(n).wait()
+            store(result, mul(xs[pl.ds(2 * half, EXTRA), :], up_tiles[n], NN))
 
 
 def start_in(at, x, gain, up, down):
     width, hidden = up.shape
-    wide, count = hidden // 4, 2
+    wide, count = hidden // 4, 4
     rows = 128 + EXTRA
-    halves = []
-    for part in range(2):
-        outs = pl.pallas_call(
-            functools.partial(start_kernel, part),
-            out_shape=half_shapes(rows, count * wide + (0 if part else LANES))
-            + [jax.ShapeDtypeStruct((256 + EXTRA if part == 0 else 16, width), bf16)],
-            in_specs=[SMEM, VMEM if part else HBM, VMEM, HBM, HBM],
-            out_specs=[VMEM] * 3,
-            scratch_shapes=[
-                pltpu.VMEM(x.shape if part == 0 else (16, 128), bf16),
-                pltpu.VMEM((count, width, wide), bf16),
-                pltpu.VMEM((count, wide, width), bf16),
-                pltpu.SemaphoreType.DMA((3, count)),
-            ],
-            compiler_params=pltpu.CompilerParams(vmem_limit_bytes=16 * 1024 * 1024),
-            cost_estimate=pl.CostEstimate(
-                flops=256 * width * hidden, bytes_accessed=width * hidden, transcendentals=0
-            ),
-            name=f"start_in_{part}",
-        )(
-            at,
-            x if part else pltpu.with_memory_space_constraint(x, pltpu.HBM),
-            gain,
-            pltpu.with_memory_space_constraint(up, pltpu.HBM),
-            pltpu.with_memory_space_constraint(down, pltpu.HBM),
-        )
-        x = outs[2]
-        halves.append(outs[:2])
-    return halves
-
-
-def up_kernel(part, at, x, gain, up, *refs):
-    outs, (xs_out, up_tiles, sems) = refs[:2], refs[2:]
+    outs = pl.pallas_call(
+        start_kernel,
+        out_shape=half_shapes(rows, hidden // 2 + LANES) + half_shapes(rows, hidden // 2),
+        in_specs=[SMEM] + [HBM] * 4,
+        out_specs=[VMEM] * 4,
+        scratch_shapes=[
+            pltpu.VMEM((256 + EXTRA, width), bf16),
+            pltpu.VMEM(x.shape, bf16),
+            pltpu.VMEM(gain.shape, f32),
+            pltpu.VMEM((count, width, wide), bf16),
+            pltpu.VMEM((count, wide, width), bf16),
+            pltpu.SemaphoreType.DMA((3, count)),
+        ],
+        compiler_params=pltpu.CompilerParams(vmem_limit_bytes=24 * 1024 * 1024),
+        cost_estimate=pl.CostEstimate(
+            flops=2 * 256 * width * hidden, bytes_accessed=2 * width * hidden, transcendentals=0
+        ),
+        name="start_in",
+    )(at, *(pltpu.with_memory_space_constraint(v, pltpu.HBM) for v in (x, gain, up, down)))
+    return outs[:2], outs[2:]
+
+
+def up_kernel(at, x, gain, up, *refs):
+    outs, (xs, up_tiles, sems) = refs[:4], refs[4:]
     count, _, wide = up_tiles.shape
+    columns = outs[2].shape[1]
 
     def up_copy(n):
-        tile = pl.ds((part * count + n) * wide, wide)
-        return pltpu.make_async_copy(up.at[:, tile], up_tiles.at[n], sems.at[n])
+        return pltpu.make_async_copy(up.at[:, pl.ds(n * wide, wide)], up_tiles.at[n], sems.at[n])
 
     for n in range(count):
         up_copy(n).start()
-    if part == 0:
-        gain_row = gain[...]
-        for kk in range(2):
-
-            def prepare(p, carry):
-                scaled, stats = norm_stats(x[kk * 4 + p], gain_row)
-                xs_out[pl.ds(pl.multiple_of((kk * 4 + p) * 32, 32), 32), :] = scaled
-                put_stats(outs[kk], pl.multiple_of(p * 32, 32), count * wide, stats, at[2])
-                return carry
-
-            lax.fori_loop(0, 4, prepare, 0)
-    xs = x if part else xs_out
+    gain_row = gain[...]
+    for kk in range(2):
+
+        def prepare(p, carry):
+            scaled, stats = norm_stats(x[(at[1] + kk) % 2 * 4 + p], gain_row)
+            xs[pl.ds(pl.multiple_of((kk * 4 + p) * 32, 32), 32), :] = scaled
+            put_stats(outs[kk], pl.multiple_of(p * 32, 32), columns, stats, at[2])
+            return carry
+
+        lax.fori_loop(0, 4, prepare, 0)
     for n in range(count):
         up_copy(n).wait()
-        store_halves(*outs, pl.ds(n * wide, wide), mul(xs[...], up_tiles[n], NN))
+        result = mul(xs[...], up_tiles[n], NN)
+        store_halves(*outs[n // 2 * 2 : n // 2 * 2 + 2], pl.ds(n % 2 * wide, wide), result)
 
 
 def up_in(at, x, gain, up):
     width, hidden = up.shape
-    wide, count = hidden // 4, 2
-    halves = []
-    for part in range(2):
-        outs = pl.pallas_call(
-            functools.partial(up_kernel, part),
-            out_shape=half_shapes(128, count * wide + (0 if part else LANES))
-            + [jax.ShapeDtypeStruct((256 if part == 0 else 16, width), bf16)],
-            in_specs=[SMEM, VMEM, VMEM, HBM],
-            out_specs=[VMEM] * 3,
-            scratch_shapes=[
-                pltpu.VMEM((count, width, wide), bf16),
-                pltpu.SemaphoreType.DMA((count,)),
-            ],
-            compiler_params=pltpu.CompilerParams(vmem_limit_bytes=10 * 1024 * 1024),
-            cost_estimate=pl.CostEstimate(
-                flops=256 * width * hidden, bytes_accessed=width * hidden, transcendentals=0
-            ),
-            name=f"up_in_{part}",
-        )(at, x, gain, pltpu.with_memory_space_constraint(up, pltpu.HBM))
-        x = outs[2]
-        halves.append(outs[:2])
-    return halves
-
-
-def down_back_kernel(part, x, down, own, other):
+    wide, count = hidden // 4, 4
+    outs = pl.pallas_call(
+        up_kernel,
+        out_shape=half_shapes(128, hidden // 2 + LANES) + half_shapes(128, hidden // 2),
+        in_specs=[SMEM, VMEM, VMEM, HBM],
+        out_specs=[VMEM] * 4,
+        scratch_shapes=[
+            pltpu.VMEM((256, width), bf16),
+            pltpu.VMEM((count, width, wide), bf16),
+            pltpu.SemaphoreType.DMA((count,)),
+        ],
+        compiler_params=pltpu.CompilerParams(vmem_limit_bytes=14 * 1024 * 1024),
+        cost_estimate=pl.CostEstimate(
+            flops=2 * 256 * width * hidden, bytes_accessed=2 * width * hidden, transcendentals=0
+        ),
+        name="up_in",
+    )(at, x, gain, pltpu.with_memory_space_constraint(up, pltpu.HBM))
+    return outs[:2], outs[2:]
+
+
+def down_back_kernel(part, at, x, down, own, other):
     wide = own.shape[1] // 2
+    rows = jnp.concatenate([x[at[1]], x[1 - at[1]]], axis=0)
     for n in range(2):
-        result = mul(x[...], down[pl.ds((2 * part + n) * wide, wide), :], NT)
+        result = mul(rows, down[pl.ds((2 * part + n) * wide, wide), :], NT)
         store_halves(own, other, pl.ds(n * wide, wide), result)
 
 
@@ -267,20 +242,20 @@
     ]
 
 
-def down_back_in(x, down):
+def down_back_in(at, x, down):
     hidden, width = down.shape
-    halves = []
-    for part in range(2):
-        outs = local_call(
+    return [
+        local_call(
             functools.partial(down_back_kernel, part),
             half_shapes(128, hidden // 2),
-            (x.reshape(256, width), down),
+            (at, x.reshape(2, 128, width), down),
             f"down_back_{part}",
             256 * width * hidden,
             width * hidden,
+            smem=True,
         )
-        halves.append(outs)
-    return halves
+        for part in range(2)
+    ]
 
 
 def row_out_kernel(mode, at, *refs):
@@ -288,7 +263,6 @@
     first = at[0] == 1
     half, columns = 128, xs.shape[1] // 2
     width = out.shape[-1]
-    slot = 0
     for i in range(2):
         for j in range(2):
             ref = inputs[2 * i + j]
@@ -308,7 +282,7 @@
                 yield (
                     i * 4 + p,
                     gain,
-                    x.at[(at[1] + i) % 2, p] if mode == 2 else x.at[i * 4 + p],
+                    x.at[(at[1] + i) % 2, p] if mode == 2 else x.at[(at[1] + i) % 2 * 4 + p],
                     (first0 + first1)[pick],
                     (second0 + second1)[pick],
                     mean[pick],
@@ -324,11 +298,11 @@
             result = mul(xs[...], tile, dims)
             if not back:
                 for k in range(8):
-                    out[slot + k, :, at_n] = result[k * 32 : k * 32 + 32].astype(bf16)
+                    out[(k + 4 * at[1]) % 8, :, at_n] = result[k * 32 : k * 32 + 32].astype(bf16)
             for k, gain, x, first_sum, second_sum, mean, inv_std in saved:
                 grad = result[k * 32 : k * 32 + 32] * gain[:, at_n]
                 normed = (x[:, at_n].astype(f32) - mean) * inv_std
-                out[slot + k, :, at_n] = (inv_std * (grad - first_sum - normed * second_sum)).astype(bf16)
+                out[(k + 4 * at[1]) % 8, :, at_n] = (inv_std * (grad - first_sum - normed * second_sum)).astype(bf16)
             return carry
 
         lax.fori_loop(0, width // 512, step, 0)
@@ -357,7 +331,8 @@
     return out
 
 
-MEAN, INV, SHIFT = 0, 1, 8
+MEAN, INV = 0, 1
+COMBOS = ((0, 0), (0, 1), (1, 0), (0, 2), (1, 1), (2, 0))
 
 
 def act_kernel(mode, part, at, *refs):
@@ -365,24 +340,35 @@
     first = at[0] == 1
     sums = [(refs.pop(0), refs.pop(0)) for _ in range(2)]
     stats = refs.pop(0) if mode == 2 or part else None
-    gains = refs.pop(0) if mode else None
+    factors = refs.pop(0) if mode != 2 and part else None
+    gains = refs.pop(0) if mode == 1 else None
+    totals = refs.pop(0) if mode else None
     saved = refs.pop(0) if mode else None
     hidden = refs.pop(0) if mode == 2 else None
     chunk = refs.pop(0)
     saved_out = refs.pop(0) if mode == 0 else None
+    gains_out = refs.pop(0) if mode == 0 else None
+    totals_out = refs.pop(0) if mode == 0 else None
     hidden_out = refs.pop(0) if mode == 1 else None
-    gains_out = refs.pop(0) if mode == 0 else None
     stats_out = refs.pop(0) if mode != 2 and part == 0 else None
+    factors_out = refs.pop(0) if mode != 2 and part == 0 else None
+    shifted = refs.pop(0) if mode != 2 else None
     wide = 1024
     total_width = 8192
     lane = lax.broadcasted_iota(jnp.int32, (1, LANES), 1)
     if mode == 0:
         gains = gains_out
+        gains[...] = jnp.zeros_like(gains)
         for q, (held, arrived) in enumerate(sums):
             columns = pl.ds(q * wide, wide)
             extra = held[pl.ds(128, EXTRA), pl.ds(0, wide)] + arrived[pl.ds(128, EXTRA), pl.ds(0, wide)].astype(f32)
-            for r in range(8):
-                gains[pl.ds(r, 1), columns] = jnp.sum(extra[3 * r : 3 * r + 3], axis=0, keepdims=True)
+            rows8 = jnp.concatenate(
+                [jnp.sum(extra[3 * r : 3 * r + 3], axis=0, keepdims=True) for r in range(8)], axis=0
+            )
+            totals_out[:, columns] = jnp.sum(rows8, axis=0, keepdims=True)
+            split = pieces32(rows8)
+            stacked = jnp.concatenate([split[j] for _, j in COMBOS], axis=0)
+            gains[pl.ds(0, 48), columns] = stacked.astype(bf16)
     if stats_out is not None:
         stats = stats_out
         held, arrived = sums[1]
@@ -397,9 +383,18 @@
             inv_std = jnp.where(first, inv_std, 1.0)
             shifts = [jnp.where(first, value, 0.0) for value in shifts]
         out = jnp.where(lane == MEAN, mean, 0.0) + jnp.where(lane == INV, inv_std, 0.0)
+        stats[...] = out
+        placed_at = jnp.zeros((128, LANES), f32)
         for r, value in enumerate(shifts):
-            out = out + jnp.where(lane == SHIFT + r, value, 0.0)
-        stats[...] = out
+            split = pieces32(value)
+            for k, (j, _) in enumerate(COMBOS):
+                placed_at = placed_at + jnp.where(lane == 8 * k + r, split[j], 0.0)
+        factors_out[...] = placed_at.astype(bf16)
+        factors = factors_out
+    if mode != 2:
+        for q in range(4):
+            columns = pl.ds(q * 512, 512)
+            shifted[:, columns] = mul(factors[...], gains[:, columns], NN)
 
     size, span = 16, 512
 
@@ -407,7 +402,6 @@
         rows = pl.ds(pl.multiple_of(i * size, size), size)
         here = stats[rows, :]
         mean, inv_std = here[:, MEAN : MEAN + 1], here[:, INV : INV + 1]
-        shifts = [here[:, SHIFT + r : SHIFT + r + 1] for r in range(8)]
         firsts = jnp.zeros((size, span), f32)
         seconds = jnp.zeros((size, span), f32)
         for n in range(2 * wide // span):
@@ -416,9 +410,7 @@
             inner = pl.ds(n * span % wide, span)
             value = held[rows, inner] + arrived[rows, inner].astype(f32)
             if mode != 2:
-                for r in range(8):
-                    value = value + shifts[r] * gains[pl.ds(r, 1), columns]
-                value = inv_std * value
+                value = inv_std * (value + shifted[rows, columns])
             pre = saved[rows, columns] if mode == 2 else value
             if mode == 0:
                 saved_out[rows, columns] = pre
@@ -436,8 +428,7 @@
             else:
                 chunk[rows, columns] = jnp.where(first, grad_sent, hidden[rows, columns])
             grad = grad_sent.astype(f32)
-            gain_sum = jnp.sum(gains[:, columns], axis=0, keepdims=True)
-            firsts = firsts + grad * gain_sum
+            firsts = firsts + grad * totals[:, columns]
             seconds = seconds + grad * pre
         if mode:
             values = [
@@ -459,20 +450,25 @@
     wide = 2048
     operands = [at] + [ref for pair in sums for ref in pair]
     if mode == 2 or part:
-        operands.append(stats)
+        operands.append(stats[0])
+    if mode != 2 and part:
+        operands.append(stats[1])
+    if mode == 1:
+        operands.append(gains[0])
     if mode:
-        operands += [gains, saved]
+        operands += [gains[1], saved]
     if mode == 2:
         operands.append(hidden)
     shapes = [jax.ShapeDtypeStruct((128, wide + (LANES if mode else 0)), bf16)]
     if mode == 0:
         shapes.append(jax.ShapeDtypeStruct((128, wide), f32))
+        shapes.append(jax.ShapeDtypeStruct((LANES, wide), bf16))
+        shapes.append(jax.ShapeDtypeStruct((1, wide), f32))
     if mode == 1:
         shapes.append(jax.ShapeDtypeStruct((128, wide), bf16))
-    if mode == 0:
-        shapes.append(jax.ShapeDtypeStruct((8, wide), f32))
     if mode != 2 and part == 0:
         shapes.append(jax.ShapeDtypeStruct((128, LANES), f32))
+        shapes.append(jax.ShapeDtypeStruct((128, LANES), bf16))
     return local_call(
         functools.partial(act_kernel, mode, part),
         shapes,
@@ -481,6 +477,7 @@
         40 * 128 * wide,
         16 * 128 * wide,
         smem=True,
+        scratch=[pltpu.VMEM((128, wide), f32)] if mode != 2 else (),
     )
 
 
@@ -528,10 +525,6 @@
     core = row_at % 2
     at = jnp.stack([is_first.astype(jnp.int32), core, row_at])
 
-    def to_global(array):
-        blocks = array.reshape(micro, rows, width)
-        return jnp.where(core == 0, blocks, blocks[::-1])
-
     def pair(i):
         return i ^ 1
 
@@ -563,27 +556,27 @@
 
     blocks = rows // block
     feeds = section_feeds[0].reshape(micro, blocks, block, width)
-    own_feed = lax.dynamic_slice(
-        feeds, ((core + tp_at // blocks) % 2, tp_at % blocks, 0, 0), (1, 1, block, width)
-    )[0, 0]
+    own_feed = lax.dynamic_index_in_dim(
+        feeds.reshape(tsize, block, width), tp_at, 0, keepdims=False
+    )
     early, late = row_sum(start_in(at, feeds, gain, up, down))
-    chunk, saved, gains, stats0 = act(0, 0, at, early, None, None, None, None)
-    chunks, saved0, gain_rows = [chunk], [saved], [gains]
-    chunk, saved, gains = act(0, 1, at, late, stats0, None, None, None)
-    chunks, saved0, gain_rows = chunks + [chunk], saved0 + [saved], gain_rows + [gains]
+    chunk0, saved00, *gains0, stats, factors = act(0, 0, at, early, None, None, None, None)
+    stats0 = (stats, factors)
+    chunk1, saved01, *gains1 = act(0, 1, at, late, stats0, None, None, None)
+    chunks, saved0, gain_rows = [chunk0, chunk1], [saved00, saved01], [gains0, gains1]
     parts = along_tp(row_out(0, at, *swapped(chunks), (down,)))
     middle = lax.ppermute(finish(parts, own_feed, False), "section", [(0, 1)])
     middles = along_tp(jnp.broadcast_to(middle[None], (tsize,) + middle.shape))
 
     early, late = row_sum(up_in(at, middles, gain, up))
-    chunk0, hidden0, stats1 = act(1, 0, at, early, None, gain_rows[0], saved0[0], None)
+    chunk0, hidden0, *stats1 = act(1, 0, at, early, None, gain_rows[0], saved0[0], None)
     chunk1, hidden1 = act(1, 1, at, late, stats1, gain_rows[1], saved0[1], None)
     chunks = [chunk0, chunk1]
     parts = along_tp(row_out(1, at, *swapped(chunks), (gain, middles, up)))
     back = lax.ppermute(finish(parts, own_feed, False), "section", [(1, 0)])
     backs = along_tp(jnp.broadcast_to(back[None], (tsize,) + back.shape))
 
-    early, late = row_sum(down_back_in(backs, down))
+    early, late = row_sum(down_back_in(at, backs, down))
     chunks = []
     for part, sums in enumerate((early, late)):
         kept = (hidden0, hidden1)[part]
@@ -591,7 +584,7 @@
         chunks.append(chunk)
     parts = along_tp(row_out(2, at, *swapped(chunks), (gain, feeds, up, down)))
     base = jnp.where(is_first, back, middle)
-    return to_global(along_tp(finish(parts, base, True)))[None]
+    return along_tp(finish(parts, base, True)).reshape(section_feeds.shape)
 
 
 def solution(mesh):

time: 237 us -> 232 us (0.979)
  blocking collectives: 35.2 us -> 47.5 us
  starting transfers between devices: 56.6 us -> 50 us
  Pallas kernels: 50.6 us -> 44.5 us
  waiting for transfers between devices: 89.6 us -> 84 us
    all_to_all x3 -> x4, blocking collectives: 35.2 us -> 47.5 us  [along_tp(): return lax.all_to_all(part, 'tp', 0, 0)]
    all_to_all x3 -> x2, waiting for transfers between devices: 28.8 us -> 19.7 us  [along_tp(): return lax.all_to_all(part, 'tp', 0, 0)]
    pallas_call x4 -> x2, Pallas kernels: 16.5 us -> 11.6 us  [the longest x1 6.57 us: start_in(): pl.pallas_call(start_kernel, out_shape=half_shapes(rows, hidden // 2 + LA...]
    all_to_all x3 -> x2, starting transfers between devices: 12.3 us -> 8.8 us  [along_tp(): return lax.all_to_all(part, 'tp', 0, 0)]
    ppermute x36, waiting for transfers between devices: 52.4 us -> 55.9 us  [permuted(): lax.ppermute(array, axis, [(i, mapping(i)) for i in range(lax.axis_size(a...]
  transfers between devices with their start and end apart: 41 -> 40, of which waited for: 23 -> 25; matrix products, arithmetic and copies ran while one was open for 1% -> 1% of each run, Pallas kernels for 12% -> 8%
where the time goes in v1:
time: 232 us
  waiting for transfers between devices  84 us (36%)
  starting transfers between devices  50 us (22%)
  blocking collectives  47.5 us (20%)
  Pallas kernels  44.5 us (19%)
  other arithmetic  2.65 us (1%)
  local copies, waits for them, and re-layouts  2.58 us (1%)
    ppermute x36, waiting for transfers between devices, permuted(): lax.ppermute(array, axis, [(i, mapping(i)) for i in range(lax.axis_size(a...  55.9 us
    all_to_all x4, blocking collectives, along_tp(): return lax.all_to_all(part, 'tp', 0, 0)  47.5 us
    pallas_call x14, Pallas kernels, local_call(): pl.pallas_call(kernel, out_shape=shapes, in_specs=specs, out_specs=[VMEM]...  32.9 us
    ppermute x36, starting transfers between devices, permuted(): lax.ppermute(array, axis, [(i, mapping(i)) for i in range(lax.axis_size(a...  32.4 us
    all_to_all x2, waiting for transfers between devices, along_tp(): return lax.all_to_all(part, 'tp', 0, 0)  19.7 us
    all_to_all x2, starting transfers between devices, along_tp(): return lax.all_to_all(part, 'tp', 0, 0)  8.8 us
    ppermute x1, starting transfers between devices, body(): middle = lax.ppermute(finish(parts, own_feed, False), 'section', [(0, 1)])  7.51 us
    pallas_call x1, Pallas kernels, start_in(): pl.pallas_call(start_kernel, out_shape=half_shapes(rows, hidden // 2 + LA...  6.57 us
  transfers between devices with their start and end apart: 40, of which 25 were waited for; matrix products, arithmetic and copies ran while one was open for 1% of the time, Pallas kernels for 8%

profile of v1, /device:TPU:0, one launch (start us, length us, event | category | flops | bytes accessed | tf_op | source)
XLA Modules:
  0.0 231.6 jit_solution(6756489176287554282)
XLA Ops:
  0.1 6.6 %start_in.1 = (f32[160,2176]{1,0:T(8,128)S(1)}, bf16[160,2176]{1,0:T(8,128)(2,1)S(1)}, f32[160,2048]{1,0:T(8,128)S(1)}, bf16[160,2048]{1,0:T(8,128)(2,1)S(1)}) custom-call(s32[3]{0:T(128)S(1)} %pad_add_fusion.at, bf16[2,4,32,1024]{3,2,1,0:T(8,128)(2,1)} %bitcast.28, f32[1,1024]{1,0:T(1,128)} %refs_4_.3, bf16[1024,4096]{1,0:T(8,128)(2,1)} %bitcast.20, ...), custom_call_target="tpu_custom_call" | custom-call | flops 2147483648 | bytes 8388608 | tf_op jit(solution)/shard_map/start_in/pallas_call | solution.py:146
  11.1 2.6 %collective-permute-start.3 = (bf16[160,1152]{1,0:T(8,128)(2,1)S(1)}, bf16[160,1152]{1,0:T(8,128)(2,1)S(1)}, u32[]{:S(2)}, u32[]{:S(2)}) collective-permute-start(bf16[160,1152]{1,0:T(8,128)(2,1)S(1)} %fusion), channel_id=1, source_target_pairs={{0,48},{8,56},{16,32},{24,40},{32,16},{40,24},{48,0},{56,8},{1,49}... | collective-permute-start | bytes 1105928 | tf_op jit(solution)/shard_map/ppermute | solution.py:510
  15.2 4.4 %collective-permute-done.1 = bf16[160,1024]{1,0:T(8,128)(2,1)S(1)} collective-permute-done((bf16[160,1024]{1,0:T(8,128)(2,1)S(1)}, bf16[160,1024]{1,0:T(8,128)(2,1)S(1)}, u32[]{:S(2)}, u32[]{:S(2)}) %collective-permute-start.1) | collective-permute-done | bytes 327712 | tf_op jit(solution)/shard_map/ppermute | solution.py:510
  19.7 4.2 %collective-permute-start.2 = (bf16[160,1024]{1,0:T(8,128)(2,1)S(1)}, bf16[160,1024]{1,0:T(8,128)(2,1)S(1)}, u32[]{:S(2)}, u32[]{:S(2)}) collective-permute-start(bf16[160,1024]{1,0:T(8,128)(2,1)S(1)} %get-tuple-element.83), channel_id=1, source_target_pairs={{0,48},{8,56},{16,32},{24,40},{32,16},{40,24},{48,0},{56,8},{1,49}... | collective-permute-start | bytes 983048 | tf_op jit(solution)/shard_map/ppermute | solution.py:510
  24.4 6.5 %collective-permute-done.8 = bf16[160,1024]{1,0:T(8,128)(2,1)S(1)} collective-permute-done((bf16[160,1024]{1,0:T(8,128)(2,1)S(1)}, bf16[160,1024]{1,0:T(8,128)(2,1)S(1)}, u32[]{:S(2)}, u32[]{:S(2)}) %collective-permute-start.8) | collective-permute-done | bytes 327712 | tf_op jit(solution)/shard_map/ppermute | solution.py:510
  31.3 2.6 %collective-permute-start.7 = (bf16[160,1024]{1,0:T(8,128)(2,1)S(1)}, bf16[160,1024]{1,0:T(8,128)(2,1)S(1)}, u32[]{:S(2)}, u32[]{:S(2)}) collective-permute-start(bf16[160,1024]{1,0:T(8,128)(2,1)S(1)} %get-tuple-element.85), channel_id=1, source_target_pairs={{0,48},{8,56},{16,32},{24,40},{32,16},{40,24},{48,0},{56,8},{1,49}... | collective-permute-start | bytes 983048 | tf_op jit(solution)/shard_map/ppermute | solution.py:510
  33.9 4.0 %collective-permute-done.2.refs_1_ = bf16[160,1024]{1,0:T(8,128)(2,1)S(1)} collective-permute-done((bf16[160,1024]{1,0:T(8,128)(2,1)S(1)}, bf16[160,1024]{1,0:T(8,128)(2,1)S(1)}, u32[]{:S(2)}, u32[]{:S(2)}) %collective-permute-start.2) | collective-permute-done | bytes 327712 | tf_op jit(solution)/shard_map/ppermute | solution.py:510
  37.9 2.9 %act_0_0.1 = (bf16[128,2048]{1,0:T(8,128)(2,1)S(1)}, f32[128,2048]{1,0:T(8,128)S(1)}, bf16[128,2048]{1,0:T(8,128)(2,1)S(1)}, f32[1,2048]{1,0:T(1,128)S(1)}, f32[...) custom-call(s32[3]{0:T(128)S(1)} %pad_add_fusion.at, f32[160,1024]{1,0:T(8,128)S(1)} %get-tuple-element.84.refs_0_, ...), custom_call_target="tpu_custom_call" | custom-call | flops 10485760 | bytes 4194304 | tf_op jit(solution)/shard_map/act_0_0/pallas_call | solution.py:226
  48.5 4.0 %row_out_0.1 = bf16[8,32,1024]{2,1,0:T(8,128)(2,1)} custom-call(s32[3]{0:T(128)S(1)} %pad_add_fusion.at, bf16[128,2048]{1,0:T(8,128)(2,1)S(1)} %get-tuple-element.35.refs_0_, bf16[128,2048]{1,0:T(8,128)(2,1)S(1)} %get-tuple-element.40.refs_1_, bf16[128,2048]{1,0:T(8,128)(2,1)S(1)} %collective-permute-done.10.refs_2_, ...), custom_call_target="tpu_custom_call" | custom-call | flops 2147483648 | bytes 8388608 | tf_op jit(solution)/shard_map/row_out_0/pallas_call | solution.py:226
  52.6 5.3 %all-to-all-start = ((bf16[8,32,1024]{2,1,0:T(8,128)(2,1)}), bf16[8,32,1024]{2,1,0:T(8,128)(2,1)S(1)}, u32[]{:S(2)}, u32[]{:S(2)}) async-start(bf16[8,32,1024]{2,1,0:T(8,128)(2,1)} %row_out_0.1), calls=%async_computation | async-start | bytes 1048576 | tf_op jit(solution)/shard_map/all_to_all | solution.py:555
  57.9 9.7 %all-to-all-done.parts = bf16[8,32,1024]{2,1,0:T(8,128)(2,1)S(1)} async-done(((bf16[8,32,1024]{2,1,0:T(8,128)(2,1)}), bf16[8,32,1024]{2,1,0:T(8,128)(2,1)S(1)}, u32[]{:S(2)}, u32[]{:S(2)}) %all-to-all-start) | async-done | bytes 524320 | tf_op jit(solution)/shard_map/all_to_all | solution.py:555
  67.7 7.5 %collective-permute-start.12 = (bf16[32,1024]{1,0:T(8,128)(2,1)S(1)}, bf16[32,1024]{1,0:T(8,128)(2,1)S(1)}, u32[]{:S(2)}, u32[]{:S(2)}) collective-permute-start(bf16[32,1024]{1,0:T(8,128)(2,1)S(1)} %finish.3), channel_id=1, source_target_pairs={{0,64},{1,65},{2,66},{3,67},{4,68},{5,69},{6,70},{7,71},{8,72},{9,... | collective-permute-start | bytes 196616 | tf_op jit(solution)/shard_map/ppermute | solution.py:568
  77.2 11.2 %all_to_all.30.x.refs_5_ = bf16[8,32,1024]{2,1,0:T(8,128)(2,1)S(1)} all-to-all(bf16[8,32,1024]{2,1,0:T(8,128)(2,1)S(1)} %broadcast_in_dim.4), channel_id=1, replica_groups=mesh['section'=2,'row'=8,'tp'=8] {'tp'}, dimensions={0} | all-to-all | bytes 1048576 | tf_op jit(solution)/shard_map/all_to_all | solution.py:555
  88.4 5.0 %up_in.1 = (f32[128,2176]{1,0:T(8,128)S(1)}, bf16[128,2176]{1,0:T(8,128)(2,1)S(1)}, f32[128,2048]{1,0:T(8,128)S(1)}, bf16[128,2048]{1,0:T(8,128)(2,1)S(1)}) custom-call(s32[3]{0:T(128)S(1)} %pad_add_fusion.at, bf16[8,32,1024]{2,1,0:T(8,128)(2,1)S(1)} %all_to_all.30.x.refs_5_, f32[1,1024]{1,0:T(1,128)S(1)} %copy-done.5, bf16[1024,4096]{1,0:T(8,128)(2,1)} %bitcast.21), custom_call_target="tpu_custom_call" | custom-call | flops 2147483648 | bytes 8388608 | tf_op jit(solution)/shard_map/up_in/pallas_call | solution.py:197
  100.1 4.7 %collective-permute-done.14 = bf16[128,1024]{1,0:T(8,128)(2,1)S(1)} collective-permute-done((bf16[128,1024]{1,0:T(8,128)(2,1)S(1)}, bf16[128,1024]{1,0:T(8,128)(2,1)S(1)}, u32[]{:S(2)}, u32[]{:S(2)}) %collective-permute-start.14) | collective-permute-done | bytes 262176 | tf_op jit(solution)/shard_map/ppermute | solution.py:510
  104.9 2.6 %collective-permute-start.15 = (bf16[128,1024]{1,0:T(8,128)(2,1)S(1)}, bf16[128,1024]{1,0:T(8,128)(2,1)S(1)}, u32[]{:S(2)}, u32[]{:S(2)}) collective-permute-start(bf16[128,1024]{1,0:T(8,128)(2,1)S(1)} %get-tuple-element.75), channel_id=1, source_target_pairs={{0,48},{8,56},{16,32},{24,40},{32,16},{40,24},{48,0},{56,8},{1,49}... | collective-permute-start | bytes 786440 | tf_op jit(solution)/shard_map/ppermute | solution.py:510
  107.9 5.2 %collective-permute-done.21 = bf16[128,1024]{1,0:T(8,128)(2,1)S(1)} collective-permute-done((bf16[128,1024]{1,0:T(8,128)(2,1)S(1)}, bf16[128,1024]{1,0:T(8,128)(2,1)S(1)}, u32[]{:S(2)}, u32[]{:S(2)}) %collective-permute-start.21) | collective-permute-done | bytes 262176 | tf_op jit(solution)/shard_map/ppermute | solution.py:510
  115.8 2.9 %collective-permute-done.15.refs_1_ = bf16[128,1024]{1,0:T(8,128)(2,1)S(1)} collective-permute-done((bf16[128,1024]{1,0:T(8,128)(2,1)S(1)}, bf16[128,1024]{1,0:T(8,128)(2,1)S(1)}, u32[]{:S(2)}, u32[]{:S(2)}) %collective-permute-start.15) | collective-permute-done | bytes 262176 | tf_op jit(solution)/shard_map/ppermute | solution.py:510
  118.7 4.0 %act_1_0.1 = (bf16[128,2176]{1,0:T(8,128)(2,1)S(1)}, bf16[128,2048]{1,0:T(8,128)(2,1)S(1)}, f32[128,128]{1,0:T(8,128)S(1)}, bf16[128,128]{1,0:T(8,128)(2,1)S(1)}) custom-call(s32[3]{0:T(128)S(1)} %pad_add_fusion.at, f32[128,1024]{1,0:T(8,128)S(1)} %get-tuple-element.76.refs_0_, bf16[128,1024]{1,0:T(8,128)(2,1)S(1)} %collective-permute-done.15.refs_1_, ...), custom_call_target="tpu_custom_call" | custom-call | flops 10485760 | bytes 4194304 | tf_op jit(solution)/shard_map/act_1_0/pallas_call | solution.py:226
  123.2 3.6 %act_1_1.1 = (bf16[128,2176]{1,0:T(8,128)(2,1)S(1)}, bf16[128,2048]{1,0:T(8,128)(2,1)S(1)}) custom-call(s32[3]{0:T(128)S(1)} %pad_add_fusion.at, f32[128,1024]{1,0:T(8,128)S(1)} %get-tuple-element.98.refs_0_, bf16[128,1024]{1,0:T(8,128)(2,1)S(1)} %collective-permute-done.20.refs_1_, f32[128,1024]{1,0:T(8,128)S(1)} %get-tuple-element.70.refs_2_, ...), custom_call_target="tpu_custom_call" | custom-call | flops 10485760 | bytes 4194304 | tf_op jit(solution)/shard_map/act_1_1/pallas_call | solution.py:226
  128.9 3.4 %row_out_1.1 = bf16[8,32,1024]{2,1,0:T(8,128)(2,1)S(1)} custom-call(s32[3]{0:T(128)S(1)} %pad_add_fusion.at, bf16[128,2176]{1,0:T(8,128)(2,1)S(1)} %get-tuple-element.46.refs_0_, bf16[128,2176]{1,0:T(8,128)(2,1)S(1)} %get-tuple-element.54.refs_1_, bf16[128,2176]{1,0:T(8,128)(2,1)S(1)} %collective-permute-done.23.refs_2_, ...), custom_call_target="tpu_custom_call" | custom-call | flops 2147483648 | bytes 8388608 | tf_op jit(solution)/shard_map/row_out_1/pallas_call | solution.py:226
  132.3 12.7 %all_to_all.31.parts = bf16[8,32,1024]{2,1,0:T(8,128)(2,1)S(1)} all-to-all(bf16[8,32,1024]{2,1,0:T(8,128)(2,1)S(1)} %row_out_1.1), channel_id=1, replica_groups=mesh['section'=2,'row'=8,'tp'=8] {'tp'}, dimensions={0} | all-to-all | bytes 1048576 | tf_op jit(solution)/shard_map/all_to_all | solution.py:555
  146.4 6.5 %collective-permute-done.25 = bf16[32,1024]{1,0:T(8,128)(2,1)S(1)} collective-permute-done((bf16[32,1024]{1,0:T(8,128)(2,1)S(1)}, bf16[32,1024]{1,0:T(8,128)(2,1)S(1)}, u32[]{:S(2)}, u32[]{:S(2)}) %collective-permute-start.25) | collective-permute-done | bytes 65568 | tf_op jit(solution)/shard_map/ppermute | solution.py:576
  153.0 11.1 %all_to_all.32 = bf16[8,32,1024]{2,1,0:T(8,128)(2,1)S(1)} all-to-all(bf16[8,32,1024]{2,1,0:T(8,128)(2,1)S(1)} %broadcast_in_dim.5), channel_id=1, replica_groups=mesh['section'=2,'row'=8,'tp'=8] {'tp'}, dimensions={0} | all-to-all | bytes 1048576 | tf_op jit(solution)/shard_map/all_to_all | solution.py:555
  173.8 5.5 %collective-permute-done.29 = bf16[128,1024]{1,0:T(8,128)(2,1)S(1)} collective-permute-done((bf16[128,1024]{1,0:T(8,128)(2,1)S(1)}, bf16[128,1024]{1,0:T(8,128)(2,1)S(1)}, u32[]{:S(2)}, u32[]{:S(2)}) %collective-permute-start.29) | collective-permute-done | bytes 262176 | tf_op jit(solution)/shard_map/ppermute | solution.py:510
  182.0 2.9 %collective-permute-done.34 = bf16[128,1024]{1,0:T(8,128)(2,1)S(1)} collective-permute-done((bf16[128,1024]{1,0:T(8,128)(2,1)S(1)}, bf16[128,1024]{1,0:T(8,128)(2,1)S(1)}, u32[]{:S(2)}, u32[]{:S(2)}) %collective-permute-start.34) | collective-permute-done | bytes 262176 | tf_op jit(solution)/shard_map/ppermute | solution.py:510
  187.6 3.7 %collective-permute-done.28.refs_1_ = bf16[128,1024]{1,0:T(8,128)(2,1)S(1)} collective-permute-done((bf16[128,1024]{1,0:T(8,128)(2,1)S(1)}, bf16[128,1024]{1,0:T(8,128)(2,1)S(1)}, u32[]{:S(2)}, u32[]{:S(2)}) %collective-permute-start.28) | collective-permute-done | bytes 262176 | tf_op jit(solution)/shard_map/ppermute | solution.py:510
  196.0 2.4 %act_2_1.1.refs_1_ = bf16[128,2176]{1,0:T(8,128)(2,1)S(1)} custom-call(s32[3]{0:T(128)S(1)} %pad_add_fusion.at, f32[128,1024]{1,0:T(8,128)S(1)} %get-tuple-element.90.refs_0_, bf16[128,1024]{1,0:T(8,128)(2,1)S(1)} %collective-permute-done.33.refs_1_, f32[128,1024]{1,0:T(8,128)S(1)} %get-tuple-element.62.refs_2_, ...), custom_call_target="tpu_custom_call" | custom-call | flops 10485760 | bytes 4194304 | tf_op jit(solution)/shard_map/act_2_1/pallas_call | solution.py:226
  200.5 4.3 %row_out_2.1 = bf16[8,32,1024]{2,1,0:T(8,128)(2,1)} custom-call(s32[3]{0:T(128)S(1)} %pad_add_fusion.at, bf16[128,2176]{1,0:T(8,128)(2,1)S(1)} %act_2_0.1.refs_0_, bf16[128,2176]{1,0:T(8,128)(2,1)S(1)} %act_2_1.1.refs_1_, bf16[128,2176]{1,0:T(8,128)(2,1)S(1)} %collective-permute-done.36.refs_2_, bf16[128,2176]{1,0:T(8,128)(2,1)S(1)} %collective-permute-done.37.refs_3_, ...), custom_call_target="tpu_custom_call" | custom-call | flops 2147483648 | bytes 8388608 | tf_op jit(solution)/shard_map/row_out_2/pallas_call | solution.py:226
  204.8 3.5 %all-to-all-start.4 = ((bf16[8,32,1024]{2,1,0:T(8,128)(2,1)}), bf16[8,32,1024]{2,1,0:T(8,128)(2,1)S(1)}, u32[]{:S(2)}, u32[]{:S(2)}) async-start(bf16[8,32,1024]{2,1,0:T(8,128)(2,1)} %row_out_2.1), calls=%async_computation.4 | async-start | bytes 1048576 | tf_op jit(solution)/shard_map/all_to_all | solution.py:555
  208.3 10.0 %all-to-all-done.4.parts = bf16[8,32,1024]{2,1,0:T(8,128)(2,1)S(1)} async-done(((bf16[8,32,1024]{2,1,0:T(8,128)(2,1)}), bf16[8,32,1024]{2,1,0:T(8,128)(2,1)S(1)}, u32[]{:S(2)}, u32[]{:S(2)}) %all-to-all-start.4) | async-done | bytes 524320 | tf_op jit(solution)/shard_map/all_to_all | solution.py:555
  218.3 12.5 %all_to_all.33 = bf16[8,32,1024]{2,1,0:T(8,128)(2,1)S(1)} all-to-all(bf16[8,32,1024]{2,1,0:T(8,128)(2,1)S(1)} %finish.5), channel_id=1, replica_groups=mesh['section'=2,'row'=8,'tp'=8] {'tp'}, dimensions={0} | all-to-all | bytes 1048576 | tf_op jit(solution)/shard_map/all_to_all | solution.py:555
  (117 shorter events, 53.0 us)
Async XLA Ops:
  6.7 7.0 %collective-permute-start.5 = (bf16[160,2048]{1,0:T(8,128)(2,1)S(1)}, bf16[160,2048]{1,0:T(8,128)(2,1)S(1)}, u32[]{:S(2)}, u32[]{:S(2)}) collective-permute-start(bf16[160,2048]{1,0:T(8,128)(2,1)S(1)} %get-tuple-element.37), channel_id=1, source_target_pairs={{0,8},{8,0},{16,24},{24,16},{32,40},{40,32},{48,56},{56,48},{1,9},... | collective-permute-start | bytes 1966088 | tf_op jit(solution)/shard_map/ppermute | solution.py:510
  9.0 10.6 %collective-permute-start.1 = (bf16[160,1024]{1,0:T(8,128)(2,1)S(1)}, bf16[160,1024]{1,0:T(8,128)(2,1)S(1)}, u32[]{:S(2)}, u32[]{:S(2)}) collective-permute-start(bf16[160,1024]{1,0:T(8,128)(2,1)S(1)} %fusion.1), channel_id=1, source_target_pairs={{0,16},{8,24},{16,0},{24,8},{32,48},{40,56},{48,32},{56,40},{1,17}... | collective-permute-start | bytes 983048 | tf_op jit(solution)/shard_map/ppermute | solution.py:510
  11.1 12.8 %collective-permute-start.3 = (bf16[160,1152]{1,0:T(8,128)(2,1)S(1)}, bf16[160,1152]{1,0:T(8,128)(2,1)S(1)}, u32[]{:S(2)}, u32[]{:S(2)}) collective-permute-start(bf16[160,1152]{1,0:T(8,128)(2,1)S(1)} %fusion), channel_id=1, source_target_pairs={{0,48},{8,56},{16,32},{24,40},{32,16},{40,24},{48,0},{56,8},{1,49}... | collective-permute-start | bytes 1105928 | tf_op jit(solution)/shard_map/ppermute | solution.py:510
  14.0 16.9 %collective-permute-start.8 = (bf16[160,1024]{1,0:T(8,128)(2,1)S(1)}, bf16[160,1024]{1,0:T(8,128)(2,1)S(1)}, u32[]{:S(2)}, u32[]{:S(2)}) collective-permute-start(bf16[160,1024]{1,0:T(8,128)(2,1)S(1)} %get-tuple-element.87), channel_id=1, source_target_pairs={{0,48},{8,56},{16,32},{24,40},{32,16},{40,24},{48,0},{56,8},{1,49}... | collective-permute-start | bytes 983048 | tf_op jit(solution)/shard_map/ppermute | solution.py:510
  14.8 16.2 %collective-permute-start.6 = (bf16[160,1024]{1,0:T(8,128)(2,1)S(1)}, bf16[160,1024]{1,0:T(8,128)(2,1)S(1)}, u32[]{:S(2)}, u32[]{:S(2)}) collective-permute-start(bf16[160,1024]{1,0:T(8,128)(2,1)S(1)} %get-tuple-element.88), channel_id=1, source_target_pairs={{0,16},{8,24},{16,0},{24,8},{32,48},{40,56},{48,32},{56,40},{1,17}... | collective-permute-start | bytes 983048 | tf_op jit(solution)/shard_map/ppermute | solution.py:510
  19.7 18.2 %collective-permute-start.2 = (bf16[160,1024]{1,0:T(8,128)(2,1)S(1)}, bf16[160,1024]{1,0:T(8,128)(2,1)S(1)}, u32[]{:S(2)}, u32[]{:S(2)}) collective-permute-start(bf16[160,1024]{1,0:T(8,128)(2,1)S(1)} %get-tuple-element.83), channel_id=1, source_target_pairs={{0,48},{8,56},{16,32},{24,40},{32,16},{40,24},{48,0},{56,8},{1,49}... | collective-permute-start | bytes 983048 | tf_op jit(solution)/shard_map/ppermute | solution.py:510
  24.1 13.9 %collective-permute-start.4 = (bf16[160,1152]{1,0:T(8,128)(2,1)S(1)}, bf16[160,1152]{1,0:T(8,128)(2,1)S(1)}, u32[]{:S(2)}, u32[]{:S(2)}) collective-permute-start(bf16[160,1152]{1,0:T(8,128)(2,1)S(1)} %get-tuple-element.81), channel_id=1, source_target_pairs={{0,16},{8,24},{16,0},{24,8},{32,48},{40,56},{48,32},{56,40},{1,17}... | collective-permute-start | bytes 1105928 | tf_op jit(solution)/shard_map/ppermute | solution.py:510
  31.3 12.5 %collective-permute-start.7 = (bf16[160,1024]{1,0:T(8,128)(2,1)S(1)}, bf16[160,1024]{1,0:T(8,128)(2,1)S(1)}, u32[]{:S(2)}, u32[]{:S(2)}) collective-permute-start(bf16[160,1024]{1,0:T(8,128)(2,1)S(1)} %get-tuple-element.85), channel_id=1, source_target_pairs={{0,48},{8,56},{16,32},{24,40},{32,16},{40,24},{48,0},{56,8},{1,49}... | collective-permute-start | bytes 983048 | tf_op jit(solution)/shard_map/ppermute | solution.py:510
  33.9 9.9 %collective-permute-start.9 = (bf16[160,1024]{1,0:T(8,128)(2,1)S(1)}, bf16[160,1024]{1,0:T(8,128)(2,1)S(1)}, u32[]{:S(2)}, u32[]{:S(2)}) collective-permute-start(bf16[160,1024]{1,0:T(8,128)(2,1)S(1)} %get-tuple-element.77), channel_id=1, source_target_pairs={{0,16},{8,24},{16,0},{24,8},{32,48},{40,56},{48,32},{56,40},{1,17}... | collective-permute-start | bytes 983048 | tf_op jit(solution)/shard_map/ppermute | solution.py:510
  41.7 4.9 %collective-permute-start.10 = (bf16[128,2048]{1,0:T(8,128)(2,1)S(1)}, bf16[128,2048]{1,0:T(8,128)(2,1)S(1)}, u32[]{:S(2)}, u32[]{:S(2)}) collective-permute-start(bf16[128,2048]{1,0:T(8,128)(2,1)S(1)} %get-tuple-element.35.refs_0_), channel_id=1, source_target_pairs={{0,8},{8,0},{16,24},{24,16},{32,40},{40,32},{48,56},{56,48},{1,9},... | collective-permute-start | bytes 1572872 | tf_op jit(solution)/shard_map/ppermute | solution.py:510
  52.6 15.1 %all-to-all-start = ((bf16[8,32,1024]{2,1,0:T(8,128)(2,1)}), bf16[8,32,1024]{2,1,0:T(8,128)(2,1)S(1)}, u32[]{:S(2)}, u32[]{:S(2)}) async-start(bf16[8,32,1024]{2,1,0:T(8,128)(2,1)} %row_out_0.1), calls=%async_computation | async-start | bytes 1048576 | tf_op jit(solution)/shard_map/all_to_all | solution.py:555
  67.7 9.4 %collective-permute-start.12 = (bf16[32,1024]{1,0:T(8,128)(2,1)S(1)}, bf16[32,1024]{1,0:T(8,128)(2,1)S(1)}, u32[]{:S(2)}, u32[]{:S(2)}) collective-permute-start(bf16[32,1024]{1,0:T(8,128)(2,1)S(1)} %finish.3), channel_id=1, source_target_pairs={{0,64},{1,65},{2,66},{3,67},{4,68},{5,69},{6,70},{7,71},{8,72},{9,... | collective-permute-start | bytes 196616 | tf_op jit(solution)/shard_map/ppermute | solution.py:568
  93.6 5.2 %collective-permute-start.18 = (bf16[128,2048]{1,0:T(8,128)(2,1)S(1)}, bf16[128,2048]{1,0:T(8,128)(2,1)S(1)}, u32[]{:S(2)}, u32[]{:S(2)}) collective-permute-start(bf16[128,2048]{1,0:T(8,128)(2,1)S(1)} %get-tuple-element.48), channel_id=1, source_target_pairs={{0,8},{8,0},{16,24},{24,16},{32,40},{40,32},{48,56},{56,48},{1,9},... | collective-permute-start | bytes 1572872 | tf_op jit(solution)/shard_map/ppermute | solution.py:510
  95.6 9.2 %collective-permute-start.14 = (bf16[128,1024]{1,0:T(8,128)(2,1)S(1)}, bf16[128,1024]{1,0:T(8,128)(2,1)S(1)}, u32[]{:S(2)}, u32[]{:S(2)}) collective-permute-start(bf16[128,1024]{1,0:T(8,128)(2,1)S(1)} %fusion.5), channel_id=1, source_target_pairs={{0,16},{8,24},{16,0},{24,8},{32,48},{40,56},{48,32},{56,40},{1,17}... | collective-permute-start | bytes 786440 | tf_op jit(solution)/shard_map/ppermute | solution.py:510
  96.3 11.2 %collective-permute-start.16 = (bf16[128,1152]{1,0:T(8,128)(2,1)S(1)}, bf16[128,1152]{1,0:T(8,128)(2,1)S(1)}, u32[]{:S(2)}, u32[]{:S(2)}) collective-permute-start(bf16[128,1152]{1,0:T(8,128)(2,1)S(1)} %fusion.4), channel_id=1, source_target_pairs={{0,48},{8,56},{16,32},{24,40},{32,16},{40,24},{48,0},{56,8},{1,49}... | collective-permute-start | bytes 884744 | tf_op jit(solution)/shard_map/ppermute | solution.py:510
  98.9 14.2 %collective-permute-start.21 = (bf16[128,1024]{1,0:T(8,128)(2,1)S(1)}, bf16[128,1024]{1,0:T(8,128)(2,1)S(1)}, u32[]{:S(2)}, u32[]{:S(2)}) collective-permute-start(bf16[128,1024]{1,0:T(8,128)(2,1)S(1)} %get-tuple-element.99), channel_id=1, source_target_pairs={{0,48},{8,56},{16,32},{24,40},{32,16},{40,24},{48,0},{56,8},{1,49}... | collective-permute-start | bytes 786440 | tf_op jit(solution)/shard_map/ppermute | solution.py:510
  99.8 13.3 %collective-permute-start.19 = (bf16[128,1024]{1,0:T(8,128)(2,1)S(1)}, bf16[128,1024]{1,0:T(8,128)(2,1)S(1)}, u32[]{:S(2)}, u32[]{:S(2)}) collective-permute-start(bf16[128,1024]{1,0:T(8,128)(2,1)S(1)} %get-tuple-element.100), channel_id=1, source_target_pairs={{0,16},{8,24},{16,0},{24,8},{32,48},{40,56},{48,32},{56,40},{1,17}... | collective-permute-start | bytes 786440 | tf_op jit(solution)/shard_map/ppermute | solution.py:510
  104.9 13.8 %collective-permute-start.15 = (bf16[128,1024]{1,0:T(8,128)(2,1)S(1)}, bf16[128,1024]{1,0:T(8,128)(2,1)S(1)}, u32[]{:S(2)}, u32[]{:S(2)}) collective-permute-start(bf16[128,1024]{1,0:T(8,128)(2,1)S(1)} %get-tuple-element.75), channel_id=1, source_target_pairs={{0,48},{8,56},{16,32},{24,40},{32,16},{40,24},{48,0},{56,8},{1,49}... | collective-permute-start | bytes 786440 | tf_op jit(solution)/shard_map/ppermute | solution.py:510
  107.6 11.1 %collective-permute-start.17 = (bf16[128,1152]{1,0:T(8,128)(2,1)S(1)}, bf16[128,1152]{1,0:T(8,128)(2,1)S(1)}, u32[]{:S(2)}, u32[]{:S(2)}) collective-permute-start(bf16[128,1152]{1,0:T(8,128)(2,1)S(1)} %get-tuple-element.73), channel_id=1, source_target_pairs={{0,16},{8,24},{16,0},{24,8},{32,48},{40,56},{48,32},{56,40},{1,17}... | collective-permute-start | bytes 884744 | tf_op jit(solution)/shard_map/ppermute | solution.py:510
  113.4 9.8 %collective-permute-start.20 = (bf16[128,1024]{1,0:T(8,128)(2,1)S(1)}, bf16[128,1024]{1,0:T(8,128)(2,1)S(1)}, u32[]{:S(2)}, u32[]{:S(2)}) collective-permute-start(bf16[128,1024]{1,0:T(8,128)(2,1)S(1)} %get-tuple-element.97), channel_id=1, source_target_pairs={{0,48},{8,56},{16,32},{24,40},{32,16},{40,24},{48,0},{56,8},{1,49}... | collective-permute-start | bytes 786440 | tf_op jit(solution)/shard_map/ppermute | solution.py:510
  115.8 7.4 %collective-permute-start.22 = (bf16[128,1024]{1,0:T(8,128)(2,1)S(1)}, bf16[128,1024]{1,0:T(8,128)(2,1)S(1)}, u32[]{:S(2)}, u32[]{:S(2)}) collective-permute-start(bf16[128,1024]{1,0:T(8,128)(2,1)S(1)} %get-tuple-element.69), channel_id=1, source_target_pairs={{0,16},{8,24},{16,0},{24,8},{32,48},{40,56},{48,32},{56,40},{1,17}... | collective-permute-start | bytes 786440 | tf_op jit(solution)/shard_map/ppermute | solution.py:510
  145.1 7.8 %collective-permute-start.25 = (bf16[32,1024]{1,0:T(8,128)(2,1)S(1)}, bf16[32,1024]{1,0:T(8,128)(2,1)S(1)}, u32[]{:S(2)}, u32[]{:S(2)}) collective-permute-start(bf16[32,1024]{1,0:T(8,128)(2,1)S(1)} %finish.4), channel_id=1, source_target_pairs={{64,0},{65,1},{66,2},{67,3},{68,4},{69,5},{70,6},{71,7},{72,8},{73... | collective-permute-start | bytes 196616 | tf_op jit(solution)/shard_map/ppermute | solution.py:576
  168.8 10.5 %collective-permute-start.29 = (bf16[128,1024]{1,0:T(8,128)(2,1)S(1)}, bf16[128,1024]{1,0:T(8,128)(2,1)S(1)}, u32[]{:S(2)}, u32[]{:S(2)}) collective-permute-start(bf16[128,1024]{1,0:T(8,128)(2,1)S(1)} %get-tuple-element.95), channel_id=1, source_target_pairs={{0,48},{8,56},{16,32},{24,40},{32,16},{40,24},{48,0},{56,8},{1,49}... | collective-permute-start | bytes 786440 | tf_op jit(solution)/shard_map/ppermute | solution.py:510
  171.2 9.2 %collective-permute-start.27 = (bf16[128,1024]{1,0:T(8,128)(2,1)S(1)}, bf16[128,1024]{1,0:T(8,128)(2,1)S(1)}, u32[]{:S(2)}, u32[]{:S(2)}) collective-permute-start(bf16[128,1024]{1,0:T(8,128)(2,1)S(1)} %get-tuple-element.96), channel_id=1, source_target_pairs={{0,16},{8,24},{16,0},{24,8},{32,48},{40,56},{48,32},{56,40},{1,17}... | collective-permute-start | bytes 786440 | tf_op jit(solution)/shard_map/ppermute | solution.py:510
  171.4 13.5 %collective-permute-start.34 = (bf16[128,1024]{1,0:T(8,128)(2,1)S(1)}, bf16[128,1024]{1,0:T(8,128)(2,1)S(1)}, u32[]{:S(2)}, u32[]{:S(2)}) collective-permute-start(bf16[128,1024]{1,0:T(8,128)(2,1)S(1)} %get-tuple-element.91), channel_id=1, source_target_pairs={{0,48},{8,56},{16,32},{24,40},{32,16},{40,24},{48,0},{56,8},{1,49}... | collective-permute-start | bytes 786440 | tf_op jit(solution)/shard_map/ppermute | solution.py:510
  172.8 13.3 %collective-permute-start.32 = (bf16[128,1024]{1,0:T(8,128)(2,1)S(1)}, bf16[128,1024]{1,0:T(8,128)(2,1)S(1)}, u32[]{:S(2)}, u32[]{:S(2)}) collective-permute-start(bf16[128,1024]{1,0:T(8,128)(2,1)S(1)} %get-tuple-element.92), channel_id=1, source_target_pairs={{0,16},{8,24},{16,0},{24,8},{32,48},{40,56},{48,32},{56,40},{1,17}... | collective-permute-start | bytes 786440 | tf_op jit(solution)/shard_map/ppermute | solution.py:510
  180.7 10.5 %collective-permute-start.28 = (bf16[128,1024]{1,0:T(8,128)(2,1)S(1)}, bf16[128,1024]{1,0:T(8,128)(2,1)S(1)}, u32[]{:S(2)}, u32[]{:S(2)}) collective-permute-start(bf16[128,1024]{1,0:T(8,128)(2,1)S(1)} %get-tuple-element.93), channel_id=1, source_target_pairs={{0,48},{8,56},{16,32},{24,40},{32,16},{40,24},{48,0},{56,8},{1,49}... | collective-permute-start | bytes 786440 | tf_op jit(solution)/shard_map/ppermute | solution.py:510
  182.0 9.7 %collective-permute-start.30 = (bf16[128,1024]{1,0:T(8,128)(2,1)S(1)}, bf16[128,1024]{1,0:T(8,128)(2,1)S(1)}, u32[]{:S(2)}, u32[]{:S(2)}) collective-permute-start(bf16[128,1024]{1,0:T(8,128)(2,1)S(1)} %get-tuple-element.65), channel_id=1, source_target_pairs={{0,16},{8,24},{16,0},{24,8},{32,48},{40,56},{48,32},{56,40},{1,17}... | collective-permute-start | bytes 786440 | tf_op jit(solution)/shard_map/ppermute | solution.py:510
  186.3 8.9 %collective-permute-start.33 = (bf16[128,1024]{1,0:T(8,128)(2,1)S(1)}, bf16[128,1024]{1,0:T(8,128)(2,1)S(1)}, u32[]{:S(2)}, u32[]{:S(2)}) collective-permute-start(bf16[128,1024]{1,0:T(8,128)(2,1)S(1)} %get-tuple-element.89), channel_id=1, source_target_pairs={{0,48},{8,56},{16,32},{24,40},{32,16},{40,24},{48,0},{56,8},{1,49}... | collective-permute-start | bytes 786440 | tf_op jit(solution)/shard_map/ppermute | solution.py:510
  187.6 8.4 %collective-permute-start.35 = (bf16[128,1024]{1,0:T(8,128)(2,1)S(1)}, bf16[128,1024]{1,0:T(8,128)(2,1)S(1)}, u32[]{:S(2)}, u32[]{:S(2)}) collective-permute-start(bf16[128,1024]{1,0:T(8,128)(2,1)S(1)} %get-tuple-element.61), channel_id=1, source_target_pairs={{0,16},{8,24},{16,0},{24,8},{32,48},{40,56},{48,32},{56,40},{1,17}... | collective-permute-start | bytes 786440 | tf_op jit(solution)/shard_map/ppermute | solution.py:510
  194.0 4.6 %collective-permute-start.36 = (bf16[128,2176]{1,0:T(8,128)(2,1)S(1)}, bf16[128,2176]{1,0:T(8,128)(2,1)S(1)}, u32[]{:S(2)}, u32[]{:S(2)}) collective-permute-start(bf16[128,2176]{1,0:T(8,128)(2,1)S(1)} %act_2_0.1.refs_0_), channel_id=1, source_target_pairs={{0,8},{8,0},{16,24},{24,16},{32,40},{40,32},{48,56},{56,48},{1,9},... | collective-permute-start | bytes 1671176 | tf_op jit(solution)/shard_map/ppermute | solution.py:510
  204.8 13.5 %all-to-all-start.4 = ((bf16[8,32,1024]{2,1,0:T(8,128)(2,1)}), bf16[8,32,1024]{2,1,0:T(8,128)(2,1)S(1)}, u32[]{:S(2)}, u32[]{:S(2)}) async-start(bf16[8,32,1024]{2,1,0:T(8,128)(2,1)} %row_out_2.1), calls=%async_computation.4 | async-start | bytes 1048576 | tf_op jit(solution)/shard_map/all_to_all | solution.py:555
  (20 other events, 268.4 us)

commit v2 on v1

--- a/solution.py
+++ b/solution.py
@@ -20,12 +20,14 @@
 SMEM = pl.BlockSpec(memory_space=pltpu.SMEM)
 
 
-def gelu_tangent(inputs):
-    return jnp.tanh(gelu_coeff * (inputs + 0.044715 * inputs * inputs * inputs))
-
-
-def gelu_value(inputs):
-    return 0.5 * inputs * (1.0 + gelu_tangent(inputs))
+def gelu_gate(inputs, square):
+    inner = inputs * (gelu_coeff + gelu_coeff * 0.044715 * square)
+    return 0.5 + 0.5 * jnp.tanh(inner)
+
+
+def gelu_slope(inputs, square, gate):
+    rise = inputs * (2.0 * gelu_coeff + 6.0 * gelu_coeff * 0.044715 * square)
+    return gate * (1.0 + (1.0 - gate) * rise)
 
 
 def pieces(value):
@@ -215,10 +217,13 @@
 
 def down_back_kernel(part, at, x, down, own, other):
     wide = own.shape[1] // 2
-    rows = jnp.concatenate([x[at[1]], x[1 - at[1]]], axis=0)
+    half = own.shape[0]
     for n in range(2):
-        result = mul(rows, down[pl.ds((2 * part + n) * wide, wide), :], NT)
-        store_halves(own, other, pl.ds(n * wide, wide), result)
+        result = mul(x[...], down[pl.ds((2 * part + n) * wide, wide), :], NT)
+        low, high = result[:half], result[half:]
+        columns = pl.ds(n * wide, wide)
+        own[:, columns] = jnp.where(at[1] == 0, low, high)
+        other[:, columns] = jnp.where(at[1] == 0, high, low).astype(bf16)
 
 
 def local_call(kernel, shapes, operands, name, flops, nbytes, smem=False, scratch=()):
@@ -248,7 +253,7 @@
         local_call(
             functools.partial(down_back_kernel, part),
             half_shapes(128, hidden // 2),
-            (at, x.reshape(2, 128, width), down),
+            (at, x.reshape(256, width), down),
             f"down_back_{part}",
             256 * width * hidden,
             width * hidden,
@@ -263,10 +268,23 @@
     first = at[0] == 1
     half, columns = 128, xs.shape[1] // 2
     width = out.shape[-1]
-    for i in range(2):
-        for j in range(2):
-            ref = inputs[2 * i + j]
-            xs[pl.ds(i * half, half), pl.ds(j * columns, columns)] = ref[:, pl.ds(0, columns)]
+    if mode:
+        for i in range(2):
+            for j in range(2):
+                ref = inputs[2 * i + j]
+                xs[pl.ds(i * half, half), pl.ds(j * columns, columns)] = ref[:, pl.ds(0, columns)]
+
+    def direct(weight):
+        def step(n, carry):
+            at_n = pl.ds(pl.multiple_of(n * 512, 512), 512)
+            for i in range(2):
+                result = mul(inputs[2 * i][...], weight[pl.ds(0, columns), at_n], NN)
+                result = result + mul(inputs[2 * i + 1][...], weight[pl.ds(columns, columns), at_n], NN)
+                for k in range(4):
+                    out[(4 * i + k + 4 * at[1]) % 8, :, at_n] = result[k * 32 : k * 32 + 32].astype(bf16)
+            return carry
+
+        lax.fori_loop(0, width // 512, step, 0)
 
     def terms():
         gain, x = rest[:2]
@@ -308,7 +326,7 @@
         lax.fori_loop(0, width // 512, step, 0)
 
     if mode == 0:
-        steps(rest[0], NN, False)
+        pl.when(first)(lambda: direct(rest[0]))
     elif mode == 1:
         steps(rest[2], NT, True)
     else:
@@ -357,18 +375,15 @@
     total_width = 8192
     lane = lax.broadcasted_iota(jnp.int32, (1, LANES), 1)
     if mode == 0:
-        gains = gains_out
-        gains[...] = jnp.zeros_like(gains)
         for q, (held, arrived) in enumerate(sums):
             columns = pl.ds(q * wide, wide)
             extra = held[pl.ds(128, EXTRA), pl.ds(0, wide)] + arrived[pl.ds(128, EXTRA), pl.ds(0, wide)].astype(f32)
             rows8 = jnp.concatenate(
                 [jnp.sum(extra[3 * r : 3 * r + 3], axis=0, keepdims=True) for r in range(8)], axis=0
             )
+            gains_out[:, columns] = rows8
             totals_out[:, columns] = jnp.sum(rows8, axis=0, keepdims=True)
-            split = pieces32(rows8)
-            stacked = jnp.concatenate([split[j] for _, j in COMBOS], axis=0)
-            gains[pl.ds(0, 48), columns] = stacked.astype(bf16)
+        gains = gains_out
     if stats_out is not None:
         stats = stats_out
         held, arrived = sums[1]
@@ -394,7 +409,10 @@
     if mode != 2:
         for q in range(4):
             columns = pl.ds(q * 512, 512)
-            shifted[:, columns] = mul(factors[...], gains[:, columns], NN)
+            split = pieces32(gains[:, columns])
+            zeros = jnp.zeros((LANES - 8 * len(COMBOS), 512), f32)
+            stacked = jnp.concatenate([split[j] for _, j in COMBOS] + [zeros], axis=0)
+            shifted[:, columns] = mul(factors[...], stacked.astype(bf16), NN)
 
     size, span = 16, 512
 
@@ -412,18 +430,17 @@
             if mode != 2:
                 value = inv_std * (value + shifted[rows, columns])
             pre = saved[rows, columns] if mode == 2 else value
+            square = pre * pre
+            gate = gelu_gate(pre, square)
             if mode == 0:
                 saved_out[rows, columns] = pre
-                chunk[rows, columns] = gelu_value(pre).astype(bf16)
+                chunk[rows, columns] = (pre * gate).astype(bf16)
                 continue
-            tangent = gelu_tangent(pre)
-            slope = 0.5 * (1.0 + tangent) + 0.5 * pre * (1.0 - tangent * tangent) * gelu_coeff * (
-                1.0 + 3.0 * 0.044715 * pre * pre
-            )
+            slope = gelu_slope(pre, square, gate)
             grad = (value if mode == 2 else saved[rows, columns]) * slope
             grad_sent = grad.astype(bf16)
             if mode == 1:
-                hidden_out[rows, columns] = (0.5 * pre * (1.0 + tangent)).astype(bf16)
+                hidden_out[rows, columns] = (pre * gate).astype(bf16)
                 chunk[rows, columns] = grad_sent
             else:
                 chunk[rows, columns] = jnp.where(first, grad_sent, hidden[rows, columns])
@@ -462,7 +479,7 @@
     shapes = [jax.ShapeDtypeStruct((128, wide + (LANES if mode else 0)), bf16)]
     if mode == 0:
         shapes.append(jax.ShapeDtypeStruct((128, wide), f32))
-        shapes.append(jax.ShapeDtypeStruct((LANES, wide), bf16))
+        shapes.append(jax.ShapeDtypeStruct((8, wide), f32))
         shapes.append(jax.ShapeDtypeStruct((1, wide), f32))
     if mode == 1:
         shapes.append(jax.ShapeDtypeStruct((128, wide), bf16))

time: 232 us -> 228 us (0.983)
  starting transfers between devices: 50 us -> 47.3 us
    ppermute x1, starting transfers between devices: 7.51 us -> 4.94 us  [body(): middle = lax.ppermute(finish(parts, own_feed, False), 'section', [(0, 1)])]
where the time goes in v2:
time: 228 us
  waiting for transfers between devices  85.3 us (37%)
  blocking collectives  47.5 us (21%)
  starting transfers between devices  47.3 us (21%)
  Pallas kernels  43.6 us (19%)
  other arithmetic  2.66 us (1%)
    ppermute x36, waiting for transfers between devices, permuted(): lax.ppermute(array, axis, [(i, mapping(i)) for i in range(lax.axis_size(a...  57.2 us
    all_to_all x4, blocking collectives, along_tp(): return lax.all_to_all(part, 'tp', 0, 0)  47.5 us
    ppermute x36, starting transfers between devices, permuted(): lax.ppermute(array, axis, [(i, mapping(i)) for i in range(lax.axis_size(a...  32.3 us
    pallas_call x14, Pallas kernels, local_call(): pl.pallas_call(kernel, out_shape=shapes, in_specs=specs, out_specs=[VMEM]...  32 us
    all_to_all x2, waiting for transfers between devices, along_tp(): return lax.all_to_all(part, 'tp', 0, 0)  19.7 us
    all_to_all x2, starting transfers between devices, along_tp(): return lax.all_to_all(part, 'tp', 0, 0)  8.8 us
    pallas_call x1, Pallas kernels, start_in(): pl.pallas_call(start_kernel, out_shape=half_shapes(rows, hidden // 2 + LA...  6.57 us
    ppermute x1, waiting for transfers between devices, body(): back = lax.ppermute(finish(parts, own_feed, False), 'section', [(1, 0)])  6.52 us
  transfers between devices with their start and end apart: 40, of which 25 were waited for; matrix products, arithmetic and copies ran while one was open for 1% of the time, Pallas kernels for 8%

profile of v2, /device:TPU:0, one launch (start us, length us, event | category | flops | bytes accessed | tf_op | source)
XLA Modules:
  0.0 227.7 jit_solution(12700818233271784235)
XLA Ops:
  0.1 6.6 %start_in.1 = (f32[160,2176]{1,0:T(8,128)S(1)}, bf16[160,2176]{1,0:T(8,128)(2,1)S(1)}, f32[160,2048]{1,0:T(8,128)S(1)}, bf16[160,2048]{1,0:T(8,128)(2,1)S(1)}) custom-call(s32[3]{0:T(128)S(1)} %pad_add_fusion.at, bf16[2,4,32,1024]{3,2,1,0:T(8,128)(2,1)} %bitcast.28, f32[1,1024]{1,0:T(1,128)} %refs_4_.3, bf16[1024,4096]{1,0:T(8,128)(2,1)} %bitcast.20, ...), custom_call_target="tpu_custom_call" | custom-call | flops 2147483648 | bytes 8388608 | tf_op jit(solution)/shard_map/start_in/pallas_call | solution.py:148
  11.1 2.6 %collective-permute-start.3 = (bf16[160,1152]{1,0:T(8,128)(2,1)S(1)}, bf16[160,1152]{1,0:T(8,128)(2,1)S(1)}, u32[]{:S(2)}, u32[]{:S(2)}) collective-permute-start(bf16[160,1152]{1,0:T(8,128)(2,1)S(1)} %fusion), channel_id=1, source_target_pairs={{0,48},{8,56},{16,32},{24,40},{32,16},{40,24},{48,0},{56,8},{1,49}... | collective-permute-start | bytes 1105928 | tf_op jit(solution)/shard_map/ppermute | solution.py:527
  15.2 4.4 %collective-permute-done.1 = bf16[160,1024]{1,0:T(8,128)(2,1)S(1)} collective-permute-done((bf16[160,1024]{1,0:T(8,128)(2,1)S(1)}, bf16[160,1024]{1,0:T(8,128)(2,1)S(1)}, u32[]{:S(2)}, u32[]{:S(2)}) %collective-permute-start.1) | collective-permute-done | bytes 327712 | tf_op jit(solution)/shard_map/ppermute | solution.py:527
  19.7 4.2 %collective-permute-start.2 = (bf16[160,1024]{1,0:T(8,128)(2,1)S(1)}, bf16[160,1024]{1,0:T(8,128)(2,1)S(1)}, u32[]{:S(2)}, u32[]{:S(2)}) collective-permute-start(bf16[160,1024]{1,0:T(8,128)(2,1)S(1)} %get-tuple-element.83), channel_id=1, source_target_pairs={{0,48},{8,56},{16,32},{24,40},{32,16},{40,24},{48,0},{56,8},{1,49}... | collective-permute-start | bytes 983048 | tf_op jit(solution)/shard_map/ppermute | solution.py:527
  24.4 6.5 %collective-permute-done.8 = bf16[160,1024]{1,0:T(8,128)(2,1)S(1)} collective-permute-done((bf16[160,1024]{1,0:T(8,128)(2,1)S(1)}, bf16[160,1024]{1,0:T(8,128)(2,1)S(1)}, u32[]{:S(2)}, u32[]{:S(2)}) %collective-permute-start.8) | collective-permute-done | bytes 327712 | tf_op jit(solution)/shard_map/ppermute | solution.py:527
  31.3 2.6 %collective-permute-start.7 = (bf16[160,1024]{1,0:T(8,128)(2,1)S(1)}, bf16[160,1024]{1,0:T(8,128)(2,1)S(1)}, u32[]{:S(2)}, u32[]{:S(2)}) collective-permute-start(bf16[160,1024]{1,0:T(8,128)(2,1)S(1)} %get-tuple-element.85), channel_id=1, source_target_pairs={{0,48},{8,56},{16,32},{24,40},{32,16},{40,24},{48,0},{56,8},{1,49}... | collective-permute-start | bytes 983048 | tf_op jit(solution)/shard_map/ppermute | solution.py:527
  33.9 4.0 %collective-permute-done.2.refs_1_ = bf16[160,1024]{1,0:T(8,128)(2,1)S(1)} collective-permute-done((bf16[160,1024]{1,0:T(8,128)(2,1)S(1)}, bf16[160,1024]{1,0:T(8,128)(2,1)S(1)}, u32[]{:S(2)}, u32[]{:S(2)}) %collective-permute-start.2) | collective-permute-done | bytes 327712 | tf_op jit(solution)/shard_map/ppermute | solution.py:527
  37.9 2.9 %act_0_0.1 = (bf16[128,2048]{1,0:T(8,128)(2,1)S(1)}, f32[128,2048]{1,0:T(8,128)S(1)}, f32[8,2048]{1,0:T(8,128)S(1)}, f32[1,2048]{1,0:T(1,128)S(1)}, f32[128,128]...) custom-call(s32[3]{0:T(128)S(1)} %pad_add_fusion.at, f32[160,1024]{1,0:T(8,128)S(1)} %get-tuple-element.84.refs_0_, ...), custom_call_target="tpu_custom_call" | custom-call | flops 10485760 | bytes 4194304 | tf_op jit(solution)/shard_map/act_0_0/pallas_call | solution.py:231
  40.9 2.9 %collective-permute-done.7.refs_1_ = bf16[160,1024]{1,0:T(8,128)(2,1)S(1)} collective-permute-done((bf16[160,1024]{1,0:T(8,128)(2,1)S(1)}, bf16[160,1024]{1,0:T(8,128)(2,1)S(1)}, u32[]{:S(2)}, u32[]{:S(2)}) %collective-permute-start.7) | collective-permute-done | bytes 327712 | tf_op jit(solution)/shard_map/ppermute | solution.py:527
  47.8 4.1 %row_out_0.1 = bf16[8,32,1024]{2,1,0:T(8,128)(2,1)} custom-call(s32[3]{0:T(128)S(1)} %pad_add_fusion.at, bf16[128,2048]{1,0:T(8,128)(2,1)S(1)} %get-tuple-element.35.refs_0_, bf16[128,2048]{1,0:T(8,128)(2,1)S(1)} %get-tuple-element.40.refs_1_, bf16[128,2048]{1,0:T(8,128)(2,1)S(1)} %collective-permute-done.10.refs_2_, ...), custom_call_target="tpu_custom_call" | custom-call | flops 2147483648 | bytes 8388608 | tf_op jit(solution)/shard_map/row_out_0/pallas_call | solution.py:231
  51.9 5.3 %all-to-all-start = ((bf16[8,32,1024]{2,1,0:T(8,128)(2,1)}), bf16[8,32,1024]{2,1,0:T(8,128)(2,1)S(1)}, u32[]{:S(2)}, u32[]{:S(2)}) async-start(bf16[8,32,1024]{2,1,0:T(8,128)(2,1)} %row_out_0.1), calls=%async_computation | async-start | bytes 1048576 | tf_op jit(solution)/shard_map/all_to_all | solution.py:572
  57.2 9.7 %all-to-all-done.parts = bf16[8,32,1024]{2,1,0:T(8,128)(2,1)S(1)} async-done(((bf16[8,32,1024]{2,1,0:T(8,128)(2,1)}), bf16[8,32,1024]{2,1,0:T(8,128)(2,1)S(1)}, u32[]{:S(2)}, u32[]{:S(2)}) %all-to-all-start) | async-done | bytes 524320 | tf_op jit(solution)/shard_map/all_to_all | solution.py:572
  67.0 4.9 %collective-permute-start.12 = (bf16[32,1024]{1,0:T(8,128)(2,1)S(1)}, bf16[32,1024]{1,0:T(8,128)(2,1)S(1)}, u32[]{:S(2)}, u32[]{:S(2)}) collective-permute-start(bf16[32,1024]{1,0:T(8,128)(2,1)S(1)} %finish.3), channel_id=1, source_target_pairs={{0,64},{1,65},{2,66},{3,67},{4,68},{5,69},{6,70},{7,71},{8,72},{9,... | collective-permute-start | bytes 196616 | tf_op jit(solution)/shard_map/ppermute | solution.py:585
  73.9 11.2 %all_to_all.30.x.refs_5_ = bf16[8,32,1024]{2,1,0:T(8,128)(2,1)S(1)} all-to-all(bf16[8,32,1024]{2,1,0:T(8,128)(2,1)S(1)} %broadcast_in_dim.4), channel_id=1, replica_groups=mesh['section'=2,'row'=8,'tp'=8] {'tp'}, dimensions={0} | all-to-all | bytes 1048576 | tf_op jit(solution)/shard_map/all_to_all | solution.py:572
  85.1 5.0 %up_in.1 = (f32[128,2176]{1,0:T(8,128)S(1)}, bf16[128,2176]{1,0:T(8,128)(2,1)S(1)}, f32[128,2048]{1,0:T(8,128)S(1)}, bf16[128,2048]{1,0:T(8,128)(2,1)S(1)}) custom-call(s32[3]{0:T(128)S(1)} %pad_add_fusion.at, bf16[8,32,1024]{2,1,0:T(8,128)(2,1)S(1)} %all_to_all.30.x.refs_5_, f32[1,1024]{1,0:T(1,128)S(1)} %copy-done.1, bf16[1024,4096]{1,0:T(8,128)(2,1)} %bitcast.21), custom_call_target="tpu_custom_call" | custom-call | flops 2147483648 | bytes 8388608 | tf_op jit(solution)/shard_map/up_in/pallas_call | solution.py:199
  96.8 4.7 %collective-permute-done.14 = bf16[128,1024]{1,0:T(8,128)(2,1)S(1)} collective-permute-done((bf16[128,1024]{1,0:T(8,128)(2,1)S(1)}, bf16[128,1024]{1,0:T(8,128)(2,1)S(1)}, u32[]{:S(2)}, u32[]{:S(2)}) %collective-permute-start.14) | collective-permute-done | bytes 262176 | tf_op jit(solution)/shard_map/ppermute | solution.py:527
  101.6 2.6 %collective-permute-start.15 = (bf16[128,1024]{1,0:T(8,128)(2,1)S(1)}, bf16[128,1024]{1,0:T(8,128)(2,1)S(1)}, u32[]{:S(2)}, u32[]{:S(2)}) collective-permute-start(bf16[128,1024]{1,0:T(8,128)(2,1)S(1)} %get-tuple-element.75), channel_id=1, source_target_pairs={{0,48},{8,56},{16,32},{24,40},{32,16},{40,24},{48,0},{56,8},{1,49}... | collective-permute-start | bytes 786440 | tf_op jit(solution)/shard_map/ppermute | solution.py:527
  104.6 5.2 %collective-permute-done.21 = bf16[128,1024]{1,0:T(8,128)(2,1)S(1)} collective-permute-done((bf16[128,1024]{1,0:T(8,128)(2,1)S(1)}, bf16[128,1024]{1,0:T(8,128)(2,1)S(1)}, u32[]{:S(2)}, u32[]{:S(2)}) %collective-permute-start.21) | collective-permute-done | bytes 262176 | tf_op jit(solution)/shard_map/ppermute | solution.py:527
  112.5 2.9 %collective-permute-done.15.refs_1_ = bf16[128,1024]{1,0:T(8,128)(2,1)S(1)} collective-permute-done((bf16[128,1024]{1,0:T(8,128)(2,1)S(1)}, bf16[128,1024]{1,0:T(8,128)(2,1)S(1)}, u32[]{:S(2)}, u32[]{:S(2)}) %collective-permute-start.15) | collective-permute-done | bytes 262176 | tf_op jit(solution)/shard_map/ppermute | solution.py:527
  115.4 3.8 %act_1_0.1 = (bf16[128,2176]{1,0:T(8,128)(2,1)S(1)}, bf16[128,2048]{1,0:T(8,128)(2,1)S(1)}, f32[128,128]{1,0:T(8,128)S(1)}, bf16[128,128]{1,0:T(8,128)(2,1)S(1)}) custom-call(s32[3]{0:T(128)S(1)} %pad_add_fusion.at, f32[128,1024]{1,0:T(8,128)S(1)} %get-tuple-element.76.refs_0_, bf16[128,1024]{1,0:T(8,128)(2,1)S(1)} %collective-permute-done.15.refs_1_, ...), custom_call_target="tpu_custom_call" | custom-call | flops 10485760 | bytes 4194304 | tf_op jit(solution)/shard_map/act_1_0/pallas_call | solution.py:231
  119.9 3.4 %act_1_1.1 = (bf16[128,2176]{1,0:T(8,128)(2,1)S(1)}, bf16[128,2048]{1,0:T(8,128)(2,1)S(1)}) custom-call(s32[3]{0:T(128)S(1)} %pad_add_fusion.at, f32[128,1024]{1,0:T(8,128)S(1)} %get-tuple-element.98.refs_0_, bf16[128,1024]{1,0:T(8,128)(2,1)S(1)} %collective-permute-done.20.refs_1_, f32[128,1024]{1,0:T(8,128)S(1)} %get-tuple-element.70.refs_2_, ...), custom_call_target="tpu_custom_call" | custom-call | flops 10485760 | bytes 4194304 | tf_op jit(solution)/shard_map/act_1_1/pallas_call | solution.py:231
  125.4 3.4 %row_out_1.1 = bf16[8,32,1024]{2,1,0:T(8,128)(2,1)S(1)} custom-call(s32[3]{0:T(128)S(1)} %pad_add_fusion.at, bf16[128,2176]{1,0:T(8,128)(2,1)S(1)} %get-tuple-element.46.refs_0_, bf16[128,2176]{1,0:T(8,128)(2,1)S(1)} %get-tuple-element.54.refs_1_, bf16[128,2176]{1,0:T(8,128)(2,1)S(1)} %collective-permute-done.23.refs_2_, ...), custom_call_target="tpu_custom_call" | custom-call | flops 2147483648 | bytes 8388608 | tf_op jit(solution)/shard_map/row_out_1/pallas_call | solution.py:231
  128.8 12.7 %all_to_all.31.parts = bf16[8,32,1024]{2,1,0:T(8,128)(2,1)S(1)} all-to-all(bf16[8,32,1024]{2,1,0:T(8,128)(2,1)S(1)} %row_out_1.1), channel_id=1, replica_groups=mesh['section'=2,'row'=8,'tp'=8] {'tp'}, dimensions={0} | all-to-all | bytes 1048576 | tf_op jit(solution)/shard_map/all_to_all | solution.py:572
  142.9 6.5 %collective-permute-done.25 = bf16[32,1024]{1,0:T(8,128)(2,1)S(1)} collective-permute-done((bf16[32,1024]{1,0:T(8,128)(2,1)S(1)}, bf16[32,1024]{1,0:T(8,128)(2,1)S(1)}, u32[]{:S(2)}, u32[]{:S(2)}) %collective-permute-start.25) | collective-permute-done | bytes 65568 | tf_op jit(solution)/shard_map/ppermute | solution.py:593
  149.5 11.1 %all_to_all.32 = bf16[8,32,1024]{2,1,0:T(8,128)(2,1)S(1)} all-to-all(bf16[8,32,1024]{2,1,0:T(8,128)(2,1)S(1)} %broadcast_in_dim.5), channel_id=1, replica_groups=mesh['section'=2,'row'=8,'tp'=8] {'tp'}, dimensions={0} | all-to-all | bytes 1048576 | tf_op jit(solution)/shard_map/all_to_all | solution.py:572
  170.1 5.5 %collective-permute-done.29 = bf16[128,1024]{1,0:T(8,128)(2,1)S(1)} collective-permute-done((bf16[128,1024]{1,0:T(8,128)(2,1)S(1)}, bf16[128,1024]{1,0:T(8,128)(2,1)S(1)}, u32[]{:S(2)}, u32[]{:S(2)}) %collective-permute-start.29) | collective-permute-done | bytes 262176 | tf_op jit(solution)/shard_map/ppermute | solution.py:527
  178.3 2.9 %collective-permute-done.34 = bf16[128,1024]{1,0:T(8,128)(2,1)S(1)} collective-permute-done((bf16[128,1024]{1,0:T(8,128)(2,1)S(1)}, bf16[128,1024]{1,0:T(8,128)(2,1)S(1)}, u32[]{:S(2)}, u32[]{:S(2)}) %collective-permute-start.34) | collective-permute-done | bytes 262176 | tf_op jit(solution)/shard_map/ppermute | solution.py:527
  183.9 3.7 %collective-permute-done.28.refs_1_ = bf16[128,1024]{1,0:T(8,128)(2,1)S(1)} collective-permute-done((bf16[128,1024]{1,0:T(8,128)(2,1)S(1)}, bf16[128,1024]{1,0:T(8,128)(2,1)S(1)}, u32[]{:S(2)}, u32[]{:S(2)}) %collective-permute-start.28) | collective-permute-done | bytes 262176 | tf_op jit(solution)/shard_map/ppermute | solution.py:527
  196.6 4.3 %row_out_2.1 = bf16[8,32,1024]{2,1,0:T(8,128)(2,1)} custom-call(s32[3]{0:T(128)S(1)} %pad_add_fusion.at, bf16[128,2176]{1,0:T(8,128)(2,1)S(1)} %act_2_0.1.refs_0_, bf16[128,2176]{1,0:T(8,128)(2,1)S(1)} %act_2_1.1.refs_1_, bf16[128,2176]{1,0:T(8,128)(2,1)S(1)} %collective-permute-done.36.refs_2_, bf16[128,2176]{1,0:T(8,128)(2,1)S(1)} %collective-permute-done.37.refs_3_, ...), custom_call_target="tpu_custom_call" | custom-call | flops 2147483648 | bytes 8388608 | tf_op jit(solution)/shard_map/row_out_2/pallas_call | solution.py:231
  200.9 3.5 %all-to-all-start.4 = ((bf16[8,32,1024]{2,1,0:T(8,128)(2,1)}), bf16[8,32,1024]{2,1,0:T(8,128)(2,1)S(1)}, u32[]{:S(2)}, u32[]{:S(2)}) async-start(bf16[8,32,1024]{2,1,0:T(8,128)(2,1)} %row_out_2.1), calls=%async_computation.4 | async-start | bytes 1048576 | tf_op jit(solution)/shard_map/all_to_all | solution.py:572
  204.4 10.0 %all-to-all-done.4.parts = bf16[8,32,1024]{2,1,0:T(8,128)(2,1)S(1)} async-done(((bf16[8,32,1024]{2,1,0:T(8,128)(2,1)}), bf16[8,32,1024]{2,1,0:T(8,128)(2,1)S(1)}, u32[]{:S(2)}, u32[]{:S(2)}) %all-to-all-start.4) | async-done | bytes 524320 | tf_op jit(solution)/shard_map/all_to_all | solution.py:572
  214.4 12.5 %all_to_all.33 = bf16[8,32,1024]{2,1,0:T(8,128)(2,1)S(1)} all-to-all(bf16[8,32,1024]{2,1,0:T(8,128)(2,1)S(1)} %finish.5), channel_id=1, replica_groups=mesh['section'=2,'row'=8,'tp'=8] {'tp'}, dimensions={0} | all-to-all | bytes 1048576 | tf_op jit(solution)/shard_map/all_to_all | solution.py:572
  (109 shorter events, 51.6 us)
Async XLA Ops:
  6.7 7.0 %collective-permute-start.5 = (bf16[160,2048]{1,0:T(8,128)(2,1)S(1)}, bf16[160,2048]{1,0:T(8,128)(2,1)S(1)}, u32[]{:S(2)}, u32[]{:S(2)}) collective-permute-start(bf16[160,2048]{1,0:T(8,128)(2,1)S(1)} %get-tuple-element.37), channel_id=1, source_target_pairs={{0,8},{8,0},{16,24},{24,16},{32,40},{40,32},{48,56},{56,48},{1,9},... | collective-permute-start | bytes 1966088 | tf_op jit(solution)/shard_map/ppermute | solution.py:527
  9.0 10.6 %collective-permute-start.1 = (bf16[160,1024]{1,0:T(8,128)(2,1)S(1)}, bf16[160,1024]{1,0:T(8,128)(2,1)S(1)}, u32[]{:S(2)}, u32[]{:S(2)}) collective-permute-start(bf16[160,1024]{1,0:T(8,128)(2,1)S(1)} %fusion.1), channel_id=1, source_target_pairs={{0,16},{8,24},{16,0},{24,8},{32,48},{40,56},{48,32},{56,40},{1,17}... | collective-permute-start | bytes 983048 | tf_op jit(solution)/shard_map/ppermute | solution.py:527
  11.1 12.8 %collective-permute-start.3 = (bf16[160,1152]{1,0:T(8,128)(2,1)S(1)}, bf16[160,1152]{1,0:T(8,128)(2,1)S(1)}, u32[]{:S(2)}, u32[]{:S(2)}) collective-permute-start(bf16[160,1152]{1,0:T(8,128)(2,1)S(1)} %fusion), channel_id=1, source_target_pairs={{0,48},{8,56},{16,32},{24,40},{32,16},{40,24},{48,0},{56,8},{1,49}... | collective-permute-start | bytes 1105928 | tf_op jit(solution)/shard_map/ppermute | solution.py:527
  14.0 16.9 %collective-permute-start.8 = (bf16[160,1024]{1,0:T(8,128)(2,1)S(1)}, bf16[160,1024]{1,0:T(8,128)(2,1)S(1)}, u32[]{:S(2)}, u32[]{:S(2)}) collective-permute-start(bf16[160,1024]{1,0:T(8,128)(2,1)S(1)} %get-tuple-element.87), channel_id=1, source_target_pairs={{0,48},{8,56},{16,32},{24,40},{32,16},{40,24},{48,0},{56,8},{1,49}... | collective-permute-start | bytes 983048 | tf_op jit(solution)/shard_map/ppermute | solution.py:527
  14.8 16.2 %collective-permute-start.6 = (bf16[160,1024]{1,0:T(8,128)(2,1)S(1)}, bf16[160,1024]{1,0:T(8,128)(2,1)S(1)}, u32[]{:S(2)}, u32[]{:S(2)}) collective-permute-start(bf16[160,1024]{1,0:T(8,128)(2,1)S(1)} %get-tuple-element.88), channel_id=1, source_target_pairs={{0,16},{8,24},{16,0},{24,8},{32,48},{40,56},{48,32},{56,40},{1,17}... | collective-permute-start | bytes 983048 | tf_op jit(solution)/shard_map/ppermute | solution.py:527
  19.7 18.2 %collective-permute-start.2 = (bf16[160,1024]{1,0:T(8,128)(2,1)S(1)}, bf16[160,1024]{1,0:T(8,128)(2,1)S(1)}, u32[]{:S(2)}, u32[]{:S(2)}) collective-permute-start(bf16[160,1024]{1,0:T(8,128)(2,1)S(1)} %get-tuple-element.83), channel_id=1, source_target_pairs={{0,48},{8,56},{16,32},{24,40},{32,16},{40,24},{48,0},{56,8},{1,49}... | collective-permute-start | bytes 983048 | tf_op jit(solution)/shard_map/ppermute | solution.py:527
  24.1 13.9 %collective-permute-start.4 = (bf16[160,1152]{1,0:T(8,128)(2,1)S(1)}, bf16[160,1152]{1,0:T(8,128)(2,1)S(1)}, u32[]{:S(2)}, u32[]{:S(2)}) collective-permute-start(bf16[160,1152]{1,0:T(8,128)(2,1)S(1)} %get-tuple-element.81), channel_id=1, source_target_pairs={{0,16},{8,24},{16,0},{24,8},{32,48},{40,56},{48,32},{56,40},{1,17}... | collective-permute-start | bytes 1105928 | tf_op jit(solution)/shard_map/ppermute | solution.py:527
  31.3 12.5 %collective-permute-start.7 = (bf16[160,1024]{1,0:T(8,128)(2,1)S(1)}, bf16[160,1024]{1,0:T(8,128)(2,1)S(1)}, u32[]{:S(2)}, u32[]{:S(2)}) collective-permute-start(bf16[160,1024]{1,0:T(8,128)(2,1)S(1)} %get-tuple-element.85), channel_id=1, source_target_pairs={{0,48},{8,56},{16,32},{24,40},{32,16},{40,24},{48,0},{56,8},{1,49}... | collective-permute-start | bytes 983048 | tf_op jit(solution)/shard_map/ppermute | solution.py:527
  33.9 9.9 %collective-permute-start.9 = (bf16[160,1024]{1,0:T(8,128)(2,1)S(1)}, bf16[160,1024]{1,0:T(8,128)(2,1)S(1)}, u32[]{:S(2)}, u32[]{:S(2)}) collective-permute-start(bf16[160,1024]{1,0:T(8,128)(2,1)S(1)} %get-tuple-element.77), channel_id=1, source_target_pairs={{0,16},{8,24},{16,0},{24,8},{32,48},{40,56},{48,32},{56,40},{1,17}... | collective-permute-start | bytes 983048 | tf_op jit(solution)/shard_map/ppermute | solution.py:527
  40.8 5.0 %collective-permute-start.10 = (bf16[128,2048]{1,0:T(8,128)(2,1)S(1)}, bf16[128,2048]{1,0:T(8,128)(2,1)S(1)}, u32[]{:S(2)}, u32[]{:S(2)}) collective-permute-start(bf16[128,2048]{1,0:T(8,128)(2,1)S(1)} %get-tuple-element.35.refs_0_), channel_id=1, source_target_pairs={{0,8},{8,0},{16,24},{24,16},{32,40},{40,32},{48,56},{56,48},{1,9},... | collective-permute-start | bytes 1572872 | tf_op jit(solution)/shard_map/ppermute | solution.py:527
  51.9 15.1 %all-to-all-start = ((bf16[8,32,1024]{2,1,0:T(8,128)(2,1)}), bf16[8,32,1024]{2,1,0:T(8,128)(2,1)S(1)}, u32[]{:S(2)}, u32[]{:S(2)}) async-start(bf16[8,32,1024]{2,1,0:T(8,128)(2,1)} %row_out_0.1), calls=%async_computation | async-start | bytes 1048576 | tf_op jit(solution)/shard_map/all_to_all | solution.py:572
  67.0 6.8 %collective-permute-start.12 = (bf16[32,1024]{1,0:T(8,128)(2,1)S(1)}, bf16[32,1024]{1,0:T(8,128)(2,1)S(1)}, u32[]{:S(2)}, u32[]{:S(2)}) collective-permute-start(bf16[32,1024]{1,0:T(8,128)(2,1)S(1)} %finish.3), channel_id=1, source_target_pairs={{0,64},{1,65},{2,66},{3,67},{4,68},{5,69},{6,70},{7,71},{8,72},{9,... | collective-permute-start | bytes 196616 | tf_op jit(solution)/shard_map/ppermute | solution.py:585
  90.3 5.2 %collective-permute-start.18 = (bf16[128,2048]{1,0:T(8,128)(2,1)S(1)}, bf16[128,2048]{1,0:T(8,128)(2,1)S(1)}, u32[]{:S(2)}, u32[]{:S(2)}) collective-permute-start(bf16[128,2048]{1,0:T(8,128)(2,1)S(1)} %get-tuple-element.48), channel_id=1, source_target_pairs={{0,8},{8,0},{16,24},{24,16},{32,40},{40,32},{48,56},{56,48},{1,9},... | collective-permute-start | bytes 1572872 | tf_op jit(solution)/shard_map/ppermute | solution.py:527
  92.3 9.2 %collective-permute-start.14 = (bf16[128,1024]{1,0:T(8,128)(2,1)S(1)}, bf16[128,1024]{1,0:T(8,128)(2,1)S(1)}, u32[]{:S(2)}, u32[]{:S(2)}) collective-permute-start(bf16[128,1024]{1,0:T(8,128)(2,1)S(1)} %fusion.5), channel_id=1, source_target_pairs={{0,16},{8,24},{16,0},{24,8},{32,48},{40,56},{48,32},{56,40},{1,17}... | collective-permute-start | bytes 786440 | tf_op jit(solution)/shard_map/ppermute | solution.py:527
  93.0 11.2 %collective-permute-start.16 = (bf16[128,1152]{1,0:T(8,128)(2,1)S(1)}, bf16[128,1152]{1,0:T(8,128)(2,1)S(1)}, u32[]{:S(2)}, u32[]{:S(2)}) collective-permute-start(bf16[128,1152]{1,0:T(8,128)(2,1)S(1)} %fusion.4), channel_id=1, source_target_pairs={{0,48},{8,56},{16,32},{24,40},{32,16},{40,24},{48,0},{56,8},{1,49}... | collective-permute-start | bytes 884744 | tf_op jit(solution)/shard_map/ppermute | solution.py:527
  95.6 14.2 %collective-permute-start.21 = (bf16[128,1024]{1,0:T(8,128)(2,1)S(1)}, bf16[128,1024]{1,0:T(8,128)(2,1)S(1)}, u32[]{:S(2)}, u32[]{:S(2)}) collective-permute-start(bf16[128,1024]{1,0:T(8,128)(2,1)S(1)} %get-tuple-element.99), channel_id=1, source_target_pairs={{0,48},{8,56},{16,32},{24,40},{32,16},{40,24},{48,0},{56,8},{1,49}... | collective-permute-start | bytes 786440 | tf_op jit(solution)/shard_map/ppermute | solution.py:527
  96.6 13.3 %collective-permute-start.19 = (bf16[128,1024]{1,0:T(8,128)(2,1)S(1)}, bf16[128,1024]{1,0:T(8,128)(2,1)S(1)}, u32[]{:S(2)}, u32[]{:S(2)}) collective-permute-start(bf16[128,1024]{1,0:T(8,128)(2,1)S(1)} %get-tuple-element.100), channel_id=1, source_target_pairs={{0,16},{8,24},{16,0},{24,8},{32,48},{40,56},{48,32},{56,40},{1,17}... | collective-permute-start | bytes 786440 | tf_op jit(solution)/shard_map/ppermute | solution.py:527
  101.6 13.8 %collective-permute-start.15 = (bf16[128,1024]{1,0:T(8,128)(2,1)S(1)}, bf16[128,1024]{1,0:T(8,128)(2,1)S(1)}, u32[]{:S(2)}, u32[]{:S(2)}) collective-permute-start(bf16[128,1024]{1,0:T(8,128)(2,1)S(1)} %get-tuple-element.75), channel_id=1, source_target_pairs={{0,48},{8,56},{16,32},{24,40},{32,16},{40,24},{48,0},{56,8},{1,49}... | collective-permute-start | bytes 786440 | tf_op jit(solution)/shard_map/ppermute | solution.py:527
  104.3 11.1 %collective-permute-start.17 = (bf16[128,1152]{1,0:T(8,128)(2,1)S(1)}, bf16[128,1152]{1,0:T(8,128)(2,1)S(1)}, u32[]{:S(2)}, u32[]{:S(2)}) collective-permute-start(bf16[128,1152]{1,0:T(8,128)(2,1)S(1)} %get-tuple-element.73), channel_id=1, source_target_pairs={{0,16},{8,24},{16,0},{24,8},{32,48},{40,56},{48,32},{56,40},{1,17}... | collective-permute-start | bytes 884744 | tf_op jit(solution)/shard_map/ppermute | solution.py:527
  110.1 9.8 %collective-permute-start.20 = (bf16[128,1024]{1,0:T(8,128)(2,1)S(1)}, bf16[128,1024]{1,0:T(8,128)(2,1)S(1)}, u32[]{:S(2)}, u32[]{:S(2)}) collective-permute-start(bf16[128,1024]{1,0:T(8,128)(2,1)S(1)} %get-tuple-element.97), channel_id=1, source_target_pairs={{0,48},{8,56},{16,32},{24,40},{32,16},{40,24},{48,0},{56,8},{1,49}... | collective-permute-start | bytes 786440 | tf_op jit(solution)/shard_map/ppermute | solution.py:527
  112.5 7.4 %collective-permute-start.22 = (bf16[128,1024]{1,0:T(8,128)(2,1)S(1)}, bf16[128,1024]{1,0:T(8,128)(2,1)S(1)}, u32[]{:S(2)}, u32[]{:S(2)}) collective-permute-start(bf16[128,1024]{1,0:T(8,128)(2,1)S(1)} %get-tuple-element.69), channel_id=1, source_target_pairs={{0,16},{8,24},{16,0},{24,8},{32,48},{40,56},{48,32},{56,40},{1,17}... | collective-permute-start | bytes 786440 | tf_op jit(solution)/shard_map/ppermute | solution.py:527
  141.6 7.8 %collective-permute-start.25 = (bf16[32,1024]{1,0:T(8,128)(2,1)S(1)}, bf16[32,1024]{1,0:T(8,128)(2,1)S(1)}, u32[]{:S(2)}, u32[]{:S(2)}) collective-permute-start(bf16[32,1024]{1,0:T(8,128)(2,1)S(1)} %finish.4), channel_id=1, source_target_pairs={{64,0},{65,1},{66,2},{67,3},{68,4},{69,5},{70,6},{71,7},{72,8},{73... | collective-permute-start | bytes 196616 | tf_op jit(solution)/shard_map/ppermute | solution.py:593
  165.1 10.5 %collective-permute-start.29 = (bf16[128,1024]{1,0:T(8,128)(2,1)S(1)}, bf16[128,1024]{1,0:T(8,128)(2,1)S(1)}, u32[]{:S(2)}, u32[]{:S(2)}) collective-permute-start(bf16[128,1024]{1,0:T(8,128)(2,1)S(1)} %get-tuple-element.95), channel_id=1, source_target_pairs={{0,48},{8,56},{16,32},{24,40},{32,16},{40,24},{48,0},{56,8},{1,49}... | collective-permute-start | bytes 786440 | tf_op jit(solution)/shard_map/ppermute | solution.py:527
  167.5 9.2 %collective-permute-start.27 = (bf16[128,1024]{1,0:T(8,128)(2,1)S(1)}, bf16[128,1024]{1,0:T(8,128)(2,1)S(1)}, u32[]{:S(2)}, u32[]{:S(2)}) collective-permute-start(bf16[128,1024]{1,0:T(8,128)(2,1)S(1)} %get-tuple-element.96), channel_id=1, source_target_pairs={{0,16},{8,24},{16,0},{24,8},{32,48},{40,56},{48,32},{56,40},{1,17}... | collective-permute-start | bytes 786440 | tf_op jit(solution)/shard_map/ppermute | solution.py:527
  167.7 13.5 %collective-permute-start.34 = (bf16[128,1024]{1,0:T(8,128)(2,1)S(1)}, bf16[128,1024]{1,0:T(8,128)(2,1)S(1)}, u32[]{:S(2)}, u32[]{:S(2)}) collective-permute-start(bf16[128,1024]{1,0:T(8,128)(2,1)S(1)} %get-tuple-element.91), channel_id=1, source_target_pairs={{0,48},{8,56},{16,32},{24,40},{32,16},{40,24},{48,0},{56,8},{1,49}... | collective-permute-start | bytes 786440 | tf_op jit(solution)/shard_map/ppermute | solution.py:527
  169.1 13.3 %collective-permute-start.32 = (bf16[128,1024]{1,0:T(8,128)(2,1)S(1)}, bf16[128,1024]{1,0:T(8,128)(2,1)S(1)}, u32[]{:S(2)}, u32[]{:S(2)}) collective-permute-start(bf16[128,1024]{1,0:T(8,128)(2,1)S(1)} %get-tuple-element.92), channel_id=1, source_target_pairs={{0,16},{8,24},{16,0},{24,8},{32,48},{40,56},{48,32},{56,40},{1,17}... | collective-permute-start | bytes 786440 | tf_op jit(solution)/shard_map/ppermute | solution.py:527
  177.0 10.5 %collective-permute-start.28 = (bf16[128,1024]{1,0:T(8,128)(2,1)S(1)}, bf16[128,1024]{1,0:T(8,128)(2,1)S(1)}, u32[]{:S(2)}, u32[]{:S(2)}) collective-permute-start(bf16[128,1024]{1,0:T(8,128)(2,1)S(1)} %get-tuple-element.93), channel_id=1, source_target_pairs={{0,48},{8,56},{16,32},{24,40},{32,16},{40,24},{48,0},{56,8},{1,49}... | collective-permute-start | bytes 786440 | tf_op jit(solution)/shard_map/ppermute | solution.py:527
  178.3 9.7 %collective-permute-start.30 = (bf16[128,1024]{1,0:T(8,128)(2,1)S(1)}, bf16[128,1024]{1,0:T(8,128)(2,1)S(1)}, u32[]{:S(2)}, u32[]{:S(2)}) collective-permute-start(bf16[128,1024]{1,0:T(8,128)(2,1)S(1)} %get-tuple-element.65), channel_id=1, source_target_pairs={{0,16},{8,24},{16,0},{24,8},{32,48},{40,56},{48,32},{56,40},{1,17}... | collective-permute-start | bytes 786440 | tf_op jit(solution)/shard_map/ppermute | solution.py:527
  182.6 8.8 %collective-permute-start.33 = (bf16[128,1024]{1,0:T(8,128)(2,1)S(1)}, bf16[128,1024]{1,0:T(8,128)(2,1)S(1)}, u32[]{:S(2)}, u32[]{:S(2)}) collective-permute-start(bf16[128,1024]{1,0:T(8,128)(2,1)S(1)} %get-tuple-element.89), channel_id=1, source_target_pairs={{0,48},{8,56},{16,32},{24,40},{32,16},{40,24},{48,0},{56,8},{1,49}... | collective-permute-start | bytes 786440 | tf_op jit(solution)/shard_map/ppermute | solution.py:527
  183.9 8.4 %collective-permute-start.35 = (bf16[128,1024]{1,0:T(8,128)(2,1)S(1)}, bf16[128,1024]{1,0:T(8,128)(2,1)S(1)}, u32[]{:S(2)}, u32[]{:S(2)}) collective-permute-start(bf16[128,1024]{1,0:T(8,128)(2,1)S(1)} %get-tuple-element.61), channel_id=1, source_target_pairs={{0,16},{8,24},{16,0},{24,8},{32,48},{40,56},{48,32},{56,40},{1,17}... | collective-permute-start | bytes 786440 | tf_op jit(solution)/shard_map/ppermute | solution.py:527
  190.0 4.6 %collective-permute-start.36 = (bf16[128,2176]{1,0:T(8,128)(2,1)S(1)}, bf16[128,2176]{1,0:T(8,128)(2,1)S(1)}, u32[]{:S(2)}, u32[]{:S(2)}) collective-permute-start(bf16[128,2176]{1,0:T(8,128)(2,1)S(1)} %act_2_0.1.refs_0_), channel_id=1, source_target_pairs={{0,8},{8,0},{16,24},{24,16},{32,40},{40,32},{48,56},{56,48},{1,9},... | collective-permute-start | bytes 1671176 | tf_op jit(solution)/shard_map/ppermute | solution.py:527
  200.9 13.5 %all-to-all-start.4 = ((bf16[8,32,1024]{2,1,0:T(8,128)(2,1)}), bf16[8,32,1024]{2,1,0:T(8,128)(2,1)S(1)}, u32[]{:S(2)}, u32[]{:S(2)}) async-start(bf16[8,32,1024]{2,1,0:T(8,128)(2,1)} %row_out_2.1), calls=%async_computation.4 | async-start | bytes 1048576 | tf_op jit(solution)/shard_map/all_to_all | solution.py:572
  (16 other events, 246.2 us)

commit v3 on v2

--- a/solution.py
+++ b/solution.py
@@ -414,7 +414,7 @@
             stacked = jnp.concatenate([split[j] for _, j in COMBOS] + [zeros], axis=0)
             shifted[:, columns] = mul(factors[...], stacked.astype(bf16), NN)
 
-    size, span = 16, 512
+    size, span = 32, 256
 
     def block(i, carry):
         rows = pl.ds(pl.multiple_of(i * size, size), size)

time: 228 us -> 227 us (level)
  Pallas kernels: 43.6 us -> 40.8 us
    pallas_call x14, Pallas kernels: 32 us -> 29.2 us  [local_call(): pl.pallas_call(kernel, out_shape=shapes, in_specs=specs, out_specs=[VMEM]...]
  transfers between devices with their start and end apart: 40 -> 40, of which waited for: 25 -> 25; matrix products, arithmetic and copies ran while one was open for 1% -> 1% of each run, Pallas kernels for 8% -> 7%
where the time goes in v3:
time: 227 us; the launch traced here: 226 us
  waiting for transfers between devices  86.5 us (38%)
  blocking collectives  47.5 us (21%)
  starting transfers between devices  47.3 us (21%)
  Pallas kernels  40.8 us (18%)
  other arithmetic  2.66 us (1%)
    ppermute x36, waiting for transfers between devices, permuted(): lax.ppermute(array, axis, [(i, mapping(i)) for i in range(lax.axis_size(a...  58.4 us
    all_to_all x4, blocking collectives, along_tp(): return lax.all_to_all(part, 'tp', 0, 0)  47.5 us
    ppermute x36, starting transfers between devices, permuted(): lax.ppermute(array, axis, [(i, mapping(i)) for i in range(lax.axis_size(a...  32.3 us
    pallas_call x14, Pallas kernels, local_call(): pl.pallas_call(kernel, out_shape=shapes, in_specs=specs, out_specs=[VMEM]...  29.2 us
    all_to_all x2, waiting for transfers between devices, along_tp(): return lax.all_to_all(part, 'tp', 0, 0)  19.7 us
    all_to_all x2, starting transfers between devices, along_tp(): return lax.all_to_all(part, 'tp', 0, 0)  8.8 us
    pallas_call x1, Pallas kernels, start_in(): pl.pallas_call(start_kernel, out_shape=half_shapes(rows, hidden // 2 + LA...  6.57 us
    ppermute x1, waiting for transfers between devices, body(): back = lax.ppermute(finish(parts, own_feed, False), 'section', [(1, 0)])  6.52 us
  transfers between devices with their start and end apart: 40, of which 25 were waited for; matrix products, arithmetic and copies ran while one was open for 1% of the time, Pallas kernels for 7%

profile of v3, /device:TPU:0, one launch (start us, length us, event | category | flops | bytes accessed | tf_op | source)
XLA Modules:
  0.0 226.2 jit_solution(16342979536998615525)
XLA Ops:
  0.1 6.6 %start_in.1 = (f32[160,2176]{1,0:T(8,128)S(1)}, bf16[160,2176]{1,0:T(8,128)(2,1)S(1)}, f32[160,2048]{1,0:T(8,128)S(1)}, bf16[160,2048]{1,0:T(8,128)(2,1)S(1)}) custom-call(s32[3]{0:T(128)S(1)} %pad_add_fusion.at, bf16[2,4,32,1024]{3,2,1,0:T(8,128)(2,1)} %bitcast.28, f32[1,1024]{1,0:T(1,128)} %refs_4_.3, bf16[1024,4096]{1,0:T(8,128)(2,1)} %bitcast.20, ...), custom_call_target="tpu_custom_call" | custom-call | flops 2147483648 | bytes 8388608 | tf_op jit(solution)/shard_map/start_in/pallas_call | solution.py:148
  11.1 2.6 %collective-permute-start.3 = (bf16[160,1152]{1,0:T(8,128)(2,1)S(1)}, bf16[160,1152]{1,0:T(8,128)(2,1)S(1)}, u32[]{:S(2)}, u32[]{:S(2)}) collective-permute-start(bf16[160,1152]{1,0:T(8,128)(2,1)S(1)} %fusion), channel_id=1, source_target_pairs={{0,48},{8,56},{16,32},{24,40},{32,16},{40,24},{48,0},{56,8},{1,49}... | collective-permute-start | bytes 1105928 | tf_op jit(solution)/shard_map/ppermute | solution.py:527
  15.2 4.4 %collective-permute-done.1 = bf16[160,1024]{1,0:T(8,128)(2,1)S(1)} collective-permute-done((bf16[160,1024]{1,0:T(8,128)(2,1)S(1)}, bf16[160,1024]{1,0:T(8,128)(2,1)S(1)}, u32[]{:S(2)}, u32[]{:S(2)}) %collective-permute-start.1) | collective-permute-done | bytes 327712 | tf_op jit(solution)/shard_map/ppermute | solution.py:527
  19.7 4.2 %collective-permute-start.2 = (bf16[160,1024]{1,0:T(8,128)(2,1)S(1)}, bf16[160,1024]{1,0:T(8,128)(2,1)S(1)}, u32[]{:S(2)}, u32[]{:S(2)}) collective-permute-start(bf16[160,1024]{1,0:T(8,128)(2,1)S(1)} %get-tuple-element.83), channel_id=1, source_target_pairs={{0,48},{8,56},{16,32},{24,40},{32,16},{40,24},{48,0},{56,8},{1,49}... | collective-permute-start | bytes 983048 | tf_op jit(solution)/shard_map/ppermute | solution.py:527
  24.4 6.5 %collective-permute-done.8 = bf16[160,1024]{1,0:T(8,128)(2,1)S(1)} collective-permute-done((bf16[160,1024]{1,0:T(8,128)(2,1)S(1)}, bf16[160,1024]{1,0:T(8,128)(2,1)S(1)}, u32[]{:S(2)}, u32[]{:S(2)}) %collective-permute-start.8) | collective-permute-done | bytes 327712 | tf_op jit(solution)/shard_map/ppermute | solution.py:527
  31.3 2.6 %collective-permute-start.7 = (bf16[160,1024]{1,0:T(8,128)(2,1)S(1)}, bf16[160,1024]{1,0:T(8,128)(2,1)S(1)}, u32[]{:S(2)}, u32[]{:S(2)}) collective-permute-start(bf16[160,1024]{1,0:T(8,128)(2,1)S(1)} %get-tuple-element.85), channel_id=1, source_target_pairs={{0,48},{8,56},{16,32},{24,40},{32,16},{40,24},{48,0},{56,8},{1,49}... | collective-permute-start | bytes 983048 | tf_op jit(solution)/shard_map/ppermute | solution.py:527
  33.9 4.0 %collective-permute-done.2.refs_1_ = bf16[160,1024]{1,0:T(8,128)(2,1)S(1)} collective-permute-done((bf16[160,1024]{1,0:T(8,128)(2,1)S(1)}, bf16[160,1024]{1,0:T(8,128)(2,1)S(1)}, u32[]{:S(2)}, u32[]{:S(2)}) %collective-permute-start.2) | collective-permute-done | bytes 327712 | tf_op jit(solution)/shard_map/ppermute | solution.py:527
  37.9 2.6 %act_0_0.1 = (bf16[128,2048]{1,0:T(8,128)(2,1)S(1)}, f32[128,2048]{1,0:T(8,128)S(1)}, f32[8,2048]{1,0:T(8,128)S(1)}, f32[1,2048]{1,0:T(1,128)S(1)}, f32[128,128]...) custom-call(s32[3]{0:T(128)S(1)} %pad_add_fusion.at, f32[160,1024]{1,0:T(8,128)S(1)} %get-tuple-element.84.refs_0_, ...), custom_call_target="tpu_custom_call" | custom-call | flops 10485760 | bytes 4194304 | tf_op jit(solution)/shard_map/act_0_0/pallas_call | solution.py:231
  40.6 3.2 %collective-permute-done.7.refs_1_ = bf16[160,1024]{1,0:T(8,128)(2,1)S(1)} collective-permute-done((bf16[160,1024]{1,0:T(8,128)(2,1)S(1)}, bf16[160,1024]{1,0:T(8,128)(2,1)S(1)}, u32[]{:S(2)}, u32[]{:S(2)}) %collective-permute-start.7) | collective-permute-done | bytes 327712 | tf_op jit(solution)/shard_map/ppermute | solution.py:527
  47.5 4.1 %row_out_0.1 = bf16[8,32,1024]{2,1,0:T(8,128)(2,1)} custom-call(s32[3]{0:T(128)S(1)} %pad_add_fusion.at, bf16[128,2048]{1,0:T(8,128)(2,1)S(1)} %get-tuple-element.35.refs_0_, bf16[128,2048]{1,0:T(8,128)(2,1)S(1)} %get-tuple-element.40.refs_1_, bf16[128,2048]{1,0:T(8,128)(2,1)S(1)} %collective-permute-done.10.refs_2_, ...), custom_call_target="tpu_custom_call" | custom-call | flops 2147483648 | bytes 8388608 | tf_op jit(solution)/shard_map/row_out_0/pallas_call | solution.py:231
  51.6 5.3 %all-to-all-start = ((bf16[8,32,1024]{2,1,0:T(8,128)(2,1)}), bf16[8,32,1024]{2,1,0:T(8,128)(2,1)S(1)}, u32[]{:S(2)}, u32[]{:S(2)}) async-start(bf16[8,32,1024]{2,1,0:T(8,128)(2,1)} %row_out_0.1), calls=%async_computation | async-start | bytes 1048576 | tf_op jit(solution)/shard_map/all_to_all | solution.py:572
  56.9 9.7 %all-to-all-done.parts = bf16[8,32,1024]{2,1,0:T(8,128)(2,1)S(1)} async-done(((bf16[8,32,1024]{2,1,0:T(8,128)(2,1)}), bf16[8,32,1024]{2,1,0:T(8,128)(2,1)S(1)}, u32[]{:S(2)}, u32[]{:S(2)}) %all-to-all-start) | async-done | bytes 524320 | tf_op jit(solution)/shard_map/all_to_all | solution.py:572
  66.7 4.9 %collective-permute-start.12 = (bf16[32,1024]{1,0:T(8,128)(2,1)S(1)}, bf16[32,1024]{1,0:T(8,128)(2,1)S(1)}, u32[]{:S(2)}, u32[]{:S(2)}) collective-permute-start(bf16[32,1024]{1,0:T(8,128)(2,1)S(1)} %finish.3), channel_id=1, source_target_pairs={{0,64},{1,65},{2,66},{3,67},{4,68},{5,69},{6,70},{7,71},{8,72},{9,... | collective-permute-start | bytes 196616 | tf_op jit(solution)/shard_map/ppermute | solution.py:585
  73.6 11.2 %all_to_all.30.x.refs_5_ = bf16[8,32,1024]{2,1,0:T(8,128)(2,1)S(1)} all-to-all(bf16[8,32,1024]{2,1,0:T(8,128)(2,1)S(1)} %broadcast_in_dim.4), channel_id=1, replica_groups=mesh['section'=2,'row'=8,'tp'=8] {'tp'}, dimensions={0} | all-to-all | bytes 1048576 | tf_op jit(solution)/shard_map/all_to_all | solution.py:572
  84.8 5.0 %up_in.1 = (f32[128,2176]{1,0:T(8,128)S(1)}, bf16[128,2176]{1,0:T(8,128)(2,1)S(1)}, f32[128,2048]{1,0:T(8,128)S(1)}, bf16[128,2048]{1,0:T(8,128)(2,1)S(1)}) custom-call(s32[3]{0:T(128)S(1)} %pad_add_fusion.at, bf16[8,32,1024]{2,1,0:T(8,128)(2,1)S(1)} %all_to_all.30.x.refs_5_, f32[1,1024]{1,0:T(1,128)S(1)} %copy-done.1, bf16[1024,4096]{1,0:T(8,128)(2,1)} %bitcast.21), custom_call_target="tpu_custom_call" | custom-call | flops 2147483648 | bytes 8388608 | tf_op jit(solution)/shard_map/up_in/pallas_call | solution.py:199
  92.7 2.4 %collective-permute-start.16 = (bf16[128,1152]{1,0:T(8,128)(2,1)S(1)}, bf16[128,1152]{1,0:T(8,128)(2,1)S(1)}, u32[]{:S(2)}, u32[]{:S(2)}) collective-permute-start(bf16[128,1152]{1,0:T(8,128)(2,1)S(1)} %fusion.4), channel_id=1, source_target_pairs={{0,48},{8,56},{16,32},{24,40},{32,16},{40,24},{48,0},{56,8},{1,49}... | collective-permute-start | bytes 884744 | tf_op jit(solution)/shard_map/ppermute | solution.py:527
  96.5 4.7 %collective-permute-done.14 = bf16[128,1024]{1,0:T(8,128)(2,1)S(1)} collective-permute-done((bf16[128,1024]{1,0:T(8,128)(2,1)S(1)}, bf16[128,1024]{1,0:T(8,128)(2,1)S(1)}, u32[]{:S(2)}, u32[]{:S(2)}) %collective-permute-start.14) | collective-permute-done | bytes 262176 | tf_op jit(solution)/shard_map/ppermute | solution.py:527
  101.3 2.6 %collective-permute-start.15 = (bf16[128,1024]{1,0:T(8,128)(2,1)S(1)}, bf16[128,1024]{1,0:T(8,128)(2,1)S(1)}, u32[]{:S(2)}, u32[]{:S(2)}) collective-permute-start(bf16[128,1024]{1,0:T(8,128)(2,1)S(1)} %get-tuple-element.75), channel_id=1, source_target_pairs={{0,48},{8,56},{16,32},{24,40},{32,16},{40,24},{48,0},{56,8},{1,49}... | collective-permute-start | bytes 786440 | tf_op jit(solution)/shard_map/ppermute | solution.py:527
  104.3 5.2 %collective-permute-done.21 = bf16[128,1024]{1,0:T(8,128)(2,1)S(1)} collective-permute-done((bf16[128,1024]{1,0:T(8,128)(2,1)S(1)}, bf16[128,1024]{1,0:T(8,128)(2,1)S(1)}, u32[]{:S(2)}, u32[]{:S(2)}) %collective-permute-start.21) | collective-permute-done | bytes 262176 | tf_op jit(solution)/shard_map/ppermute | solution.py:527
  112.2 2.9 %collective-permute-done.15.refs_1_ = bf16[128,1024]{1,0:T(8,128)(2,1)S(1)} collective-permute-done((bf16[128,1024]{1,0:T(8,128)(2,1)S(1)}, bf16[128,1024]{1,0:T(8,128)(2,1)S(1)}, u32[]{:S(2)}, u32[]{:S(2)}) %collective-permute-start.15) | collective-permute-done | bytes 262176 | tf_op jit(solution)/shard_map/ppermute | solution.py:527
  115.1 3.2 %act_1_0.1 = (bf16[128,2176]{1,0:T(8,128)(2,1)S(1)}, bf16[128,2048]{1,0:T(8,128)(2,1)S(1)}, f32[128,128]{1,0:T(8,128)S(1)}, bf16[128,128]{1,0:T(8,128)(2,1)S(1)}) custom-call(s32[3]{0:T(128)S(1)} %pad_add_fusion.at, f32[128,1024]{1,0:T(8,128)S(1)} %get-tuple-element.76.refs_0_, bf16[128,1024]{1,0:T(8,128)(2,1)S(1)} %collective-permute-done.15.refs_1_, ...), custom_call_target="tpu_custom_call" | custom-call | flops 10485760 | bytes 4194304 | tf_op jit(solution)/shard_map/act_1_0/pallas_call | solution.py:231
  124.0 3.4 %row_out_1.1 = bf16[8,32,1024]{2,1,0:T(8,128)(2,1)S(1)} custom-call(s32[3]{0:T(128)S(1)} %pad_add_fusion.at, bf16[128,2176]{1,0:T(8,128)(2,1)S(1)} %get-tuple-element.46.refs_0_, bf16[128,2176]{1,0:T(8,128)(2,1)S(1)} %get-tuple-element.54.refs_1_, bf16[128,2176]{1,0:T(8,128)(2,1)S(1)} %collective-permute-done.23.refs_2_, ...), custom_call_target="tpu_custom_call" | custom-call | flops 2147483648 | bytes 8388608 | tf_op jit(solution)/shard_map/row_out_1/pallas_call | solution.py:231
  127.5 12.7 %all_to_all.31.parts = bf16[8,32,1024]{2,1,0:T(8,128)(2,1)S(1)} all-to-all(bf16[8,32,1024]{2,1,0:T(8,128)(2,1)S(1)} %row_out_1.1), channel_id=1, replica_groups=mesh['section'=2,'row'=8,'tp'=8] {'tp'}, dimensions={0} | all-to-all | bytes 1048576 | tf_op jit(solution)/shard_map/all_to_all | solution.py:572
  141.6 6.5 %collective-permute-done.25 = bf16[32,1024]{1,0:T(8,128)(2,1)S(1)} collective-permute-done((bf16[32,1024]{1,0:T(8,128)(2,1)S(1)}, bf16[32,1024]{1,0:T(8,128)(2,1)S(1)}, u32[]{:S(2)}, u32[]{:S(2)}) %collective-permute-start.25) | collective-permute-done | bytes 65568 | tf_op jit(solution)/shard_map/ppermute | solution.py:593
  148.2 11.1 %all_to_all.32 = bf16[8,32,1024]{2,1,0:T(8,128)(2,1)S(1)} all-to-all(bf16[8,32,1024]{2,1,0:T(8,128)(2,1)S(1)} %broadcast_in_dim.5), channel_id=1, replica_groups=mesh['section'=2,'row'=8,'tp'=8] {'tp'}, dimensions={0} | all-to-all | bytes 1048576 | tf_op jit(solution)/shard_map/all_to_all | solution.py:572
  168.7 5.5 %collective-permute-done.29 = bf16[128,1024]{1,0:T(8,128)(2,1)S(1)} collective-permute-done((bf16[128,1024]{1,0:T(8,128)(2,1)S(1)}, bf16[128,1024]{1,0:T(8,128)(2,1)S(1)}, u32[]{:S(2)}, u32[]{:S(2)}) %collective-permute-start.29) | collective-permute-done | bytes 262176 | tf_op jit(solution)/shard_map/ppermute | solution.py:527
  176.9 2.9 %collective-permute-done.34 = bf16[128,1024]{1,0:T(8,128)(2,1)S(1)} collective-permute-done((bf16[128,1024]{1,0:T(8,128)(2,1)S(1)}, bf16[128,1024]{1,0:T(8,128)(2,1)S(1)}, u32[]{:S(2)}, u32[]{:S(2)}) %collective-permute-start.34) | collective-permute-done | bytes 262176 | tf_op jit(solution)/shard_map/ppermute | solution.py:527
  182.5 3.7 %collective-permute-done.28.refs_1_ = bf16[128,1024]{1,0:T(8,128)(2,1)S(1)} collective-permute-done((bf16[128,1024]{1,0:T(8,128)(2,1)S(1)}, bf16[128,1024]{1,0:T(8,128)(2,1)S(1)}, u32[]{:S(2)}, u32[]{:S(2)}) %collective-permute-start.28) | collective-permute-done | bytes 262176 | tf_op jit(solution)/shard_map/ppermute | solution.py:527
  195.1 4.3 %row_out_2.1 = bf16[8,32,1024]{2,1,0:T(8,128)(2,1)} custom-call(s32[3]{0:T(128)S(1)} %pad_add_fusion.at, bf16[128,2176]{1,0:T(8,128)(2,1)S(1)} %act_2_0.1.refs_0_, bf16[128,2176]{1,0:T(8,128)(2,1)S(1)} %act_2_1.1.refs_1_, bf16[128,2176]{1,0:T(8,128)(2,1)S(1)} %collective-permute-done.36.refs_2_, bf16[128,2176]{1,0:T(8,128)(2,1)S(1)} %collective-permute-done.37.refs_3_, ...), custom_call_target="tpu_custom_call" | custom-call | flops 2147483648 | bytes 8388608 | tf_op jit(solution)/shard_map/row_out_2/pallas_call | solution.py:231
  199.3 3.5 %all-to-all-start.4 = ((bf16[8,32,1024]{2,1,0:T(8,128)(2,1)}), bf16[8,32,1024]{2,1,0:T(8,128)(2,1)S(1)}, u32[]{:S(2)}, u32[]{:S(2)}) async-start(bf16[8,32,1024]{2,1,0:T(8,128)(2,1)} %row_out_2.1), calls=%async_computation.4 | async-start | bytes 1048576 | tf_op jit(solution)/shard_map/all_to_all | solution.py:572
  202.9 10.0 %all-to-all-done.4.parts = bf16[8,32,1024]{2,1,0:T(8,128)(2,1)S(1)} async-done(((bf16[8,32,1024]{2,1,0:T(8,128)(2,1)}), bf16[8,32,1024]{2,1,0:T(8,128)(2,1)S(1)}, u32[]{:S(2)}, u32[]{:S(2)}) %all-to-all-start.4) | async-done | bytes 524320 | tf_op jit(solution)/shard_map/all_to_all | solution.py:572
  212.9 12.5 %all_to_all.33 = bf16[8,32,1024]{2,1,0:T(8,128)(2,1)S(1)} all-to-all(bf16[8,32,1024]{2,1,0:T(8,128)(2,1)S(1)} %finish.5), channel_id=1, replica_groups=mesh['section'=2,'row'=8,'tp'=8] {'tp'}, dimensions={0} | all-to-all | bytes 1048576 | tf_op jit(solution)/shard_map/all_to_all | solution.py:572
  (109 shorter events, 51.6 us)
Async XLA Ops:
  6.7 7.0 %collective-permute-start.5 = (bf16[160,2048]{1,0:T(8,128)(2,1)S(1)}, bf16[160,2048]{1,0:T(8,128)(2,1)S(1)}, u32[]{:S(2)}, u32[]{:S(2)}) collective-permute-start(bf16[160,2048]{1,0:T(8,128)(2,1)S(1)} %get-tuple-element.37), channel_id=1, source_target_pairs={{0,8},{8,0},{16,24},{24,16},{32,40},{40,32},{48,56},{56,48},{1,9},... | collective-permute-start | bytes 1966088 | tf_op jit(solution)/shard_map/ppermute | solution.py:527
  9.0 10.6 %collective-permute-start.1 = (bf16[160,1024]{1,0:T(8,128)(2,1)S(1)}, bf16[160,1024]{1,0:T(8,128)(2,1)S(1)}, u32[]{:S(2)}, u32[]{:S(2)}) collective-permute-start(bf16[160,1024]{1,0:T(8,128)(2,1)S(1)} %fusion.1), channel_id=1, source_target_pairs={{0,16},{8,24},{16,0},{24,8},{32,48},{40,56},{48,32},{56,40},{1,17}... | collective-permute-start | bytes 983048 | tf_op jit(solution)/shard_map/ppermute | solution.py:527
  11.1 12.8 %collective-permute-start.3 = (bf16[160,1152]{1,0:T(8,128)(2,1)S(1)}, bf16[160,1152]{1,0:T(8,128)(2,1)S(1)}, u32[]{:S(2)}, u32[]{:S(2)}) collective-permute-start(bf16[160,1152]{1,0:T(8,128)(2,1)S(1)} %fusion), channel_id=1, source_target_pairs={{0,48},{8,56},{16,32},{24,40},{32,16},{40,24},{48,0},{56,8},{1,49}... | collective-permute-start | bytes 1105928 | tf_op jit(solution)/shard_map/ppermute | solution.py:527
  14.0 16.9 %collective-permute-start.8 = (bf16[160,1024]{1,0:T(8,128)(2,1)S(1)}, bf16[160,1024]{1,0:T(8,128)(2,1)S(1)}, u32[]{:S(2)}, u32[]{:S(2)}) collective-permute-start(bf16[160,1024]{1,0:T(8,128)(2,1)S(1)} %get-tuple-element.87), channel_id=1, source_target_pairs={{0,48},{8,56},{16,32},{24,40},{32,16},{40,24},{48,0},{56,8},{1,49}... | collective-permute-start | bytes 983048 | tf_op jit(solution)/shard_map/ppermute | solution.py:527
  14.8 16.2 %collective-permute-start.6 = (bf16[160,1024]{1,0:T(8,128)(2,1)S(1)}, bf16[160,1024]{1,0:T(8,128)(2,1)S(1)}, u32[]{:S(2)}, u32[]{:S(2)}) collective-permute-start(bf16[160,1024]{1,0:T(8,128)(2,1)S(1)} %get-tuple-element.88), channel_id=1, source_target_pairs={{0,16},{8,24},{16,0},{24,8},{32,48},{40,56},{48,32},{56,40},{1,17}... | collective-permute-start | bytes 983048 | tf_op jit(solution)/shard_map/ppermute | solution.py:527
  19.7 18.2 %collective-permute-start.2 = (bf16[160,1024]{1,0:T(8,128)(2,1)S(1)}, bf16[160,1024]{1,0:T(8,128)(2,1)S(1)}, u32[]{:S(2)}, u32[]{:S(2)}) collective-permute-start(bf16[160,1024]{1,0:T(8,128)(2,1)S(1)} %get-tuple-element.83), channel_id=1, source_target_pairs={{0,48},{8,56},{16,32},{24,40},{32,16},{40,24},{48,0},{56,8},{1,49}... | collective-permute-start | bytes 983048 | tf_op jit(solution)/shard_map/ppermute | solution.py:527
  24.1 13.9 %collective-permute-start.4 = (bf16[160,1152]{1,0:T(8,128)(2,1)S(1)}, bf16[160,1152]{1,0:T(8,128)(2,1)S(1)}, u32[]{:S(2)}, u32[]{:S(2)}) collective-permute-start(bf16[160,1152]{1,0:T(8,128)(2,1)S(1)} %get-tuple-element.81), channel_id=1, source_target_pairs={{0,16},{8,24},{16,0},{24,8},{32,48},{40,56},{48,32},{56,40},{1,17}... | collective-permute-start | bytes 1105928 | tf_op jit(solution)/shard_map/ppermute | solution.py:527
  31.3 12.5 %collective-permute-start.7 = (bf16[160,1024]{1,0:T(8,128)(2,1)S(1)}, bf16[160,1024]{1,0:T(8,128)(2,1)S(1)}, u32[]{:S(2)}, u32[]{:S(2)}) collective-permute-start(bf16[160,1024]{1,0:T(8,128)(2,1)S(1)} %get-tuple-element.85), channel_id=1, source_target_pairs={{0,48},{8,56},{16,32},{24,40},{32,16},{40,24},{48,0},{56,8},{1,49}... | collective-permute-start | bytes 983048 | tf_op jit(solution)/shard_map/ppermute | solution.py:527
  33.9 9.9 %collective-permute-start.9 = (bf16[160,1024]{1,0:T(8,128)(2,1)S(1)}, bf16[160,1024]{1,0:T(8,128)(2,1)S(1)}, u32[]{:S(2)}, u32[]{:S(2)}) collective-permute-start(bf16[160,1024]{1,0:T(8,128)(2,1)S(1)} %get-tuple-element.77), channel_id=1, source_target_pairs={{0,16},{8,24},{16,0},{24,8},{32,48},{40,56},{48,32},{56,40},{1,17}... | collective-permute-start | bytes 983048 | tf_op jit(solution)/shard_map/ppermute | solution.py:527
  40.5 5.0 %collective-permute-start.10 = (bf16[128,2048]{1,0:T(8,128)(2,1)S(1)}, bf16[128,2048]{1,0:T(8,128)(2,1)S(1)}, u32[]{:S(2)}, u32[]{:S(2)}) collective-permute-start(bf16[128,2048]{1,0:T(8,128)(2,1)S(1)} %get-tuple-element.35.refs_0_), channel_id=1, source_target_pairs={{0,8},{8,0},{16,24},{24,16},{32,40},{40,32},{48,56},{56,48},{1,9},... | collective-permute-start | bytes 1572872 | tf_op jit(solution)/shard_map/ppermute | solution.py:527
  51.6 15.1 %all-to-all-start = ((bf16[8,32,1024]{2,1,0:T(8,128)(2,1)}), bf16[8,32,1024]{2,1,0:T(8,128)(2,1)S(1)}, u32[]{:S(2)}, u32[]{:S(2)}) async-start(bf16[8,32,1024]{2,1,0:T(8,128)(2,1)} %row_out_0.1), calls=%async_computation | async-start | bytes 1048576 | tf_op jit(solution)/shard_map/all_to_all | solution.py:572
  66.7 6.8 %collective-permute-start.12 = (bf16[32,1024]{1,0:T(8,128)(2,1)S(1)}, bf16[32,1024]{1,0:T(8,128)(2,1)S(1)}, u32[]{:S(2)}, u32[]{:S(2)}) collective-permute-start(bf16[32,1024]{1,0:T(8,128)(2,1)S(1)} %finish.3), channel_id=1, source_target_pairs={{0,64},{1,65},{2,66},{3,67},{4,68},{5,69},{6,70},{7,71},{8,72},{9,... | collective-permute-start | bytes 196616 | tf_op jit(solution)/shard_map/ppermute | solution.py:585
  90.0 5.2 %collective-permute-start.18 = (bf16[128,2048]{1,0:T(8,128)(2,1)S(1)}, bf16[128,2048]{1,0:T(8,128)(2,1)S(1)}, u32[]{:S(2)}, u32[]{:S(2)}) collective-permute-start(bf16[128,2048]{1,0:T(8,128)(2,1)S(1)} %get-tuple-element.48), channel_id=1, source_target_pairs={{0,8},{8,0},{16,24},{24,16},{32,40},{40,32},{48,56},{56,48},{1,9},... | collective-permute-start | bytes 1572872 | tf_op jit(solution)/shard_map/ppermute | solution.py:527
  92.0 9.2 %collective-permute-start.14 = (bf16[128,1024]{1,0:T(8,128)(2,1)S(1)}, bf16[128,1024]{1,0:T(8,128)(2,1)S(1)}, u32[]{:S(2)}, u32[]{:S(2)}) collective-permute-start(bf16[128,1024]{1,0:T(8,128)(2,1)S(1)} %fusion.5), channel_id=1, source_target_pairs={{0,16},{8,24},{16,0},{24,8},{32,48},{40,56},{48,32},{56,40},{1,17}... | collective-permute-start | bytes 786440 | tf_op jit(solution)/shard_map/ppermute | solution.py:527
  92.7 11.2 %collective-permute-start.16 = (bf16[128,1152]{1,0:T(8,128)(2,1)S(1)}, bf16[128,1152]{1,0:T(8,128)(2,1)S(1)}, u32[]{:S(2)}, u32[]{:S(2)}) collective-permute-start(bf16[128,1152]{1,0:T(8,128)(2,1)S(1)} %fusion.4), channel_id=1, source_target_pairs={{0,48},{8,56},{16,32},{24,40},{32,16},{40,24},{48,0},{56,8},{1,49}... | collective-permute-start | bytes 884744 | tf_op jit(solution)/shard_map/ppermute | solution.py:527
  95.3 14.2 %collective-permute-start.21 = (bf16[128,1024]{1,0:T(8,128)(2,1)S(1)}, bf16[128,1024]{1,0:T(8,128)(2,1)S(1)}, u32[]{:S(2)}, u32[]{:S(2)}) collective-permute-start(bf16[128,1024]{1,0:T(8,128)(2,1)S(1)} %get-tuple-element.99), channel_id=1, source_target_pairs={{0,48},{8,56},{16,32},{24,40},{32,16},{40,24},{48,0},{56,8},{1,49}... | collective-permute-start | bytes 786440 | tf_op jit(solution)/shard_map/ppermute | solution.py:527
  96.2 13.3 %collective-permute-start.19 = (bf16[128,1024]{1,0:T(8,128)(2,1)S(1)}, bf16[128,1024]{1,0:T(8,128)(2,1)S(1)}, u32[]{:S(2)}, u32[]{:S(2)}) collective-permute-start(bf16[128,1024]{1,0:T(8,128)(2,1)S(1)} %get-tuple-element.100), channel_id=1, source_target_pairs={{0,16},{8,24},{16,0},{24,8},{32,48},{40,56},{48,32},{56,40},{1,17}... | collective-permute-start | bytes 786440 | tf_op jit(solution)/shard_map/ppermute | solution.py:527
  101.3 13.8 %collective-permute-start.15 = (bf16[128,1024]{1,0:T(8,128)(2,1)S(1)}, bf16[128,1024]{1,0:T(8,128)(2,1)S(1)}, u32[]{:S(2)}, u32[]{:S(2)}) collective-permute-start(bf16[128,1024]{1,0:T(8,128)(2,1)S(1)} %get-tuple-element.75), channel_id=1, source_target_pairs={{0,48},{8,56},{16,32},{24,40},{32,16},{40,24},{48,0},{56,8},{1,49}... | collective-permute-start | bytes 786440 | tf_op jit(solution)/shard_map/ppermute | solution.py:527
  104.0 11.1 %collective-permute-start.17 = (bf16[128,1152]{1,0:T(8,128)(2,1)S(1)}, bf16[128,1152]{1,0:T(8,128)(2,1)S(1)}, u32[]{:S(2)}, u32[]{:S(2)}) collective-permute-start(bf16[128,1152]{1,0:T(8,128)(2,1)S(1)} %get-tuple-element.73), channel_id=1, source_target_pairs={{0,16},{8,24},{16,0},{24,8},{32,48},{40,56},{48,32},{56,40},{1,17}... | collective-permute-start | bytes 884744 | tf_op jit(solution)/shard_map/ppermute | solution.py:527
  109.8 9.8 %collective-permute-start.20 = (bf16[128,1024]{1,0:T(8,128)(2,1)S(1)}, bf16[128,1024]{1,0:T(8,128)(2,1)S(1)}, u32[]{:S(2)}, u32[]{:S(2)}) collective-permute-start(bf16[128,1024]{1,0:T(8,128)(2,1)S(1)} %get-tuple-element.97), channel_id=1, source_target_pairs={{0,48},{8,56},{16,32},{24,40},{32,16},{40,24},{48,0},{56,8},{1,49}... | collective-permute-start | bytes 786440 | tf_op jit(solution)/shard_map/ppermute | solution.py:527
  112.2 7.4 %collective-permute-start.22 = (bf16[128,1024]{1,0:T(8,128)(2,1)S(1)}, bf16[128,1024]{1,0:T(8,128)(2,1)S(1)}, u32[]{:S(2)}, u32[]{:S(2)}) collective-permute-start(bf16[128,1024]{1,0:T(8,128)(2,1)S(1)} %get-tuple-element.69), channel_id=1, source_target_pairs={{0,16},{8,24},{16,0},{24,8},{32,48},{40,56},{48,32},{56,40},{1,17}... | collective-permute-start | bytes 786440 | tf_op jit(solution)/shard_map/ppermute | solution.py:527
  140.3 7.8 %collective-permute-start.25 = (bf16[32,1024]{1,0:T(8,128)(2,1)S(1)}, bf16[32,1024]{1,0:T(8,128)(2,1)S(1)}, u32[]{:S(2)}, u32[]{:S(2)}) collective-permute-start(bf16[32,1024]{1,0:T(8,128)(2,1)S(1)} %finish.4), channel_id=1, source_target_pairs={{64,0},{65,1},{66,2},{67,3},{68,4},{69,5},{70,6},{71,7},{72,8},{73... | collective-permute-start | bytes 196616 | tf_op jit(solution)/shard_map/ppermute | solution.py:593
  163.8 10.5 %collective-permute-start.29 = (bf16[128,1024]{1,0:T(8,128)(2,1)S(1)}, bf16[128,1024]{1,0:T(8,128)(2,1)S(1)}, u32[]{:S(2)}, u32[]{:S(2)}) collective-permute-start(bf16[128,1024]{1,0:T(8,128)(2,1)S(1)} %get-tuple-element.95), channel_id=1, source_target_pairs={{0,48},{8,56},{16,32},{24,40},{32,16},{40,24},{48,0},{56,8},{1,49}... | collective-permute-start | bytes 786440 | tf_op jit(solution)/shard_map/ppermute | solution.py:527
  166.2 9.2 %collective-permute-start.27 = (bf16[128,1024]{1,0:T(8,128)(2,1)S(1)}, bf16[128,1024]{1,0:T(8,128)(2,1)S(1)}, u32[]{:S(2)}, u32[]{:S(2)}) collective-permute-start(bf16[128,1024]{1,0:T(8,128)(2,1)S(1)} %get-tuple-element.96), channel_id=1, source_target_pairs={{0,16},{8,24},{16,0},{24,8},{32,48},{40,56},{48,32},{56,40},{1,17}... | collective-permute-start | bytes 786440 | tf_op jit(solution)/shard_map/ppermute | solution.py:527
  166.3 13.5 %collective-permute-start.34 = (bf16[128,1024]{1,0:T(8,128)(2,1)S(1)}, bf16[128,1024]{1,0:T(8,128)(2,1)S(1)}, u32[]{:S(2)}, u32[]{:S(2)}) collective-permute-start(bf16[128,1024]{1,0:T(8,128)(2,1)S(1)} %get-tuple-element.91), channel_id=1, source_target_pairs={{0,48},{8,56},{16,32},{24,40},{32,16},{40,24},{48,0},{56,8},{1,49}... | collective-permute-start | bytes 786440 | tf_op jit(solution)/shard_map/ppermute | solution.py:527
  167.7 13.3 %collective-permute-start.32 = (bf16[128,1024]{1,0:T(8,128)(2,1)S(1)}, bf16[128,1024]{1,0:T(8,128)(2,1)S(1)}, u32[]{:S(2)}, u32[]{:S(2)}) collective-permute-start(bf16[128,1024]{1,0:T(8,128)(2,1)S(1)} %get-tuple-element.92), channel_id=1, source_target_pairs={{0,16},{8,24},{16,0},{24,8},{32,48},{40,56},{48,32},{56,40},{1,17}... | collective-permute-start | bytes 786440 | tf_op jit(solution)/shard_map/ppermute | solution.py:527
  175.7 10.5 %collective-permute-start.28 = (bf16[128,1024]{1,0:T(8,128)(2,1)S(1)}, bf16[128,1024]{1,0:T(8,128)(2,1)S(1)}, u32[]{:S(2)}, u32[]{:S(2)}) collective-permute-start(bf16[128,1024]{1,0:T(8,128)(2,1)S(1)} %get-tuple-element.93), channel_id=1, source_target_pairs={{0,48},{8,56},{16,32},{24,40},{32,16},{40,24},{48,0},{56,8},{1,49}... | collective-permute-start | bytes 786440 | tf_op jit(solution)/shard_map/ppermute | solution.py:527
  176.9 9.7 %collective-permute-start.30 = (bf16[128,1024]{1,0:T(8,128)(2,1)S(1)}, bf16[128,1024]{1,0:T(8,128)(2,1)S(1)}, u32[]{:S(2)}, u32[]{:S(2)}) collective-permute-start(bf16[128,1024]{1,0:T(8,128)(2,1)S(1)} %get-tuple-element.65), channel_id=1, source_target_pairs={{0,16},{8,24},{16,0},{24,8},{32,48},{40,56},{48,32},{56,40},{1,17}... | collective-permute-start | bytes 786440 | tf_op jit(solution)/shard_map/ppermute | solution.py:527
  181.3 8.8 %collective-permute-start.33 = (bf16[128,1024]{1,0:T(8,128)(2,1)S(1)}, bf16[128,1024]{1,0:T(8,128)(2,1)S(1)}, u32[]{:S(2)}, u32[]{:S(2)}) collective-permute-start(bf16[128,1024]{1,0:T(8,128)(2,1)S(1)} %get-tuple-element.89), channel_id=1, source_target_pairs={{0,48},{8,56},{16,32},{24,40},{32,16},{40,24},{48,0},{56,8},{1,49}... | collective-permute-start | bytes 786440 | tf_op jit(solution)/shard_map/ppermute | solution.py:527
  182.5 8.4 %collective-permute-start.35 = (bf16[128,1024]{1,0:T(8,128)(2,1)S(1)}, bf16[128,1024]{1,0:T(8,128)(2,1)S(1)}, u32[]{:S(2)}, u32[]{:S(2)}) collective-permute-start(bf16[128,1024]{1,0:T(8,128)(2,1)S(1)} %get-tuple-element.61), channel_id=1, source_target_pairs={{0,16},{8,24},{16,0},{24,8},{32,48},{40,56},{48,32},{56,40},{1,17}... | collective-permute-start | bytes 786440 | tf_op jit(solution)/shard_map/ppermute | solution.py:527
  188.4 4.8 %collective-permute-start.36 = (bf16[128,2176]{1,0:T(8,128)(2,1)S(1)}, bf16[128,2176]{1,0:T(8,128)(2,1)S(1)}, u32[]{:S(2)}, u32[]{:S(2)}) collective-permute-start(bf16[128,2176]{1,0:T(8,128)(2,1)S(1)} %act_2_0.1.refs_0_), channel_id=1, source_target_pairs={{0,8},{8,0},{16,24},{24,16},{32,40},{40,32},{48,56},{56,48},{1,9},... | collective-permute-start | bytes 1671176 | tf_op jit(solution)/shard_map/ppermute | solution.py:527
  199.3 13.5 %all-to-all-start.4 = ((bf16[8,32,1024]{2,1,0:T(8,128)(2,1)}), bf16[8,32,1024]{2,1,0:T(8,128)(2,1)S(1)}, u32[]{:S(2)}, u32[]{:S(2)}) async-start(bf16[8,32,1024]{2,1,0:T(8,128)(2,1)} %row_out_2.1), calls=%async_computation.4 | async-start | bytes 1048576 | tf_op jit(solution)/shard_map/all_to_all | solution.py:572
  (16 other events, 242.1 us)
